TPU v7x, 32 devices: a whole 2x2x4 slice. The times are simulated.
32 devices in a mesh: gx: 4 (over y, x), gy: 8 (over z, core).
Axes of the slice: x: 2, y: 2, z: 4, core: 2. Of those that a mesh axis runs over, the one named last changes fastest.
Arguments:
- charges: float32 [4, 8, 16384], P('gx', 'gy'), may hold values from -1.2 to 1.2
- fractions: float32 [4, 8, 3, 16384], P('gx', 'gy'), may hold values from 0 to 1
- cells: int32 [4, 8, 2, 16384], P('gx', 'gy'), may hold values from 0 to 127, as said below
Outputs:
- potential_grid: float32 [128, 128, 128], P('gx', 'gy')
- atom_potential: float32 [4, 8, 16384], P('gx', 'gy')
Inputs may be any that keep to these rules, and one draw needn't show every extreme that they name: cells[i, j, 0, a] lies in i-independent range j * 16 + 1 to j * 16 + 16, taken modulo 128; cells[i, j, 1, a] is a cell along the third dimension.
All inputs are finite; a program needn't handle non-finite values.
Results may differ from a plain program's by a relative error of at most 0.0003.
Values sent between devices are 32-bit elements; how exact they have to be, the bound alone decides.
No kernel may reach another device: no remote copies, remote signals or barrier semaphores. Data moves between devices by JAX's collectives and lax.ppermute only.
A program may use at most 128 MiB of HBM per device.

v0:
```python
import jax
import jax.numpy as jnp
import numpy as np
from jax import lax
from jax.sharding import PartitionSpec as P

CX = 32
CY = 16
NZ = 128
ATOMS_DEV = 16384


HIGHEST = lax.Precision.HIGHEST
restrict_taps = ((-3, -0.0625), (-1, 0.5625), (0, 1.0), (1, 0.5625), (3, -0.0625))


def padded_2(value, sides, width):
    for axis, dim in sides:
        size, length = (lax.axis_size(axis), value.shape[dim])
        up = [(i, (i + 1) % size) for i in range(size)]
        down = [(j, i) for i, j in up]
        last = lax.slice_in_dim(value, length - width, length, axis=dim)
        initial = lax.slice_in_dim(value, 0, width, axis=dim)
        before = lax.ppermute(last, axis, up)
        after = lax.ppermute(initial, axis, down)
        value = jnp.concatenate([before, value, after], axis=dim)
    return value


def shifted(value, axis, steps):
    count = lax.axis_size(axis)
    pairs = [(source, (source + steps) % count) for source in range(count)]
    return lax.ppermute(value, axis, pairs)


def spline_weights(frac):

    def near_weight(distance):
        return (1.0 - distance) * (1.0 + distance - 1.5 * distance * distance)

    def far_weight(distance):
        return -0.5 * (distance - 1.0) * (2.0 - distance) * (2.0 - distance)

    return jnp.stack(
        [
            far_weight(1.0 + frac),
            near_weight(frac),
            near_weight(1.0 - frac),
            far_weight(2.0 - frac),
        ],
        axis=-1,
    )


def smooth_numpy(rho):
    return np.where(
        rho < 1.0, 1.875 - 1.25 * rho * rho + 0.375 * rho**4, 1.0 / np.maximum(rho, 1.0)
    )


def smooth_jnp(rho):
    return jnp.where(
        rho < 1.0, 1.875 - 1.25 * rho * rho + 0.375 * rho**4, 1.0 / jnp.maximum(rho, 1.0)
    )


def depth_circulants(level, extent):
    offsets = np.arange(-3, 4) * 1.0
    radius = np.sqrt(
        offsets[:, None, None] ** 2 + offsets[None, :, None] ** 2 + offsets[None, None, :] ** 2
    )
    stencil = (smooth_numpy(radius / 1.5) / 1.5 - smooth_numpy(radius / 3.0) / 3.0) / 2.0 ** (
        level - 1
    )
    places = np.arange(extent)
    differ = (places[:, None] - places[None, :]) % extent
    signed = np.where(differ > extent // 2, differ - extent, differ)
    matrices = np.zeros((4, 4, extent, extent))
    for first in range(4):
        for second in range(4):
            for depth in range(-3, 4):
                matrices[first, second] += np.where(
                    signed == depth, stencil[first + 3, second + 3, depth + 3], 0.0
                )
    return matrices.astype(np.float32)


def apply_stencil(padded, level, count_x, count_y):
    extent = padded.shape[2]
    matrices = depth_circulants(level, extent)
    total = jnp.zeros((count_x * count_y, extent), jnp.float32)
    for first in range(4):
        for second in range(4):
            summed = jnp.zeros((count_x, count_y, extent), jnp.float32)
            for shift_x in sorted({first, -first}):
                for shift_y in sorted({second, -second}):
                    summed = (
                        summed
                        + padded[
                            3 + shift_x : 3 + shift_x + count_x, 3 + shift_y : 3 + shift_y + count_y
                        ]
                    )
            total = total + jnp.dot(
                summed.reshape(count_x * count_y, extent),
                jnp.asarray(matrices[first, second]),
                precision=HIGHEST,
            )
    return total.reshape(count_x, count_y, extent)


def restrict_padded(padded, count_x, count_y):
    field = padded
    for axis, count in ((0, count_x), (1, count_y)):
        total = 0.0
        for offset, weight in restrict_taps:
            total = total + weight * lax.slice_in_dim(
                field, 3 + offset, 3 + offset + count, 2, axis
            )
        field = total
    total = 0.0
    for offset, weight in restrict_taps:
        total = total + weight * jnp.roll(field, -offset, axis=2)
    return total[:, :, ::2]


def alternate_rows(even_rows, odd_rows, axis):
    stacked = jnp.stack([even_rows, odd_rows], axis=axis + 1)
    shape = list(even_rows.shape)
    shape[axis] = 2 * shape[axis]
    return stacked.reshape(shape)


def prolong_padded(padded, count_x, count_y):
    field = padded
    for axis, count in ((0, count_x), (1, count_y)):

        def taken(start):
            return lax.slice_in_dim(field, 2 + start, 2 + start + count, 1, axis)

        odd_rows = 0.5625 * (taken(0) + taken(1)) - 0.0625 * (taken(-1) + taken(2))
        field = alternate_rows(taken(0), odd_rows, axis)
    odd_rows = 0.5625 * (field + jnp.roll(field, -1, axis=2)) - 0.0625 * (
        jnp.roll(field, 1, axis=2) + jnp.roll(field, -2, axis=2)
    )
    return alternate_rows(field, odd_rows, 2)


def signed_offsets(count):
    places = jnp.arange(count, dtype=jnp.float32)
    return jnp.where(places > count // 2, places - count, places)


def coarse_field(whole, start_x, count_x, start_y, count_y):
    extent_x, extent_y, extent_z = whole.shape
    first = signed_offsets(extent_x)[:, None, None]
    second = signed_offsets(extent_y)[None, :, None]
    third = signed_offsets(extent_z)[None, None, :]
    kernel = smooth_jnp(jnp.sqrt(first * first + second * second + third * third) / 1.5) / 12.0
    doubled = jnp.concatenate([kernel, kernel], axis=0)
    doubled = jnp.concatenate([doubled, doubled], axis=1)
    sources = whole.reshape(extent_x * extent_y, extent_z)
    places = np.arange(extent_z)
    folding = jnp.asarray(
        (
            (places[None, :, None] + places[:, None, None]) % extent_z == places[None, None, :]
        ).astype(np.float32)
    )
    numbers = jnp.arange(count_x * count_y, dtype=jnp.int32)
    place_x = (start_x + numbers // count_y) % extent_x
    place_y = (start_y + numbers % count_y) % extent_y

    def window_at(offset_x, offset_y):
        return lax.dynamic_slice(
            doubled,
            ((extent_x - offset_x) % extent_x, (extent_y - offset_y) % extent_y, 0),
            (extent_x, extent_y, extent_z),
        )

    windows = jax.vmap(window_at)(place_x, place_y).reshape(
        count_x * count_y, extent_x * extent_y, extent_z
    )
    paired = jnp.einsum("csd,sw->cdw", windows, sources, precision=HIGHEST)
    values = jnp.einsum("cdw,dwz->cz", paired, folding, precision=HIGHEST)
    return values.reshape(count_x, count_y, extent_z)


def grid_rims(field, width):
    return padded_2(field, (("gx", 0), ("gy", 1)), width)


def local(charges, fractions, cells):
    size_x = lax.axis_size("gx")
    size_y = lax.axis_size("gy")
    index_x = lax.axis_index("gx")
    index_y = lax.axis_index("gy")
    per_plane = ATOMS_DEV // CX
    pairs = CX // 2
    total_y = CY * size_y
    charge_flat = charges.reshape(pairs, 2 * per_plane)
    weight_x = spline_weights(fractions[0, 0, 0]).reshape(pairs, 2 * per_plane, 4)
    weight_y = spline_weights(fractions[0, 0, 1]).reshape(pairs, 2 * per_plane, 4)
    weight_z = spline_weights(fractions[0, 0, 2]).reshape(pairs, 2 * per_plane, 4)
    cell_y = ((cells[0, 0, 0] - index_y * CY - 1) % total_y).reshape(pairs, 2 * per_plane)
    cell_z = cells[0, 0, 1].reshape(pairs, 2 * per_plane)
    places_y = jnp.arange(CY + 3, dtype=jnp.int32)
    places_z = jnp.arange(NZ, dtype=jnp.int32)

    def pair_tables(along_x, along_y, along_z, block_y, block_z):
        onehot_y = jnp.zeros((along_y.shape[0], CY + 3), jnp.float32)
        onehot_z = jnp.zeros((along_z.shape[0], NZ), jnp.float32)
        for tap in range(4):
            onehot_y = onehot_y + along_y[:, tap : tap + 1] * (
                places_y[None, :] == block_y[:, None] + tap
            )
            onehot_z = onehot_z + along_z[:, tap : tap + 1] * (
                places_z[None, :] == (block_z[:, None] + tap - 1) % NZ
            )
        spread = (along_x[:, :, None] * onehot_y[:, None, :]).reshape(
            along_x.shape[0], 4 * (CY + 3)
        )
        return (spread, onehot_z)

    def deposit_step(carried, inputs):
        block_charge, along_x, along_y, along_z, block_y, block_z = inputs
        spread, onehot_z = pair_tables(along_x, along_y, along_z, block_y, block_z)
        spread = spread * block_charge[:, None]
        contrib = jnp.einsum(
            "kpa,kpz->kaz",
            spread.reshape(2, per_plane, 4 * (CY + 3)),
            onehot_z.reshape(2, per_plane, NZ),
            precision=HIGHEST,
        )
        contrib = contrib.reshape(2, 4, CY + 3, NZ)
        layers = jnp.pad(contrib[0], ((0, 1), (0, 0), (0, 0))) + jnp.pad(
            contrib[1], ((1, 0), (0, 0), (0, 0))
        )
        return (carried, layers)

    unused_start, pair_layers = lax.scan(
        deposit_step, jnp.float32(0.0), (charge_flat, weight_x, weight_y, weight_z, cell_y, cell_z)
    )
    lower_part = pair_layers[:, 0:2].reshape(CX, CY + 3, NZ)
    middle_part = pair_layers[:, 2:4].reshape(CX, CY + 3, NZ)
    upper_part = jnp.stack([pair_layers[:, 4], jnp.zeros_like(pair_layers[:, 4])], axis=1).reshape(
        CX, CY + 3, NZ
    )
    grid_sum = (
        jnp.pad(lower_part, ((0, 4), (0, 0), (0, 0)))
        + jnp.pad(middle_part, ((2, 2), (0, 0), (0, 0)))
        + jnp.pad(upper_part, ((4, 0), (0, 0), (0, 0)))
    )
    grid_sum = grid_sum[: CX + 3]
    upper_x = shifted(grid_sum[CX:], "gx", 1)
    reduced_x = jnp.concatenate([grid_sum[:3] + upper_x, grid_sum[3:CX]], axis=0)
    upper_y = shifted(reduced_x[:, CY:], "gy", 1)
    level_one = jnp.concatenate([reduced_x[:, :3] + upper_y, reduced_x[:, 3:CY]], axis=1)
    padded_one = grid_rims(level_one, 3)
    smooth_one = apply_stencil(padded_one, 1, CX, CY)
    level_two = restrict_padded(padded_one, CX, CY)
    padded_two = grid_rims(level_two, 3)
    smooth_two = apply_stencil(padded_two, 2, CX // 2, CY // 2)
    level_three = restrict_padded(padded_two, CX // 2, CY // 2)
    coarse_x = CX // 8
    coarse_y = CY // 8
    padded_three = grid_rims(level_three, 3)
    smooth_three = apply_stencil(padded_three, 3, CX // 4, CY // 4)
    level_four = restrict_padded(padded_three, CX // 4, CY // 4)
    gathered = lax.all_gather(level_four.reshape(1, -1), ("gx", "gy"), axis=0, tiled=True)
    whole = gathered.reshape(size_x, size_y, coarse_x, coarse_y, NZ // 8).transpose(0, 2, 1, 3, 4)
    whole = whole.reshape(size_x * coarse_x, size_y * coarse_y, NZ // 8)
    coarse_padded = coarse_field(
        whole, index_x * coarse_x - 2, coarse_x + 4, index_y * coarse_y - 2, coarse_y + 4
    )
    level_three_potential = smooth_three + prolong_padded(coarse_padded, coarse_x, coarse_y)
    padded_potential = grid_rims(level_three_potential, 2)
    level_two_potential = smooth_two + prolong_padded(padded_potential, CX // 4, CY // 4)
    padded_two_potential = grid_rims(level_two_potential, 2)
    potential = smooth_one + prolong_padded(padded_two_potential, CX // 2, CY // 2)
    lower_x = shifted(potential[:3], "gx", -1)
    extended = jnp.concatenate([potential, lower_x], axis=0)
    lower_y = shifted(extended[:, :3], "gy", -1)
    extended = jnp.concatenate([extended, lower_y], axis=1)
    pair_windows = jnp.stack([extended[offset : offset + CX : 2] for offset in range(5)], axis=1)

    def sample_step(carried, inputs):
        window, along_x, along_y, along_z, block_y, block_z = inputs
        spread, onehot_z = pair_tables(along_x, along_y, along_z, block_y, block_z)
        stacked = jnp.stack([window[0:4], window[1:5]]).reshape(2, 4 * (CY + 3), NZ)
        projected = jnp.einsum(
            "kaz,kpz->kpa", stacked, onehot_z.reshape(2, per_plane, NZ), precision=HIGHEST
        )
        return (carried, jnp.sum(projected.reshape(2 * per_plane, 4 * (CY + 3)) * spread, axis=1))

    unused_carry, sampled = lax.scan(
        sample_step, jnp.float32(0.0), (pair_windows, weight_x, weight_y, weight_z, cell_y, cell_z)
    )
    return (potential, sampled.reshape(1, 1, ATOMS_DEV))


def solution(mesh):
    placed = (P("gx", "gy", None), P("gx", "gy", None, None), P("gx", "gy", None, None))
    return jax.shard_map(
        local,
        mesh=mesh,
        in_specs=placed,
        out_specs=(P("gx", "gy", None), P("gx", "gy", None)),
        check_vma=False,
    )
```

profile of v0, /device:TPU:0, one launch (start us, length us, event | category | flops | bytes accessed | tf_op | source)
XLA Modules:
  0.0 438.3 jit_solution(14634039486226826152)
XLA Ops:
  6.4 40.6 %while.36 = (s32[]{:T(128)}, f32[16,5,19,128]{3,2,1,0:T(8,128)S(1)}, f32[16,1024,4]{1,2,0:T(4,128)S(1)}, s32[16,1024]{1,0:T(8,128)S(1)}, f32[16,1024,4]{1,2,0:T(...) while((s32[]{:T(128)}, ...), condition=%wide.region_1.2_spmd.clone.clone, body=%wide.region_0.1_spmd.clone.clone.sunk | while | flops 121412480 | bytes 2965617 | solution.py:239
  47.7 3.0 collective-permute-start
  51.2 129.3 %while.35 = (s32[]{:T(128)}, f32[32,32,16]{1,2,0:T(8,128)S(1)}, s32[48,3]{0,1:T(4,128)S(1)}, f32[48,16,16,16]{2,3,1,0:T(8,128)}, s32[]{:T(128)}) while((s32[]{:T(128)}, f32[32,32,16]{1,2,0:T(8,128)S(1)}, s32[48,3]{0,1:T(4,128)S(1)}, f32[48,16,16,16]{2,3,1,0:T(8,128)}, s32[]{:T(128)}) %tuple.245), condition=%wide.while_cond, body=%wide.while_body.sunk | while | flops 2 | bytes 149097 | solution.py:173
  51.8 2.0 bitcast_dynamic-update-slice_fusion.9
  54.5 2.0 bitcast_dynamic-update-slice_fusion.9
  62.6 2.0 bitcast_dynamic-update-slice_fusion.9
  68.0 2.0 bitcast_dynamic-update-slice_fusion.9
  73.4 2.0 bitcast_dynamic-update-slice_fusion.9
  76.1 2.0 bitcast_dynamic-update-slice_fusion.9
  78.8 2.0 bitcast_dynamic-update-slice_fusion.9
  84.2 2.0 bitcast_dynamic-update-slice_fusion.9
  89.6 2.0 bitcast_dynamic-update-slice_fusion.9
  94.9 2.0 bitcast_dynamic-update-slice_fusion.9
  97.6 2.0 bitcast_dynamic-update-slice_fusion.9
  100.3 2.0 bitcast_dynamic-update-slice_fusion.9
  103.0 2.0 bitcast_dynamic-update-slice_fusion.9
  111.1 2.0 bitcast_dynamic-update-slice_fusion.9
  116.5 2.0 bitcast_dynamic-update-slice_fusion.9
  119.2 2.0 bitcast_dynamic-update-slice_fusion.9
  127.2 2.0 bitcast_dynamic-update-slice_fusion.9
  129.9 2.0 bitcast_dynamic-update-slice_fusion.9
  135.3 2.0 bitcast_dynamic-update-slice_fusion.9
  138.0 2.0 bitcast_dynamic-update-slice_fusion.9
  140.7 2.1 bitcast_dynamic-update-slice_fusion.9
  146.1 2.0 bitcast_dynamic-update-slice_fusion.9
  148.8 2.0 bitcast_dynamic-update-slice_fusion.9
  151.5 2.0 bitcast_dynamic-update-slice_fusion.9
  154.2 2.0 bitcast_dynamic-update-slice_fusion.9
  156.9 2.0 bitcast_dynamic-update-slice_fusion.9
  159.6 2.0 bitcast_dynamic-update-slice_fusion.9
  165.0 2.0 bitcast_dynamic-update-slice_fusion.9
  170.4 2.0 bitcast_dynamic-update-slice_fusion.9
  173.1 2.0 bitcast_dynamic-update-slice_fusion.9
  175.8 2.1 bitcast_dynamic-update-slice_fusion.9
  181.3 5.7 %copy.330 = f32[48,16,16,16]{0,2,1,3:T(8,128)S(1)} copy(f32[48,16,16,16]{2,3,1,0:T(8,128)} %get-tuple-element.518) | data formatting | bytes 1572864 | tf_op jit(solution)/shard_map/reshape | solution.py:179
  189.0 4.5 %collective-permute-done.1 = f32[32,3,128]{2,1,0:T(4,128)S(1)} collective-permute-done((f32[32,3,128]{2,1,0:T(4,128)S(1)}, f32[32,3,128]{2,1,0:T(4,128)S(1)}, u32[]{:S(2)}, u32[]{:S(2)}) %collective-permute-start.1) | collective-permute-done | bytes 49184 | tf_op jit(solution)/shard_map/ppermute | solution.py:33
  199.9 3.5 collective-permute-start.5
  211.2 2.4 collective-permute-start.6
  229.9 3.5 collective-permute-start.9
  251.6 3.5 collective-permute-start.13
  257.5 37.6 %all-gather = f32[32,1,128]{2,1,0:T(1,128)S(1)} all-gather(f32[1,1,128]{2,1,0:T(1,128)S(1)} %reshape.2194), channel_id=1, replica_groups=mesh['gx'=4,'gy'=8] {'gx','gy'}, dimensions={0}, use_global_device_ids=true | all-gather | bytes 16896 | tf_op jit(solution)/shard_map/all_gather | solution.py:268
  309.7 2.9 collective-permute-start.15
  316.5 3.5 collective-permute-start.17
  327.6 3.5 collective-permute-start.21
  335.2 2.4 collective-permute-start.22
  339.9 3.0 collective-permute-start.23
  343.6 3.1 collective-permute-done.23
  350.1 87.5 %while.37 = (s32[]{:T(128)}, f32[16,1024]{1,0:T(8,128)S(1)}, s32[16,1024]{1,0:T(8,128)}, f32[16,1024,4]{1,2,0:T(4,128)}, f32[16,5,19,128]{3,0,2,1:T(8,128)S(1)},...) while((s32[]{:T(128)}, f32[16,1024]{1,0:T(8,128)S(1)}, ...), condition=%wide.region_4.5_spmd.clone.clone, body=%wide.region_2.4_spmd.clone.clone.sunk | while | flops 121496576 | bytes 2150545 | solution.py:294
  353.0 2.4 fusion.343
  358.4 2.4 fusion.343
  363.9 2.4 fusion.343
  369.4 2.4 fusion.343
  374.9 2.4 fusion.343
  380.3 2.4 fusion.343
  385.8 2.4 fusion.343
  391.3 2.4 fusion.343
  396.7 2.4 fusion.343
  402.2 2.4 fusion.343
  407.7 2.4 fusion.343
  413.1 2.4 fusion.343
  418.6 2.4 fusion.343
  424.1 2.4 fusion.343
  429.5 2.4 fusion.343
  435.0 2.4 fusion.343
  (1120 shorter events, 247.2 us)
Async XLA Ops:
  47.0 0.6 copy-start.9
  47.0 134.3 %copy-start.2 = (f32[16,1024,4]{1,2,0:T(4,128)}, f32[16,1024,4]{1,2,0:T(4,128)S(1)}, u32[]{:S(2)}) copy-start(f32[16,1024,4]{1,2,0:T(4,128)S(1)} %get-tuple-element.1177) | copy-start | bytes 786436
  47.0 134.3 %copy-start.3 = (f32[16,1024,4]{1,2,0:T(4,128)}, f32[16,1024,4]{1,2,0:T(4,128)S(1)}, u32[]{:S(2)}) copy-start(f32[16,1024,4]{1,2,0:T(4,128)S(1)} %get-tuple-element.1178) | copy-start | bytes 786436
  47.0 134.3 %copy-start.4 = (f32[16,1024,4]{1,2,0:T(4,128)}, f32[16,1024,4]{1,2,0:T(4,128)S(1)}, u32[]{:S(2)}) copy-start(f32[16,1024,4]{1,2,0:T(4,128)S(1)} %get-tuple-element.1179) | copy-start | bytes 786436
  47.0 134.3 %copy-start.8 = (s32[16,1024]{1,0:T(8,128)}, s32[16,1024]{1,0:T(8,128)S(1)}, u32[]{:S(2)}) copy-start(s32[16,1024]{1,0:T(8,128)S(1)} %get-tuple-element.1189) | copy-start | bytes 196612
  47.7 139.3 %collective-permute-start = (f32[3,19,128]{2,1,0:T(8,128)S(1)}, f32[3,19,128]{2,1,0:T(8,128)S(1)}, u32[]{:S(2)}, u32[]{:S(2)}) collective-permute-start(f32[3,19,128]{2,1,0:T(8,128)S(1)} %pad_add_fusion.2), channel_id=1, source_target_pairs={{0,8},{8,16},{16,24},{24,0},{1,9},{9,17},{17,25},{25,1},{2,10},{10... | collective-permute-start | bytes 87560 | tf_op jit(solution)/shard_map/ppermute | solution.py:33
  187.9 5.5 %collective-permute-start.1 = (f32[32,3,128]{2,1,0:T(4,128)S(1)}, f32[32,3,128]{2,1,0:T(4,128)S(1)}, u32[]{:S(2)}, u32[]{:S(2)}) collective-permute-start(f32[32,3,128]{2,1,0:T(4,128)S(1)} %pad_maximum_fusion.26), channel_id=1, source_target_pairs={{0,1},{1,2},{2,3},{3,4},{4,5},{5,6},{6,7},{7,0},{8,9},{9,10},{10,1... | collective-permute-start | bytes 147464 | tf_op jit(solution)/shard_map/ppermute | solution.py:33
  194.4 4.8 %collective-permute-start.2 = (f32[3,16,128]{2,1,0:T(8,128)S(1)}, f32[3,16,128]{2,1,0:T(8,128)S(1)}, u32[]{:S(2)}, u32[]{:S(2)}) collective-permute-start(f32[3,16,128]{2,1,0:T(8,128)S(1)} %get-tuple-element.791), channel_id=1, source_target_pairs={{0,8},{8,16},{16,24},{24,0},{1,9},{9,17},{17,25},{25,1},{2,10},{10... | collective-permute-start | bytes 73736 | tf_op jit(solution)/shard_map/ppermute | solution.py:24
  195.9 3.8 collective-permute-start.3
  199.8 6.2 %collective-permute-start.4 = (f32[38,3,128]{2,1,0:T(4,128)S(1)}, f32[38,3,128]{2,1,0:T(4,128)S(1)}, u32[]{:S(2)}, u32[]{:S(2)}) collective-permute-start(f32[38,3,128]{2,1,0:T(4,128)S(1)} %get-tuple-element.787), channel_id=1, source_target_pairs={{0,1},{1,2},{2,3},{3,4},{4,5},{5,6},{6,7},{7,0},{8,9},{9,10},{10,1... | collective-permute-start | bytes 175112 | tf_op jit(solution)/shard_map/ppermute | solution.py:24
  199.9 6.1 %collective-permute-start.5 = (f32[38,3,128]{2,1,0:T(4,128)S(1)}, f32[38,3,128]{2,1,0:T(4,128)S(1)}, u32[]{:S(2)}, u32[]{:S(2)}) collective-permute-start(f32[38,3,128]{2,1,0:T(4,128)S(1)} %get-tuple-element.788), channel_id=1, source_target_pairs={{1,0},{2,1},{3,2},{4,3},{5,4},{6,5},{7,6},{0,7},{9,8},{10,9},{11,1... | collective-permute-start | bytes 175112 | tf_op jit(solution)/shard_map/ppermute | solution.py:25
  206.8 7.4 %copy-start.5 = (f32[128,128]{1,0:T(8,128)S(1)}, f32[128,128]{1,0:T(8,128)}, u32[]{:S(2)}) copy-start(f32[128,128]{1,0:T(8,128)} %constant.492.clone) | copy-start | bytes 196612
  207.9 9.0 %copy-start.7 = (f32[128,128]{1,0:T(8,128)S(1)}, f32[128,128]{1,0:T(8,128)}, u32[]{:S(2)}) copy-start(f32[128,128]{1,0:T(8,128)} %constant.493.clone) | copy-start | bytes 196612
  207.9 14.3 %copy-start.6 = (f32[128,128]{1,0:T(8,128)S(1)}, f32[128,128]{1,0:T(8,128)}, u32[]{:S(2)}) copy-start(f32[128,128]{1,0:T(8,128)} %constant.496.clone) | copy-start | bytes 196612
  209.9 23.5 %copy-start.14 = (f32[64,64]{1,0:T(8,128)S(1)}, f32[64,64]{1,0:T(8,128)}, u32[]{:S(2)}) copy-start(f32[64,64]{1,0:T(8,128)} %constant.498.clone) | copy-start | bytes 49156
  211.2 16.2 %copy-start.1 = (f32[32,16,128]{2,1,0:T(8,128)S(1)}, f32[32,16,128]{2,1,0:T(8,128)}, u32[]{:S(2)}) copy-start(f32[32,16,128]{2,1,0:T(8,128)} %get-tuple-element.780) | copy-start | bytes 786436
  211.2 17.5 %copy-start = (f32[32,16,128]{2,1,0:T(8,128)S(1)}, f32[32,16,128]{2,1,0:T(8,128)}, u32[]{:S(2)}) copy-start(f32[32,16,128]{2,1,0:T(8,128)} %get-tuple-element.775) | copy-start | bytes 786436
  211.2 18.5 %collective-permute-start.6 = (f32[3,8,64]{2,1,0:T(8,128)S(1)}, f32[3,8,64]{2,1,0:T(8,128)S(1)}, u32[]{:S(2)}, u32[]{:S(2)}) collective-permute-start(f32[3,8,64]{2,1,0:T(8,128)S(1)} %get-tuple-element.829), channel_id=1, source_target_pairs={{0,8},{8,16},{16,24},{24,0},{1,9},{9,17},{17,25},{25,1},{2,10},{10... | collective-permute-start | bytes 18440 | tf_op jit(solution)/shard_map/ppermute | solution.py:24
  213.7 16.1 %collective-permute-start.7 = (f32[3,8,64]{2,1,0:T(8,128)S(1)}, f32[3,8,64]{2,1,0:T(8,128)S(1)}, u32[]{:S(2)}, u32[]{:S(2)}) collective-permute-start(f32[3,8,64]{2,1,0:T(8,128)S(1)} %get-tuple-element.830), channel_id=1, source_target_pairs={{8,0},{16,8},{24,16},{0,24},{9,1},{17,9},{25,17},{1,25},{10,2},{18... | collective-permute-start | bytes 18440 | tf_op jit(solution)/shard_map/ppermute | solution.py:25
  227.4 71.1 %copy-start.10 = (f32[16,16,16]{1,2,0:T(8,128)S(1)}, f32[16,16,16]{1,2,0:T(8,128)}, u32[]{:S(2)}) copy-start(f32[16,16,16]{1,2,0:T(8,128)} %constant.510.clone) | copy-start | bytes 49156
  229.8 5.4 %collective-permute-start.8 = (f32[22,3,64]{2,1,0:T(4,128)S(1)}, f32[22,3,64]{2,1,0:T(4,128)S(1)}, u32[]{:S(2)}, u32[]{:S(2)}) collective-permute-start(f32[22,3,64]{2,1,0:T(4,128)S(1)} %get-tuple-element.815), channel_id=1, source_target_pairs={{0,1},{1,2},{2,3},{3,4},{4,5},{5,6},{6,7},{7,0},{8,9},{9,10},{10,1... | collective-permute-start | bytes 50696 | tf_op jit(solution)/shard_map/ppermute | solution.py:24
  229.9 5.3 %collective-permute-start.9 = (f32[22,3,64]{2,1,0:T(4,128)S(1)}, f32[22,3,64]{2,1,0:T(4,128)S(1)}, u32[]{:S(2)}, u32[]{:S(2)}) collective-permute-start(f32[22,3,64]{2,1,0:T(4,128)S(1)} %get-tuple-element.816), channel_id=1, source_target_pairs={{1,0},{2,1},{3,2},{4,3},{5,4},{6,5},{7,6},{0,7},{9,8},{10,9},{11,1... | collective-permute-start | bytes 50696 | tf_op jit(solution)/shard_map/ppermute | solution.py:25
  246.3 4.6 %collective-permute-start.10 = (f32[3,4,32]{2,1,0:T(4,128)S(1)}, f32[3,4,32]{2,1,0:T(4,128)S(1)}, u32[]{:S(2)}, u32[]{:S(2)}) collective-permute-start(f32[3,4,32]{2,1,0:T(4,128)S(1)} %get-tuple-element.868), channel_id=1, source_target_pairs={{0,8},{8,16},{16,24},{24,0},{1,9},{9,17},{17,25},{25,1},{2,10},{10... | collective-permute-start | bytes 4616 | tf_op jit(solution)/shard_map/ppermute | solution.py:24
  247.9 3.6 collective-permute-start.11
  250.9 44.2 %copy-start.12 = (f32[3,4,32]{2,1,0:T(4,128)}, f32[3,4,32]{2,1,0:T(4,128)S(1)}, u32[]{:S(2)}) copy-start(f32[3,4,32]{2,1,0:T(4,128)S(1)} %collective-permute-done.10) | copy-start | bytes 4612
  251.5 43.6 %copy-start.13 = (f32[3,4,32]{2,1,0:T(4,128)}, f32[3,4,32]{2,1,0:T(4,128)S(1)}, u32[]{:S(2)}) copy-start(f32[3,4,32]{2,1,0:T(4,128)S(1)} %collective-permute-done.11) | copy-start | bytes 4612
  251.5 5.1 %collective-permute-start.12 = (f32[14,3,32]{2,1,0:T(4,128)S(1)}, f32[14,3,32]{2,1,0:T(4,128)S(1)}, u32[]{:S(2)}, u32[]{:S(2)}) collective-permute-start(f32[14,3,32]{2,1,0:T(4,128)S(1)} %get-tuple-element.858), channel_id=1, source_target_pairs={{0,1},{1,2},{2,3},{3,4},{4,5},{5,6},{6,7},{7,0},{8,9},{9,10},{10,1... | collective-permute-start | bytes 16136 | tf_op jit(solution)/shard_map/ppermute | solution.py:24
  251.6 5.1 %collective-permute-start.13 = (f32[14,3,32]{2,1,0:T(4,128)S(1)}, f32[14,3,32]{2,1,0:T(4,128)S(1)}, u32[]{:S(2)}, u32[]{:S(2)}) collective-permute-start(f32[14,3,32]{2,1,0:T(4,128)S(1)} %get-tuple-element.859), channel_id=1, source_target_pairs={{1,0},{2,1},{3,2},{4,3},{5,4},{6,5},{7,6},{0,7},{9,8},{10,9},{11,1... | collective-permute-start | bytes 16136 | tf_op jit(solution)/shard_map/ppermute | solution.py:25
  256.7 38.4 %copy-start.11 = (f32[14,3,32]{2,1,0:T(4,128)}, f32[14,3,32]{2,1,0:T(4,128)S(1)}, u32[]{:S(2)}) copy-start(f32[14,3,32]{2,1,0:T(4,128)S(1)} %collective-permute-done.13) | copy-start | bytes 16132
  309.6 5.9 %collective-permute-start.14 = (f32[2,4,32]{0,2,1:T(8,128)S(1)}, f32[2,4,32]{0,2,1:T(8,128)S(1)}, u32[]{:S(2)}, u32[]{:S(2)}) collective-permute-start(f32[2,4,32]{0,2,1:T(8,128)S(1)} %get-tuple-element.827), channel_id=1, source_target_pairs={{0,8},{8,16},{16,24},{24,0},{1,9},{9,17},{17,25},{25,1},{2,10},{10... | collective-permute-start | bytes 3080 | tf_op jit(solution)/shard_map/ppermute | solution.py:24
  309.7 6.6 %collective-permute-start.15 = (f32[2,4,32]{0,2,1:T(8,128)S(1)}, f32[2,4,32]{0,2,1:T(8,128)S(1)}, u32[]{:S(2)}, u32[]{:S(2)}) collective-permute-start(f32[2,4,32]{0,2,1:T(8,128)S(1)} %get-tuple-element.828), channel_id=1, source_target_pairs={{8,0},{16,8},{24,16},{0,24},{9,1},{17,9},{25,17},{1,25},{10,2},{18... | collective-permute-start | bytes 3080 | tf_op jit(solution)/shard_map/ppermute | solution.py:25
  316.4 5.0 %collective-permute-start.16 = (f32[12,2,32]{2,1,0:T(2,128)S(1)}, f32[12,2,32]{2,1,0:T(2,128)S(1)}, u32[]{:S(2)}, u32[]{:S(2)}) collective-permute-start(f32[12,2,32]{2,1,0:T(2,128)S(1)} %get-tuple-element.860), channel_id=1, source_target_pairs={{0,1},{1,2},{2,3},{3,4},{4,5},{5,6},{6,7},{7,0},{8,9},{9,10},{10,1... | collective-permute-start | bytes 9224 | tf_op jit(solution)/shard_map/ppermute | solution.py:24
  316.5 4.9 %collective-permute-start.17 = (f32[12,2,32]{2,1,0:T(2,128)S(1)}, f32[12,2,32]{2,1,0:T(2,128)S(1)}, u32[]{:S(2)}, u32[]{:S(2)}) collective-permute-start(f32[12,2,32]{2,1,0:T(2,128)S(1)} %get-tuple-element.861), channel_id=1, source_target_pairs={{1,0},{2,1},{3,2},{4,3},{5,4},{6,5},{7,6},{0,7},{9,8},{10,9},{11,1... | collective-permute-start | bytes 9224 | tf_op jit(solution)/shard_map/ppermute | solution.py:25
  322.3 4.6 %collective-permute-start.18 = (f32[2,8,64]{2,1,0:T(8,128)S(1)}, f32[2,8,64]{2,1,0:T(8,128)S(1)}, u32[]{:S(2)}, u32[]{:S(2)}) collective-permute-start(f32[2,8,64]{2,1,0:T(8,128)S(1)} %get-tuple-element.819), channel_id=1, source_target_pairs={{0,8},{8,16},{16,24},{24,0},{1,9},{9,17},{17,25},{25,1},{2,10},{10... | collective-permute-start | bytes 12296 | tf_op jit(solution)/shard_map/ppermute | solution.py:24
  323.8 3.7 collective-permute-start.19
  327.5 5.1 %collective-permute-start.20 = (f32[20,2,64]{2,1,0:T(2,128)S(1)}, f32[20,2,64]{2,1,0:T(2,128)S(1)}, u32[]{:S(2)}, u32[]{:S(2)}) collective-permute-start(f32[20,2,64]{2,1,0:T(2,128)S(1)} %get-tuple-element.817), channel_id=1, source_target_pairs={{0,1},{1,2},{2,3},{3,4},{4,5},{5,6},{6,7},{7,0},{8,9},{9,10},{10,1... | collective-permute-start | bytes 30728 | tf_op jit(solution)/shard_map/ppermute | solution.py:24
  327.6 5.0 %collective-permute-start.21 = (f32[20,2,64]{2,1,0:T(2,128)S(1)}, f32[20,2,64]{2,1,0:T(2,128)S(1)}, u32[]{:S(2)}, u32[]{:S(2)}) collective-permute-start(f32[20,2,64]{2,1,0:T(2,128)S(1)} %get-tuple-element.818), channel_id=1, source_target_pairs={{1,0},{2,1},{3,2},{4,3},{5,4},{6,5},{7,6},{0,7},{9,8},{10,9},{11,1... | collective-permute-start | bytes 30728 | tf_op jit(solution)/shard_map/ppermute | solution.py:25
  335.2 3.9 collective-permute-start.22
  339.9 6.8 %collective-permute-start.23 = (f32[35,3,128]{0,1,2:T(4,128)S(1)}, f32[35,3,128]{0,1,2:T(4,128)}, u32[]{:S(2)}, u32[]{:S(2)}) collective-permute-start(f32[35,3,128]{0,1,2:T(4,128)S(1)} %fusion.57), channel_id=1, source_target_pairs={{0,7},{1,0},{2,1},{3,2},{4,3},{5,4},{6,5},{7,6},{8,15},{9,8},{10,9... | collective-permute-start | bytes 161288 | tf_op jit(solution)/shard_map/ppermute | solution.py:33
where the time goes:
time: 445 us; the launch traced here: 438 us
  local copies, waits for them, and re-layouts  205 us (46%)
  matrix products  106 us (24%)
  starting transfers between devices  41.2 us (9%)
  blocking collectives  37.6 us (8%)
  other arithmetic  21.6 us (5%)
  waiting for transfers between devices  19.8 us (4%)
  loops' own time  4.81 us (1%)
    gather x144, local copies, waits for them, and re-layouts  129 us
    dot_general x16, matrix products, sample_step(): jnp.einsum('kaz,kpz->kpa', stacked, onehot_z.reshape(2, per_plane, NZ), p...  38.6 us
    dot_general x48, matrix products, apply_stencil(): jnp.dot(summed.reshape(count_x * count_y, extent), jnp.asarray(matrices[f...  38.4 us
    all_gather x1, blocking collectives, local(): lax.all_gather(level_four.reshape(1, -1), ('gx', 'gy'), axis=0, tiled=True)  37.6 us
    dot_general x16, matrix products, deposit_step(): jnp.einsum('kpa,kpz->kaz', spread.reshape(2, per_plane, 4 * (CY + 3)), on...  27.9 us
    ppermute x10, starting transfers between devices, padded_2(): after = lax.ppermute(initial, axis, down)  25.4 us
    squeeze x48, local copies, waits for them, and re-layouts, local(): lax.scan(deposit_step, jnp.float32(0.0), (charge_flat, weight_x, weight_y...  23.7 us
    dynamic_slice x48, local copies, waits for them, and re-layouts, local(): lax.scan(deposit_step, jnp.float32(0.0), (charge_flat, weight_x, weight_y...  13.6 us
  transfers between devices with their start and end apart: 24, of which 16 were waited for; matrix products, arithmetic and copies ran while one was open for 37% of the time, Pallas kernels for 0%

commit v1 on v0

v1 whole, which is shorter than its diff:
```python
import functools

import jax
import jax.numpy as jnp
import numpy as np
from jax import lax
from jax.experimental import pallas as pl
from jax.experimental.pallas import tpu as pltpu
from jax.sharding import PartitionSpec as P

CX = 32
CY = 16
NZ = 128
ATOMS_DEV = 16384

HIGHEST = lax.Precision.HIGHEST
RESTRICT_TAPS = ((-3, -0.0625), (-1, 0.5625), (0, 1.0), (1, 0.5625), (3, -0.0625))
PER_PLANE = ATOMS_DEV // CX
LANES = 128
CHUNKS = PER_PLANE // LANES
Z2, Z3, Z4 = (NZ // 2, NZ // 4, NZ // 8)
LANE3 = Z2
LANE4 = Z2 + Z3

X1, Y1 = (0, CX + 3), (0, CY + 3)


def coarser(window):
    first, count = window
    last = first + count - 1
    starts = [m for m in range(first - 4, last + 4) if any(first <= 2 * m + k <= last for k, _ in RESTRICT_TAPS)]
    return (starts[0], starts[-1] - starts[0] + 1)


X2, Y2 = coarser(X1), coarser(Y1)
X3, Y3 = coarser(X2), coarser(Y2)
X4, Y4 = coarser(X3), coarser(Y3)


def up8(count):
    return -(-count // 8) * 8


YP1, YP2, YP3, YP4 = (up8(Y1[1]), up8(Y2[1]), up8(Y3[1]), up8(Y4[1]))
PAD = 8


def real_basis(count):
    places = np.arange(count)
    rows = [np.full(count, 1.0 / np.sqrt(count))]
    for k in range(1, count // 2):
        rows.append(np.sqrt(2.0 / count) * np.cos(2 * np.pi * k * places / count))
        rows.append(np.sqrt(2.0 / count) * np.sin(2 * np.pi * k * places / count))
    rows.append(np.where(places % 2 == 0, 1.0, -1.0) / np.sqrt(count))
    return np.stack(rows)


def basis_frequency(count):
    return np.array([0] + [k for k in range(1, count // 2) for _ in range(2)] + [count // 2])


def restrict_matrix(count):
    matrix = np.zeros((count // 2, count))
    for m in range(count // 2):
        for k, weight in RESTRICT_TAPS:
            matrix[m, (2 * m + k) % count] += weight
    return matrix


def depth_matrix():
    first = restrict_matrix(NZ)
    second = restrict_matrix(Z2) @ first
    third = restrict_matrix(Z3) @ second
    parts = [real_basis(NZ), real_basis(Z2) @ first, real_basis(Z3) @ second, real_basis(Z4) @ third]
    parts.append(np.zeros((2 * LANES - sum(p.shape[0] for p in parts), NZ)))
    return np.concatenate(parts, axis=0)


def smooth_numpy(rho):
    return np.where(rho < 1.0, 1.875 - 1.25 * rho * rho + 0.375 * rho**4, 1.0 / np.maximum(rho, 1.0))


def stencil_spectrum(level, count):
    offsets = np.arange(-3, 4) * 1.0
    near = np.arange(0, 4) * 1.0
    radius = np.sqrt(near[:, None, None] ** 2 + near[None, :, None] ** 2 + offsets[None, None, :] ** 2)
    stencil = (smooth_numpy(radius / 1.5) / 1.5 - smooth_numpy(radius / 3.0) / 3.0) / 2.0 ** (level - 1)
    waves = np.cos(2 * np.pi * offsets[:, None] * basis_frequency(count)[None, :] / count)
    return np.einsum("abd,dk->abk", stencil, waves)


def spectra():
    fine = stencil_spectrum(1, NZ).reshape(16, NZ)
    coarse = np.zeros((16, LANES))
    coarse[:, :Z2] = stencil_spectrum(2, Z2).reshape(16, Z2)
    coarse[:, LANE3:LANE4] = stencil_spectrum(3, Z3).reshape(16, Z3)
    return np.stack([fine, coarse])


def signed(count):
    places = np.arange(count)
    return np.where(places > count // 2, places - count, places) * 1.0


def coarse_tables(size_x, size_y):
    total_x = CX // 8 * size_x
    total_y = CY // 8 * size_y
    first = signed(total_x)[:, None, None]
    second = signed(total_y)[None, :, None]
    third = signed(Z4)[None, None, :]
    kernel = smooth_numpy(np.sqrt(first**2 + second**2 + third**2) / 1.5) / 12.0

    def cosines(count):
        return np.cos(2 * np.pi * basis_frequency(count)[:, None] * np.arange(count)[None, :] / count)

    spectrum = np.einsum("xyz,ax,by,cz->abc", kernel, cosines(total_x), cosines(total_y), cosines(Z4), optimize=True)
    spectrum = spectrum.reshape(total_x, total_y * Z4)
    basis_x = real_basis(total_x)
    basis_y = np.kron(real_basis(total_y), np.eye(Z4))
    span = X4[1]
    tail = up8(size_x)
    gather = np.zeros((total_x, 8 * size_x + tail))
    window = np.zeros((size_x, up8(span), total_x))
    for i in range(size_x):
        for a in range(span):
            place = (i * (CX // 8) + X4[0] + a) % total_x
            gather[:, i * 8 + a if a < 8 else 8 * size_x + i] = basis_x[:, place]
            window[i, a, :] = basis_x[:, place]
    return [t.astype(np.float32) for t in (gather, basis_y, spectrum, window)]


def spline_weights(frac):
    def near_weight(distance):
        return (1.0 - distance) * (1.0 + distance - 1.5 * distance * distance)

    def far_weight(distance):
        return -0.5 * (distance - 1.0) * (2.0 - distance) * (2.0 - distance)

    return [far_weight(1.0 + frac), near_weight(frac), near_weight(1.0 - frac), far_weight(2.0 - frac)]


def plane_rows(frac_ref, cell_ref, start, first_y, total_y):
    frac = frac_ref[0, 0, :, pl.ds(start, PER_PLANE)]
    cell = cell_ref[0, 0, :, pl.ds(start, PER_PLANE)]
    weights = spline_weights(frac)
    block_y = cell[0:1] - first_y
    block_y = jnp.where(block_y < 0, block_y + total_y, block_y)
    depth = []
    for tap in range(4):
        place = cell[1:2] + (tap - 1)
        place = jnp.where(place < 0, place + NZ, place)
        depth.append(jnp.where(place >= NZ, place - NZ, place))
    return weights, block_y, depth


def along_y(weights, block_y, lanes):
    places = lax.broadcasted_iota(jnp.int32, (YP1, LANES), 0)
    offset = places - block_y[:, lanes]
    table = jnp.zeros((YP1, LANES), jnp.float32)
    for tap in range(4):
        table = jnp.where(offset == tap, weights[tap][1:2, lanes], table)
    return table


def along_z(weights, depth, lanes):
    places = lax.broadcasted_iota(jnp.int32, (NZ, LANES), 0).astype(jnp.bfloat16).reshape(NZ // 16, 16, LANES)
    high = jnp.zeros((NZ // 16, 16, LANES), jnp.bfloat16)
    low = jnp.zeros((NZ // 16, 16, LANES), jnp.bfloat16)
    for tap in range(4):
        place = jnp.broadcast_to(depth[tap][:, lanes].astype(jnp.float32), (16, LANES)).astype(jnp.bfloat16)
        weight = jnp.broadcast_to(weights[tap][2:3, lanes], (16, LANES))
        weight_high = weight.astype(jnp.bfloat16)
        weight_low = (weight - weight_high.astype(jnp.float32)).astype(jnp.bfloat16)
        same = places == place[None]
        high = jnp.where(same, weight_high[None], high)
        low = jnp.where(same, weight_low[None], low)
    return high.reshape(NZ, LANES), low.reshape(NZ, LANES)


def halves(value):
    high = value.astype(jnp.bfloat16)
    low = (value - high.astype(jnp.float32)).astype(jnp.bfloat16)
    return high, low


def lane_index(shape):
    return lax.broadcasted_iota(jnp.int32, shape, len(shape) - 1)


def restrict_x(load, window_in, window_out):
    first, count = window_in
    outs = []
    for m in range(window_out[0], window_out[0] + window_out[1]):
        total = None
        for k, weight in RESTRICT_TAPS:
            place = 2 * m + k - first
            if 0 <= place < count:
                term = load(place) if weight == 1.0 else weight * load(place)
                total = term if total is None else total + term
        outs.append(total)
    return outs


def restrict_y(source, window_in, window_out, rows_out):
    total = None
    for k, weight in RESTRICT_TAPS:
        start = 2 * window_out[0] + k - window_in[0] + PAD
        term = source[:, pl.ds(start, rows_out, stride=2), :]
        term = term if weight == 1.0 else weight * term
        total = term if total is None else total + term
    places = lax.broadcasted_iota(jnp.int32, total.shape, 1)
    return jnp.where(places < window_out[1], total, 0.0)


def deposit_kernel(
    place_ref, charge_ref, frac_ref, cell_ref, depth_ref,
    raw_ref, part_ref, low_ref, high_ref, message_ref,
    grid, coarse, half2, half3, half4, last,
    *, total_y, devices,
):
    first_y = place_ref[1] * CY + 1
    grid[...] = jnp.zeros_like(grid)

    def step(plane, carry):
        start = pl.multiple_of(plane * PER_PLANE, PER_PLANE)
        weights, block_y, depth = plane_rows(frac_ref, cell_ref, start, first_y, total_y)
        charge = charge_ref[0, 0:1, pl.ds(start, PER_PLANE)]
        lefts, rights = [], []
        for chunk in range(CHUNKS):
            lanes = slice(chunk * LANES, (chunk + 1) * LANES)
            table = along_y(weights, block_y, lanes)
            spread = jnp.concatenate([table * (charge * weights[m][0:1])[:, lanes] for m in range(4)], axis=0)
            lefts.append(jnp.concatenate(halves(spread), axis=0))
            rights.append(jnp.concatenate(along_z(weights, depth, lanes), axis=0))
        left = jnp.concatenate(lefts, axis=1)
        right = jnp.concatenate(rights, axis=1)
        product = lax.dot_general(left, right, (((1,), (1,)), ((), ())), preferred_element_type=jnp.float32)
        rows = 4 * YP1
        layers = product[:rows, :NZ] + (product[:rows, NZ:] + product[rows:, :NZ] + product[rows:, NZ:])
        for m in range(4):
            grid[plane + m] = grid[plane + m] + layers[m * YP1 : (m + 1) * YP1]
        return carry

    lax.fori_loop(0, CX, step, 0)
    flat = grid[...].reshape(X1[1] * YP1, NZ)
    table = depth_ref[...]
    deep = (((1,), (1,)), ((), ()))
    raw = lax.dot_general(flat, table[:LANES], deep, precision=HIGHEST, preferred_element_type=jnp.float32)
    raw_ref[...] = raw.reshape(X1[1], YP1, LANES)
    below = lax.dot_general(flat, table[LANES:], deep, precision=HIGHEST, preferred_element_type=jnp.float32)
    coarse[...] = below.reshape(X1[1], YP1, LANES)

    def padded(half, outs, rows):
        half[...] = jnp.zeros_like(half)
        for i, value in enumerate(outs):
            half[i, PAD : PAD + rows, :] = value

    padded(half2, restrict_x(lambda i: coarse[i], X1, X2), YP1)
    level2 = restrict_y(half2, Y1, Y2, YP2)
    padded(half3, restrict_x(lambda i: level2[i], X2, X3), YP2)
    level3 = restrict_y(half3, Y2, Y3, YP3)
    padded(half4, restrict_x(lambda i: level3[i], X3, X4), YP3)
    last[...] = restrict_y(half4, Y3, Y4, YP4).reshape(X4[1] * YP4, LANES)

    lane2 = lane_index((YP2, LANES)) < Z2
    for i in range(X2[1]):
        other = level3[i] if i < X3[1] else jnp.zeros((YP2, LANES), jnp.float32)
        part_ref[i] = jnp.where(lane2, level2[i], other)
    for r in range(6):
        low_ref[r * YP1 : (r + 1) * YP1] = raw_ref[r]
        high_ref[r * YP1 : (r + 1) * YP1] = raw_ref[CX - 3 + r]
    for r in range(8):
        base = 6 * YP1 + r * YP2
        low_ref[base : base + YP2] = part_ref[r]
        two = part_ref[CX // 2 - 4 - X2[0] + r] if r < 7 else jnp.zeros((YP2, LANES), jnp.float32)
        high_ref[base : base + YP2] = jnp.where(lane2, two, part_ref[CX // 4 - 5 - X3[0] + r])
    lanes = lane_index((8, LANES))
    message = jnp.zeros((8, LANES), jnp.float32)
    for b in range(Y4[1]):
        rows = last[pl.ds(b, 8, stride=YP4), :]
        moved = pltpu.roll(rows, (b * Z4 - LANE4) % LANES, 1)
        message = jnp.where((lanes >= b * Z4) & (lanes < (b + 1) * Z4), moved, message)
    tail = pltpu.roll(last[8 * YP4 : 9 * YP4, :], Y4[1] * Z4 - LANE4, 1)
    message = jnp.where(lanes >= Y4[1] * Z4, tail, message)
    for d in range(devices):
        message_ref[d] = message


def merge_x_kernel(raw_ref, part_ref, below_ref, above_ref, fine_ref, pair_ref, up_ref, down_ref, up2_ref, down2_ref):
    lane2 = lane_index((YP2, LANES)) < Z2
    for r in range(X1[1]):
        fine_ref[3 + r] = raw_ref[r]
    for r in range(6):
        slab = slice(r * YP1, (r + 1) * YP1)
        if r < 3:
            fine_ref[r] = below_ref[slab]
            fine_ref[CX + 3 + r] = fine_ref[CX + 3 + r] + above_ref[slab]
        else:
            fine_ref[r] = fine_ref[r] + below_ref[slab]
            fine_ref[CX + 3 + r] = above_ref[slab]
    count = CX // 2 + 10
    pair_ref[...] = jnp.zeros_like(pair_ref)
    for r in range(X2[1]):
        pair_ref[3 + r] = part_ref[r]
    for r in range(8):
        slab = slice(6 * YP1 + r * YP2, 6 * YP1 + (r + 1) * YP2)
        pair_ref[r] = pair_ref[r] + below_ref[slab]
        at3 = CX // 4 + 3 + r
        pair_ref[at3] = pair_ref[at3] + jnp.where(lane2, 0.0, above_ref[slab])
        at2 = CX // 2 + 3 + r
        if at2 < count:
            pair_ref[at2] = pair_ref[at2] + jnp.where(lane2, above_ref[slab], 0.0)
    rows = X1[1] + 6
    narrow2 = lane_index((8, LANES)) < Z2
    for r in range(rows):
        up_ref[r] = fine_ref[r, CY - 3 : CY + 5, :]
        down_ref[r] = fine_ref[r, 0:8, :]
    row = lax.broadcasted_iota(jnp.int32, (8, LANES), 0)
    for r in range(count):
        two = jnp.where(row < 7, pair_ref[r, CY // 2 - 3 : CY // 2 + 5, :], 0.0)
        up_ref[rows + r] = jnp.where(narrow2, two, pair_ref[r, CY // 4 - 3 : CY // 4 + 5, :])
        down_ref[rows + r] = pair_ref[r, 0:8, :]
    span = CX // 4 + 11
    packed = (span + 1) // 2
    for r in range(span):
        at = slice(4 * (r // packed), 4 * (r // packed) + 4)
        up2_ref[r % packed, at, :] = pair_ref[r, CY // 2 - 3 : CY // 2 + 1, :]
        down2_ref[r % packed, at, :] = pair_ref[r, 0:4, :]
    if span % 2:
        up2_ref[packed - 1, 4:8, :] = jnp.zeros((4, LANES), jnp.float32)
        down2_ref[packed - 1, 4:8, :] = jnp.zeros((4, LANES), jnp.float32)


def stencil_rows(source, count, rows_out, table, out_ref, planes):
    total = count + 6

    def terms(i):
        sums = [source[i, 3 : 3 + rows_out, :]]
        for b in range(1, 4):
            sums.append(source[i, 3 - b : 3 - b + rows_out, :] + source[i, 3 + b : 3 + b + rows_out, :])
        for a in range(4):
            value = table[4 * a : 4 * a + 1] * sums[0]
            for b in range(1, 4):
                value = value + table[4 * a + b : 4 * a + b + 1] * sums[b]
            planes[a, i] = value

    def first(i, carry):
        terms(i)
        return carry

    lax.fori_loop(0, total, first, 0)

    def second(i, carry):
        value = planes[0, i + 3]
        for a in range(1, 4):
            value = value + (planes[a, i + 3 - a] + planes[a, i + 3 + a])
        out_ref[i] = value
        return carry

    lax.fori_loop(0, count, second, 0)


def stencil_kernel(
    fine_ref, pair_ref, below_ref, above_ref, below2_ref, above2_ref, spectrum_ref,
    smooth_ref, smooth_pair_ref,
    fine, pair, planes, planes_pair,
):
    rows = X1[1] + 6
    count = CX // 2 + 10
    fine[:, YP1 + 3 :, :] = jnp.zeros((rows, 32 - YP1 - 3, LANES), jnp.float32)
    fine[:, 0:3, :] = jnp.zeros((rows, 3, LANES), jnp.float32)
    fine[:, 3 : 3 + YP1, :] = fine_ref[...]
    fine[:, 0:6, :] = fine[:, 0:6, :] + below_ref[0:rows, 0:6, :]
    fine[:, CY + 3 : CY + 9, :] = fine[:, CY + 3 : CY + 9, :] + above_ref[0:rows, 0:6, :]
    pair[...] = jnp.zeros_like(pair)
    pair[:, 3 : 3 + YP2, :] = pair_ref[...]
    pair[:, 0:8, :] = pair[:, 0:8, :] + below_ref[rows:, :, :]
    lane2 = lane_index((count, 8, LANES)) < Z2
    above = above_ref[rows:, :, :]
    at2, at3 = (CY // 2 + 3, CY // 4 + 3)
    pair[:, at2 : at2 + 8, :] = pair[:, at2 : at2 + 8, :] + jnp.where(lane2, above, 0.0)
    pair[:, at3 : at3 + 8, :] = pair[:, at3 : at3 + 8, :] + jnp.where(lane2, 0.0, above)
    span = CX // 4 + 11
    packed = (span + 1) // 2
    lane3 = lane_index((4, LANES))
    lane3 = (lane3 >= LANE3) & (lane3 < LANE4)
    far = CY // 2 + 3
    for r in range(span):
        at = slice(4 * (r // packed), 4 * (r // packed) + 4)
        pair[r, 0:4, :] = pair[r, 0:4, :] + jnp.where(lane3, below2_ref[r % packed, at, :], 0.0)
        pair[r, far : far + 4, :] = pair[r, far : far + 4, :] + jnp.where(lane3, above2_ref[r % packed, at, :], 0.0)
    stencil_rows(fine, X1[1], YP1, spectrum_ref[0], smooth_ref, planes)
    stencil_rows(pair, X2[1], YP2, spectrum_ref[1], smooth_pair_ref, planes_pair)


def prolong_x(load, window_in, window_out):
    outs = []
    first = window_in[0]
    for n in range(window_out[0], window_out[0] + window_out[1]):
        if n % 2 == 0:
            outs.append(load(n // 2 - first))
        else:
            m = (n - 1) // 2 - first
            outs.append(0.5625 * (load(m) + load(m + 1)) - 0.0625 * (load(m - 1) + load(m + 2)))
    return outs


def prolong_y(source, window_in, window_out, target):
    first, count = window_out
    even = first % 2
    evens = (count - even + 1) // 2
    start = (first + even) // 2 - window_in[0]
    target[:, pl.ds(even, evens, stride=2), :] = source[:, start : start + evens, :]
    odds = count - evens
    m = (first + 1 - even - 1) // 2 - window_in[0]

    def taken(shift):
        return source[:, m + shift : m + shift + odds, :]

    target[:, pl.ds(1 - even, odds, stride=2), :] = 0.5625 * (taken(0) + taken(1)) - 0.0625 * (taken(-1) + taken(2))


def field_kernel(
    place_ref, message_ref, gather_ref, basis_ref, spectrum_ref, window_ref, smooth_ref, pair_ref, depth_ref,
    frac_ref, cell_ref,
    potential_ref, atom_ref,
    ninth, level4, half3, level3, half2, level2, half1, level1, field,
    *, size_x, size_y,
):
    total_y = CY * size_y
    devices = size_x * size_y
    width = CY // 8 * size_y * Z4
    blocks = width // LANES
    lanes8 = lane_index((8, LANES))
    used = Y4[1] * Z4
    tails = lane_index((devices, LANES))
    gathered = jnp.zeros((devices, LANES), jnp.float32)
    for b in range(Y4[1]):
        rows = message_ref[pl.ds(b, devices, stride=8), :]
        moved = pltpu.roll(rows, (b * Z4 - used) % LANES, 1)
        gathered = jnp.where((tails >= b * Z4) & (tails < (b + 1) * Z4), moved, gathered)
    ninth[...] = gathered

    def assemble(load, rows):
        total = [jnp.zeros((rows, LANES), jnp.float32) for _ in range(blocks)]
        lanes = lane_index((rows, LANES))
        for j in range(size_y):
            position = (j * (CY // 8) + Y4[0]) * Z4 % width
            block, offset = (position // LANES, position % LANES)
            value = jnp.where(lanes < used, load(j), 0.0)
            if offset == 0:
                total[block] = total[block] + value
                continue
            value = pltpu.roll(value, offset, 1)
            following = (block + 1) % blocks
            total[block] = total[block] + jnp.where(lanes >= offset, value, 0.0)
            total[following] = total[following] + jnp.where(lanes < offset, value, 0.0)
        return jnp.concatenate(total, axis=1)

    strips = []
    for i in range(size_x):
        strips.append(assemble(lambda j: message_ref[(i * size_y + j) * 8 : (i * size_y + j + 1) * 8, :], 8))
    tail = assemble(lambda j: ninth[pl.ds(j, size_x, stride=size_y), :], size_x)
    if size_x % 8:
        tail = jnp.concatenate([tail, jnp.zeros((8 - size_x % 8, width), jnp.float32)], axis=0)
    strips.append(tail)
    strips = jnp.concatenate(strips, axis=0)
    exact = dict(precision=HIGHEST, preferred_element_type=jnp.float32)
    modes = jnp.dot(gather_ref[...], strips, **exact)
    modes = lax.dot_general(modes, basis_ref[...], (((1,), (1,)), ((), ())), **exact)
    modes = jnp.dot(modes * spectrum_ref[...], basis_ref[...], **exact)
    shift = (width - (place_ref[1] * (CY // 8) + Y4[0]) * Z4) % width
    modes = pltpu.roll(modes, shift, 1)[:, :LANES]
    own = jnp.dot(window_ref[place_ref[0]], modes, **exact)
    lanes = lane_index(own.shape)
    inside4 = (lanes >= LANE4) & (lanes < LANE4 + Z4)
    level4[...] = jnp.zeros_like(level4)
    for b in range(Y4[1]):
        moved = jnp.where(inside4, pltpu.roll(own, (LANE4 - b * Z4) % LANES, 1), 0.0)
        level4[pl.ds(b, X4[1], stride=YP4), :] = moved[: X4[1]]

    def rise(load, window_in, window_out, wide_in, wide_out, half, target):
        target[...] = jnp.zeros_like(target)
        for r, value in enumerate(prolong_x(load, window_in, window_out)):
            half[r] = value
        prolong_y(half, wide_in, wide_out, target)

    rise(lambda i: level4[i * YP4 : (i + 1) * YP4, :], X4, X3, Y4, Y3, half3, level3)
    lanes3 = lane_index((YP3, LANES))
    inside3 = (lanes3 >= LANE3) & (lanes3 < LANE4)
    for r in range(X3[1]):
        level3[r] = level3[r] + jnp.where(inside3, pair_ref[r, 0:YP3, :], 0.0)
    rise(lambda i: level3[i], X3, X2, Y3, Y2, half2, level2)
    inside2 = lane_index((YP2, LANES)) < Z2
    for r in range(X2[1]):
        level2[r] = level2[r] + jnp.where(inside2, pair_ref[r], 0.0)
    rise(lambda i: level2[i], X2, X1, Y2, Y1, half1, level1)

    table = depth_ref[...]
    rows = X1[1] * YP1
    total = jnp.dot(smooth_ref[...].reshape(rows, LANES), table[:LANES], **exact)
    total = total + jnp.dot(level1[...].reshape(rows, LANES), table[LANES:], **exact)
    field[...] = total.reshape(X1[1], YP1, NZ)
    potential_ref[...] = field[0:CX, 0:CY, :]

    first_y = place_ref[1] * CY + 1

    def step(plane, carry):
        start = pl.multiple_of(plane * PER_PLANE, PER_PLANE)
        weights, block_y, depth = plane_rows(frac_ref, cell_ref, start, first_y, total_y)
        high, low = halves(jnp.concatenate([field[plane + m] for m in range(4)], axis=0))
        left = jnp.concatenate(
            [jnp.concatenate([high, high], axis=1), jnp.concatenate([low, low], axis=1)], axis=0
        )
        right = jnp.concatenate(
            [
                jnp.concatenate(along_z(weights, depth, slice(c * LANES, (c + 1) * LANES)), axis=0)
                for c in range(CHUNKS)
            ],
            axis=1,
        )
        product = jnp.dot(left, right, preferred_element_type=jnp.float32)
        sums = []
        for c in range(CHUNKS):
            lanes = slice(c * LANES, (c + 1) * LANES)
            total = jnp.zeros((YP1, LANES), jnp.float32)
            for m in range(4):
                layer = product[m * YP1 : (m + 1) * YP1, lanes] + product[(4 + m) * YP1 : (5 + m) * YP1, lanes]
                total = total + layer * weights[m][0:1, lanes]
            sums.append(jnp.sum(total * along_y(weights, block_y, lanes), axis=0, keepdims=True))
        atom_ref[0, 0:1, pl.ds(start, PER_PLANE)] = jnp.concatenate(sums, axis=1)
        return carry

    lax.fori_loop(0, CX, step, 0)


VM = pl.BlockSpec(memory_space=pltpu.VMEM)
SM = pl.BlockSpec(memory_space=pltpu.SMEM)


def f32(*shape):
    return jax.ShapeDtypeStruct(shape, jnp.float32)


def scratch(*shape):
    return pltpu.VMEM(shape, jnp.float32)


def shifted(value, axis, steps):
    count = lax.axis_size(axis)
    return lax.ppermute(value, axis, [(source, (source + steps) % count) for source in range(count)])


def local(charges, fractions, cells, interpret=False):
    size_x = lax.axis_size("gx")
    size_y = lax.axis_size("gy")
    devices = size_x * size_y
    place = jnp.stack([lax.axis_index("gx"), lax.axis_index("gy")]).astype(jnp.int32)
    depth = jnp.asarray(depth_matrix().astype(np.float32))
    gather, basis, coarse_spectrum, window = (jnp.asarray(t) for t in coarse_tables(size_x, size_y))
    slab = 6 * YP1 + 8 * YP2
    raw, part, low, high, message = pl.pallas_call(
        functools.partial(deposit_kernel, total_y=CY * size_y, devices=devices),
        in_specs=[SM, VM, VM, VM, VM],
        out_specs=[VM] * 5,
        out_shape=[
            f32(X1[1], YP1, LANES),
            f32(X2[1], YP2, LANES),
            f32(slab, LANES),
            f32(slab, LANES),
            f32(devices, 8, LANES),
        ],
        scratch_shapes=[
            scratch(X1[1], YP1, NZ),
            scratch(X1[1], YP1, LANES),
            scratch(X2[1], YP1 + 16, LANES),
            scratch(X3[1], YP2 + 24, LANES),
            scratch(X4[1], YP3 + 16, LANES),
            scratch(X4[1] * YP4, LANES),
        ],
        interpret=interpret,
        name="deposit",
    )(place, charges, fractions, cells, depth)
    everyone = lax.all_to_all(message, ("gx", "gy"), 0, 0)
    below = shifted(high, "gx", 1)
    above = shifted(low, "gx", -1)
    rows = X1[1] + 6
    count = CX // 2 + 10
    packed = (CX // 4 + 12) // 2
    fine, pair, up, down, up2, down2 = pl.pallas_call(
        merge_x_kernel,
        in_specs=[VM] * 4,
        out_specs=[VM] * 6,
        out_shape=[
            f32(rows, YP1, LANES),
            f32(count, YP2, LANES),
            f32(rows + count, 8, LANES),
            f32(rows + count, 8, LANES),
            f32(packed, 8, LANES),
            f32(packed, 8, LANES),
        ],
        interpret=interpret,
        name="merge_x",
    )(raw, part, below, above)
    below = shifted(up, "gy", 1)
    above = shifted(down, "gy", -1)
    below2 = shifted(up2, "gy", 2)
    above2 = shifted(down2, "gy", -2)
    smooth, smooth_pair = pl.pallas_call(
        stencil_kernel,
        in_specs=[VM] * 7,
        out_specs=[VM] * 2,
        out_shape=[f32(X1[1], YP1, LANES), f32(X2[1], YP2, LANES)],
        scratch_shapes=[
            scratch(rows, 32, LANES),
            scratch(count, 24, LANES),
            scratch(4, rows, YP1, LANES),
            scratch(4, count, YP2, LANES),
        ],
        interpret=interpret,
        name="stencils",
    )(fine, pair, below, above, below2, above2, jnp.asarray(spectra().astype(np.float32)))
    potential, atoms = pl.pallas_call(
        functools.partial(field_kernel, size_x=size_x, size_y=size_y),
        in_specs=[SM] + [VM] * 10,
        out_specs=[VM] * 2,
        out_shape=[f32(CX, CY, NZ), f32(1, 1, ATOMS_DEV)],
        scratch_shapes=[
            scratch(devices, LANES),
            scratch(X4[1] * YP4, LANES),
            scratch(X3[1], YP4, LANES),
            scratch(X3[1], YP3, LANES),
            scratch(X2[1], YP3, LANES),
            scratch(X2[1], YP2, LANES),
            scratch(X1[1], YP2, LANES),
            scratch(X1[1], YP1, LANES),
            scratch(X1[1], YP1, NZ),
        ],
        interpret=interpret,
        name="field",
    )(
        place, everyone.reshape(devices * 8, LANES), gather, basis, coarse_spectrum, window, smooth, smooth_pair, depth,
        fractions, cells,
    )
    return (potential, atoms)


def solution(mesh):
    placed = (P("gx", "gy", None), P("gx", "gy", None, None), P("gx", "gy", None, None))
    return jax.shard_map(
        local,
        mesh=mesh,
        in_specs=placed,
        out_specs=(P("gx", "gy", None), P("gx", "gy", None)),
        check_vma=False,
    )
```

time: 445 us -> 65.9 us (0.15); the launches traced: 438 us -> 65.6 us
  local copies, waits for them, and re-layouts: 205 us -> 3.89 us
  matrix products: 106 us -> 0 us
  blocking collectives: 37.6 us -> 0 us
  Pallas kernels: 0 us -> 34.5 us
  starting transfers between devices: 41.2 us -> 14.4 us
  other arithmetic: 21.6 us -> 0.66 us
  waiting for transfers between devices: 19.8 us -> 11.3 us
  loops' own time: 4.81 us -> 0 us
    gather x144 -> x0, local copies, waits for them, and re-layouts: 129 us -> none
    dot_general x82 -> x0, matrix products: 106 us -> none  [the longest x16 38.6 us: sample_step(): jnp.einsum('kaz,kpz->kpa', stacked, onehot_z.reshape(2, per_plane, NZ), p...]
    all_gather x1 -> x0, blocking collectives: 37.6 us -> none  [local(): lax.all_gather(level_four.reshape(1, -1), ('gx', 'gy'), axis=0, tiled=True)]
    pallas_call x0 -> x4, Pallas kernels: none -> 34.5 us  [the longest x1 14.7 us: local(): pl.pallas_call(functools.partial(field_kernel, size_x=size_x, size_y=size...]
    ppermute x24 -> x6, starting transfers between devices: 41.2 us -> 11.4 us  [shifted(): lax.ppermute(value, axis, [(source, (source + steps) % count) for source...]
    squeeze x83 -> x0, local copies, waits for them, and re-layouts: 23.9 us -> none  [the longest x48 23.7 us: local(): lax.scan(deposit_step, jnp.float32(0.0), (charge_flat, weight_x, weight_y...]
    dynamic_slice x48 -> x0, local copies, waits for them, and re-layouts: 13.6 us -> none  [local(): lax.scan(deposit_step, jnp.float32(0.0), (charge_flat, weight_x, weight_y...]
    slice x145 -> x0, local copies, waits for them, and re-layouts: 10.1 us -> none  [the longest x5 2.1 us: local(): extended[offset:offset + CX:2]]
  transfers between devices with their start and end apart: 24 -> 7, of which waited for: 16 -> 3; matrix products, arithmetic and copies ran while one was open for 37% -> 0% of each run, Pallas kernels for 0% -> 6%
where the time goes in v1:
time: 65.9 us; the launch traced here: 65.6 us
  Pallas kernels  34.5 us (52%)
  starting transfers between devices  14.4 us (22%)
  waiting for transfers between devices  11.3 us (17%)
  local copies, waits for them, and re-layouts  3.89 us (6%)
  between operations  0.69 us (1%)
  other arithmetic  0.66 us (1%)
    pallas_call x1, Pallas kernels, local(): pl.pallas_call(functools.partial(field_kernel, size_x=size_x, size_y=size...  14.7 us
    pallas_call x1, Pallas kernels, local(): pl.pallas_call(functools.partial(deposit_kernel, total_y=CY * size_y, dev...  13.4 us
    ppermute x6, starting transfers between devices, shifted(): lax.ppermute(value, axis, [(source, (source + steps) % count) for source...  11.4 us
    ppermute x6, waiting for transfers between devices, shifted(): lax.ppermute(value, axis, [(source, (source + steps) % count) for source...  11.3 us
    pallas_call x1, Pallas kernels, local(): pl.pallas_call(stencil_kernel, in_specs=[VM] * 7, out_specs=[VM] * 2, out...  4.14 us
    unnamed x19, local copies, waits for them, and re-layouts  3.89 us
    all_to_all x1, starting transfers between devices, local(): everyone = lax.all_to_all(message, ('gx', 'gy'), 0, 0)  3.1 us
    pallas_call x1, Pallas kernels, local(): pl.pallas_call(merge_x_kernel, in_specs=[VM] * 4, out_specs=[VM] * 6, out...  2.24 us
  transfers between devices with their start and end apart: 7, of which 3 were waited for; matrix products, arithmetic and copies ran while one was open for 0% of the time, Pallas kernels for 6%

profile of v1, /device:TPU:0, one launch (start us, length us, event | category | flops | bytes accessed | tf_op | source)
XLA Modules:
  0.0 65.6 jit_solution(15533673973113046967)
XLA Ops:
  0.6 1.8 %copy.11.frac_ref = f32[1,1,3,16384]{3,2,1,0:T(4,128)} copy(f32[1,1,3,16384]{3,1,2,0:T(1,128)} %param.10) | data formatting | bytes 393216 | tf_op args[1]
  2.4 0.7 %pad_add_fusion.place_ref = s32[2]{0:T(128)} fusion(s32[1]{0:T(128)} %bitcast.1, s32[1]{0:T(128)} %bitcast), kind=kLoop, calls=%fused_computation | loop fusion | flops 2 | bytes 16 | tf_op jit(solution)/shard_map/stack | solution.py:558
  3.1 13.4 %deposit.1 = (f32[35,24,128]{2,1,0:T(8,128)}, f32[20,16,128]{2,1,0:T(8,128)}, f32[272,128]{1,0:T(8,128)}, f32[272,128]{1,0:T(8,128)}, f32[32,8,128]{2,1,0:T(8,128)}) custom-call(s32[2]{0:T(128)} %pad_add_fusion.place_ref, f32[1,1,16384]{2,1,0:T(1,128)} %charge_ref.1, f32[1,1,3,16384]{3,2,1,0:T(4,128)} %copy.11.frac_ref, s32[1,1,2,16384]{3,2,1,0:T(2,128)} %cell_ref.3, ...), custom_call_target="tpu_custom_call" | custom-call | tf_op jit(solution)/shard_map/deposit/pallas_call | solution.py:562
  16.5 3.0 %collective-permute-start = (f32[272,128]{1,0:T(8,128)}, f32[272,128]{1,0:T(8,128)S(1)}, u32[]{:S(2)}, u32[]{:S(2)}) collective-permute-start(f32[272,128]{1,0:T(8,128)} %get-tuple-element.18), channel_id=1, source_target_pairs={{0,8},{8,16},{16,24},{24,0},{1,9},{9,17},{17,25},{25,1},{2,10},{10... | collective-permute-start | bytes 417800 | tf_op jit(solution)/shard_map/ppermute | solution.py:551
  19.5 1.0 %collective-permute-start.1 = (f32[272,128]{1,0:T(8,128)}, f32[272,128]{1,0:T(8,128)S(1)}, u32[]{:S(2)}, u32[]{:S(2)}) collective-permute-start(f32[272,128]{1,0:T(8,128)} %get-tuple-element.19), channel_id=1, source_target_pairs={{0,24},{8,0},{16,8},{24,16},{1,25},{9,1},{17,9},{25,17},{2,26},{10... | collective-permute-start | bytes 417800 | tf_op jit(solution)/shard_map/ppermute | solution.py:551
  20.4 4.7 %collective-permute-done.below_ref = f32[272,128]{1,0:T(8,128)S(1)} collective-permute-done((f32[272,128]{1,0:T(8,128)}, f32[272,128]{1,0:T(8,128)S(1)}, u32[]{:S(2)}, u32[]{:S(2)}) %collective-permute-start) | collective-permute-done | bytes 139296 | tf_op jit(solution)/shard_map/ppermute | solution.py:551
  25.2 0.0 copy-start.3
  25.2 2.4 %collective-permute-done.1.above_ref = f32[272,128]{1,0:T(8,128)S(1)} collective-permute-done((f32[272,128]{1,0:T(8,128)}, f32[272,128]{1,0:T(8,128)S(1)}, u32[]{:S(2)}, u32[]{:S(2)}) %collective-permute-start.1) | collective-permute-done | bytes 139296 | tf_op jit(solution)/shard_map/ppermute | solution.py:551
  27.5 0.0 copy-start.4
  27.5 0.0 copy-done.3
  27.5 0.6 copy-done.4
  28.2 2.2 %merge_x.1 = (f32[41,24,128]{2,1,0:T(8,128)}, f32[26,16,128]{2,1,0:T(8,128)}, f32[67,8,128]{2,1,0:T(8,128)}, f32[67,8,128]{2,1,0:T(8,128)}, f32[10,8,128]{2,1,0:T(8,128)}, /*index=5*/f32[10,8,128]{2,1,0:T(8,128)}) custom-call(f32[35,24,128]{2,1,0:T(8,128)} %get-tuple-element.16.raw_ref, f32[20,16,128]{2,1,0:T(8,128)} %get-tuple-element.17.part_ref, ...), custom_call_target="tpu_custom_call" | custom-call | tf_op jit(solution)/shard_map/merge_x/pallas_call | solution.py:590
  30.4 0.0 collective-permute-start.2
  30.4 3.5 %collective-permute-start.3 = (f32[67,8,128]{2,1,0:T(8,128)}, f32[67,8,128]{2,1,0:T(8,128)S(1)}, u32[]{:S(2)}, u32[]{:S(2)}) collective-permute-start(f32[67,8,128]{2,1,0:T(8,128)} %get-tuple-element.23), channel_id=1, source_target_pairs={{0,7},{1,0},{2,1},{3,2},{4,3},{5,4},{6,5},{7,6},{8,15},{9,8},{10,9... | collective-permute-start | bytes 823304 | tf_op jit(solution)/shard_map/ppermute | solution.py:551
  34.0 0.0 copy-start.8
  34.0 0.0 copy-start.7
  34.0 3.1 %all-to-all-start = ((f32[32,8,128]{2,1,0:T(8,128)}), f32[32,8,128]{2,1,0:T(8,128)S(1)}, u32[]{:S(2)}, u32[]{:S(2)}) async-start(f32[32,8,128]{2,1,0:T(8,128)} %get-tuple-element.15), calls=%async_computation | async-start | bytes 262144 | tf_op jit(solution)/shard_map/all_to_all | solution.py:584
  37.1 0.0 copy-done.8
  37.1 1.8 %collective-permute-start.4 = (f32[10,8,128]{2,1,0:T(8,128)S(1)}, f32[10,8,128]{2,1,0:T(8,128)S(1)}, u32[]{:S(2)}, u32[]{:S(2)}) collective-permute-start(f32[10,8,128]{2,1,0:T(8,128)S(1)} %copy-done.8), channel_id=1, source_target_pairs={{0,2},{1,3},{2,4},{3,5},{4,6},{5,7},{6,0},{7,1},{8,10},{9,11},{10,... | collective-permute-start | bytes 122888 | tf_op jit(solution)/shard_map/ppermute | solution.py:551
  38.9 0.0 copy-done.7
  38.9 2.1 %collective-permute-start.5 = (f32[10,8,128]{2,1,0:T(8,128)S(1)}, f32[10,8,128]{2,1,0:T(8,128)S(1)}, u32[]{:S(2)}, u32[]{:S(2)}) collective-permute-start(f32[10,8,128]{2,1,0:T(8,128)S(1)} %copy-done.7), channel_id=1, source_target_pairs={{0,6},{1,7},{2,0},{3,1},{4,2},{5,3},{6,4},{7,5},{8,14},{9,15},{10,... | collective-permute-start | bytes 122888 | tf_op jit(solution)/shard_map/ppermute | solution.py:551
  41.0 4.2 %collective-permute-done.4.below2_ref = f32[10,8,128]{2,1,0:T(8,128)S(1)} collective-permute-done((f32[10,8,128]{2,1,0:T(8,128)S(1)}, f32[10,8,128]{2,1,0:T(8,128)S(1)}, u32[]{:S(2)}, u32[]{:S(2)}) %collective-permute-start.4) | collective-permute-done | bytes 40992 | tf_op jit(solution)/shard_map/ppermute | solution.py:551
  45.2 0.0 copy-start.5
  45.2 0.0 collective-permute-done.5.above2_ref
  45.2 0.0 copy-start.6
  45.2 0.0 collective-permute-done.2.below_ref
  45.2 0.0 copy-start.1
  45.2 0.0 collective-permute-done.3.above_ref
  45.2 0.0 copy-start.2
  45.2 0.6 copy-done.5
  45.8 0.0 copy-done.6
  45.8 0.1 copy-done.1
  45.9 0.1 copy-done.2
  46.0 4.1 %stencils.1 = (f32[35,24,128]{2,1,0:T(8,128)}, f32[20,16,128]{2,1,0:T(8,128)}) custom-call(f32[41,24,128]{2,1,0:T(8,128)} %get-tuple-element.20.fine_ref, f32[26,16,128]{2,1,0:T(8,128)} %get-tuple-element.21.pair_ref, f32[67,8,128]{2,1,0:T(8,128)} %copy-done.1, f32[67,8,128]{2,1,0:T(8,128)} %copy-done.2, f32[10,8,128]{2,1,0:T(8,128)} %copy-done.5, ...), custom_call_target="tpu_custom_call" | custom-call | tf_op jit(solution)/shard_map/stencils/pallas_call | solution.py:609
  50.2 0.0 all-to-all-done
  50.2 0.0 copy-start
  50.2 0.7 copy-done
  50.8 14.7 %field.1 = (f32[32,16,128]{2,1,0:T(8,128)}, f32[1,1,16384]{2,1,0:T(1,128)}) custom-call(s32[2]{0:T(128)} %pad_add_fusion.place_ref, f32[256,128]{1,0:T(8,128)} %bitcast.3, f32[16,40]{1,0:T(8,128)} %constant.21.clone.gather_ref, f32[256,256]{1,0:T(8,128)} %constant.22.clone.basis_ref, f32[16,256]{1,0:T(8,128)} %constant.23.clone.spectrum_ref, ...), custom_call_target="tpu_custom_call" | custom-call | tf_op jit(solution)/shard_map/field/pallas_call | solution.py:623
Async XLA Ops:
  16.5 8.7 %collective-permute-start = (f32[272,128]{1,0:T(8,128)}, f32[272,128]{1,0:T(8,128)S(1)}, u32[]{:S(2)}, u32[]{:S(2)}) collective-permute-start(f32[272,128]{1,0:T(8,128)} %get-tuple-element.18), channel_id=1, source_target_pairs={{0,8},{8,16},{16,24},{24,0},{1,9},{9,17},{17,25},{25,1},{2,10},{10... | collective-permute-start | bytes 417800 | tf_op jit(solution)/shard_map/ppermute | solution.py:551
  19.5 8.1 %collective-permute-start.1 = (f32[272,128]{1,0:T(8,128)}, f32[272,128]{1,0:T(8,128)S(1)}, u32[]{:S(2)}, u32[]{:S(2)}) collective-permute-start(f32[272,128]{1,0:T(8,128)} %get-tuple-element.19), channel_id=1, source_target_pairs={{0,24},{8,0},{16,8},{24,16},{1,25},{9,1},{17,9},{25,17},{2,26},{10... | collective-permute-start | bytes 417800 | tf_op jit(solution)/shard_map/ppermute | solution.py:551
  25.2 2.4 %copy-start.3 = (f32[272,128]{1,0:T(8,128)}, f32[272,128]{1,0:T(8,128)S(1)}, u32[]{:S(2)}) copy-start(f32[272,128]{1,0:T(8,128)S(1)} %collective-permute-done.below_ref) | copy-start | bytes 417796
  27.5 0.7 copy-start.4
  30.4 14.8 %collective-permute-start.2 = (f32[67,8,128]{2,1,0:T(8,128)}, f32[67,8,128]{2,1,0:T(8,128)S(1)}, u32[]{:S(2)}, u32[]{:S(2)}) collective-permute-start(f32[67,8,128]{2,1,0:T(8,128)} %get-tuple-element.22), channel_id=1, source_target_pairs={{0,1},{1,2},{2,3},{3,4},{4,5},{5,6},{6,7},{7,0},{8,9},{9,10},{10,1... | collective-permute-start | bytes 823304 | tf_op jit(solution)/shard_map/ppermute | solution.py:551
  30.4 14.8 %collective-permute-start.3 = (f32[67,8,128]{2,1,0:T(8,128)}, f32[67,8,128]{2,1,0:T(8,128)S(1)}, u32[]{:S(2)}, u32[]{:S(2)}) collective-permute-start(f32[67,8,128]{2,1,0:T(8,128)} %get-tuple-element.23), channel_id=1, source_target_pairs={{0,7},{1,0},{2,1},{3,2},{4,3},{5,4},{6,5},{7,6},{8,15},{9,8},{10,9... | collective-permute-start | bytes 823304 | tf_op jit(solution)/shard_map/ppermute | solution.py:551
  34.0 3.1 %copy-start.8 = (f32[10,8,128]{2,1,0:T(8,128)S(1)}, f32[10,8,128]{2,1,0:T(8,128)}, u32[]{:S(2)}) copy-start(f32[10,8,128]{2,1,0:T(8,128)} %get-tuple-element.24) | copy-start | bytes 122884
  34.0 4.9 %copy-start.7 = (f32[10,8,128]{2,1,0:T(8,128)S(1)}, f32[10,8,128]{2,1,0:T(8,128)}, u32[]{:S(2)}) copy-start(f32[10,8,128]{2,1,0:T(8,128)} %get-tuple-element.25) | copy-start | bytes 122884
  34.0 16.2 %all-to-all-start = ((f32[32,8,128]{2,1,0:T(8,128)}), f32[32,8,128]{2,1,0:T(8,128)S(1)}, u32[]{:S(2)}, u32[]{:S(2)}) async-start(f32[32,8,128]{2,1,0:T(8,128)} %get-tuple-element.15), calls=%async_computation | async-start | bytes 262144 | tf_op jit(solution)/shard_map/all_to_all | solution.py:584
  37.1 8.1 %collective-permute-start.4 = (f32[10,8,128]{2,1,0:T(8,128)S(1)}, f32[10,8,128]{2,1,0:T(8,128)S(1)}, u32[]{:S(2)}, u32[]{:S(2)}) collective-permute-start(f32[10,8,128]{2,1,0:T(8,128)S(1)} %copy-done.8), channel_id=1, source_target_pairs={{0,2},{1,3},{2,4},{3,5},{4,6},{5,7},{6,0},{7,1},{8,10},{9,11},{10,... | collective-permute-start | bytes 122888 | tf_op jit(solution)/shard_map/ppermute | solution.py:551
  38.9 6.3 %collective-permute-start.5 = (f32[10,8,128]{2,1,0:T(8,128)S(1)}, f32[10,8,128]{2,1,0:T(8,128)S(1)}, u32[]{:S(2)}, u32[]{:S(2)}) collective-permute-start(f32[10,8,128]{2,1,0:T(8,128)S(1)} %copy-done.7), channel_id=1, source_target_pairs={{0,6},{1,7},{2,0},{3,1},{4,2},{5,3},{6,4},{7,5},{8,14},{9,15},{10,... | collective-permute-start | bytes 122888 | tf_op jit(solution)/shard_map/ppermute | solution.py:551
  45.2 0.6 copy-start.5
  45.2 0.6 copy-start.6
  45.2 0.7 %copy-start.1 = (f32[67,8,128]{2,1,0:T(8,128)}, f32[67,8,128]{2,1,0:T(8,128)S(1)}, u32[]{:S(2)}) copy-start(f32[67,8,128]{2,1,0:T(8,128)S(1)} %collective-permute-done.2.below_ref) | copy-start | bytes 823300
  45.2 0.8 %copy-start.2 = (f32[67,8,128]{2,1,0:T(8,128)}, f32[67,8,128]{2,1,0:T(8,128)S(1)}, u32[]{:S(2)}) copy-start(f32[67,8,128]{2,1,0:T(8,128)S(1)} %collective-permute-done.3.above_ref) | copy-start | bytes 823300
  50.2 0.7 copy-start

commit v2 on v1

v2 whole, which is shorter than its diff:
```python
import functools

import jax
import jax.numpy as jnp
import numpy as np
from jax import lax
from jax.experimental import pallas as pl
from jax.experimental.pallas import tpu as pltpu
from jax.sharding import PartitionSpec as P

CX = 32
CY = 16
NZ = 128
ATOMS_DEV = 16384

HIGHEST = lax.Precision.HIGHEST
RESTRICT_TAPS = ((-3, -0.0625), (-1, 0.5625), (0, 1.0), (1, 0.5625), (3, -0.0625))
PER_PLANE = ATOMS_DEV // CX
LANES = 128
CHUNKS = PER_PLANE // LANES
Z2, Z3, Z4 = (NZ // 2, NZ // 4, NZ // 8)
LANE3 = Z2
LANE4 = Z2 + Z3

X1, Y1 = (0, CX + 3), (0, CY + 3)


def coarser(window):
    first, count = window
    last = first + count - 1
    starts = [m for m in range(first - 4, last + 4) if any(first <= 2 * m + k <= last for k, _ in RESTRICT_TAPS)]
    return (starts[0], starts[-1] - starts[0] + 1)


X2, Y2 = coarser(X1), coarser(Y1)
X3, Y3 = coarser(X2), coarser(Y2)
X4, Y4 = coarser(X3), coarser(Y3)


def up8(count):
    return -(-count // 8) * 8


SLAB2 = 6 * Y1[1]
SLAB3 = SLAB2 + 4 * Y2[1]
SLAB = up8(SLAB3 + 2 * Y3[1])
FINE_X = X1[1] + 6
PAIR_X = CX // 2 + 10
SPAN3 = CX // 4 + 11
PACK2 = (PAIR_X + 1) // 2
PACK3 = (SPAN3 + 3) // 4
EDGE2 = up8(6 * FINE_X)
EDGE3 = EDGE2 + 8 * PACK2
EDGE = EDGE3 + 8 * PACK3
FAR = up8(4 * PACK3)
YP1, YP2, YP3, YP4 = (up8(Y1[1]), up8(Y2[1]), up8(Y3[1]), up8(Y4[1]))
PAD = 8


def real_basis(count):
    places = np.arange(count)
    rows = [np.full(count, 1.0 / np.sqrt(count))]
    for k in range(1, count // 2):
        rows.append(np.sqrt(2.0 / count) * np.cos(2 * np.pi * k * places / count))
        rows.append(np.sqrt(2.0 / count) * np.sin(2 * np.pi * k * places / count))
    rows.append(np.where(places % 2 == 0, 1.0, -1.0) / np.sqrt(count))
    return np.stack(rows)


def basis_frequency(count):
    return np.array([0] + [k for k in range(1, count // 2) for _ in range(2)] + [count // 2])


def restrict_matrix(count):
    matrix = np.zeros((count // 2, count))
    for m in range(count // 2):
        for k, weight in RESTRICT_TAPS:
            matrix[m, (2 * m + k) % count] += weight
    return matrix


def depth_matrix():
    first = restrict_matrix(NZ)
    second = restrict_matrix(Z2) @ first
    third = restrict_matrix(Z3) @ second
    parts = [real_basis(NZ), real_basis(Z2) @ first, real_basis(Z3) @ second, real_basis(Z4) @ third]
    parts.append(np.zeros((2 * LANES - sum(p.shape[0] for p in parts), NZ)))
    return np.concatenate(parts, axis=0)


def split_numpy(value):
    high = value.astype(np.float32).astype(jnp.bfloat16)
    low = (value - high.astype(np.float64)).astype(np.float32).astype(jnp.bfloat16)
    return high, low


def depth_tables():
    high, low = split_numpy(depth_matrix())
    down = np.concatenate([high.T, high.T, low.T], axis=0)
    up = np.concatenate([high, high, low], axis=0)
    return jnp.asarray(down), jnp.asarray(up)


def smooth_numpy(rho):
    return np.where(rho < 1.0, 1.875 - 1.25 * rho * rho + 0.375 * rho**4, 1.0 / np.maximum(rho, 1.0))


def stencil_spectrum(level, count):
    offsets = np.arange(-3, 4) * 1.0
    near = np.arange(0, 4) * 1.0
    radius = np.sqrt(near[:, None, None] ** 2 + near[None, :, None] ** 2 + offsets[None, None, :] ** 2)
    stencil = (smooth_numpy(radius / 1.5) / 1.5 - smooth_numpy(radius / 3.0) / 3.0) / 2.0 ** (level - 1)
    waves = np.cos(2 * np.pi * offsets[:, None] * basis_frequency(count)[None, :] / count)
    return np.einsum("abd,dk->abk", stencil, waves)


def spectra():
    fine = stencil_spectrum(1, NZ).reshape(16, NZ)
    coarse = np.zeros((16, LANES))
    coarse[:, :Z2] = stencil_spectrum(2, Z2).reshape(16, Z2)
    coarse[:, LANE3:LANE4] = stencil_spectrum(3, Z3).reshape(16, Z3)
    return np.stack([fine, coarse])


def signed(count):
    places = np.arange(count)
    return np.where(places > count // 2, places - count, places) * 1.0


def coarse_tables(size_x, size_y):
    total_x = CX // 8 * size_x
    total_y = CY // 8 * size_y
    first = signed(total_x)[:, None, None]
    second = signed(total_y)[None, :, None]
    third = signed(Z4)[None, None, :]
    kernel = smooth_numpy(np.sqrt(first**2 + second**2 + third**2) / 1.5) / 12.0

    def cosines(count):
        return np.cos(2 * np.pi * basis_frequency(count)[:, None] * np.arange(count)[None, :] / count)

    spectrum = np.einsum("xyz,ax,by,cz->abc", kernel, cosines(total_x), cosines(total_y), cosines(Z4), optimize=True)
    spectrum = spectrum.reshape(total_x, total_y * Z4)
    basis_x = real_basis(total_x)
    basis_y = np.kron(real_basis(total_y), np.eye(Z4))
    span = X4[1]
    tail = up8(size_x)
    gather = np.zeros((total_x, 8 * size_x + tail))
    window = np.zeros((size_x, up8(span), total_x))
    for i in range(size_x):
        for a in range(span):
            place = (i * (CX // 8) + X4[0] + a) % total_x
            gather[:, i * 8 + a if a < 8 else 8 * size_x + i] = basis_x[:, place]
            window[i, a, :] = basis_x[:, place]
    return [t.astype(np.float32) for t in (gather, basis_y, spectrum, window)]


def spline_weights(frac):
    def near_weight(distance):
        return (1.0 - distance) * (1.0 + distance - 1.5 * distance * distance)

    def far_weight(distance):
        return -0.5 * (distance - 1.0) * (2.0 - distance) * (2.0 - distance)

    return [far_weight(1.0 + frac), near_weight(frac), near_weight(1.0 - frac), far_weight(2.0 - frac)]


ROWS = ATOMS_DEV // LANES
GROUP = 4
TILES_Y = YP1 // 8
TILES_Z = NZ // 16
REAL_X, REAL_Y, REAL_Z, REAL_TY, REAL_TZ = 0, 4, 8, 12, 14
REALS, PLACES = 16, 8


def fill_tables(reals, places, charge, frac_ref, cell_ref, total_y):
    first_y = lax.axis_index("gy") * CY + 1

    def put(ref, index, value):
        ref[index * ROWS : (index + 1) * ROWS, :] = value

    for dim, base in ((0, REAL_X), (1, REAL_Y), (2, REAL_Z)):
        weights = spline_weights(frac_ref[dim])
        for tap in range(4):
            put(reals, base + tap, weights[tap] if charge is None or dim else weights[tap] * charge)
    block_y = cell_ref[pl.ds(0, ROWS, stride=2), :] - first_y
    block_y = jnp.where(block_y < 0, block_y + total_y, block_y)
    block_z = (cell_ref[pl.ds(1, ROWS, stride=2), :] - 1) & (NZ - 1)
    for tap in range(4):
        put(places, tap, (block_y + tap) & 7)
        put(places, 4 + tap, (block_z + tap) & 15)
    tile_y = block_y >> 3
    tile_z = block_z >> 4
    put(reals, REAL_TY, tile_y.astype(jnp.float32))
    put(reals, REAL_TY + 1, (tile_y + 1).astype(jnp.float32))
    put(reals, REAL_TZ, tile_z.astype(jnp.float32))
    put(reals, REAL_TZ + 1, ((tile_z + 1) & (TILES_Z - 1)).astype(jnp.float32))


def spread_row(ref, index, row):
    return ref[pl.ds(index * ROWS + row, 8, stride=0), :]


def pattern_y(reals, places, row):
    index = lax.broadcasted_iota(jnp.int32, (8, LANES), 0)
    table = jnp.zeros((8, LANES), jnp.float32)
    for tap in range(4):
        place = spread_row(places, tap, row)
        table = jnp.where(index == place, spread_row(reals, REAL_Y + tap, row), table)
    start = spread_row(places, 0, row)
    tile = jnp.where(index >= start, spread_row(reals, REAL_TY, row), spread_row(reals, REAL_TY + 1, row))
    return table, tile


def along_z(reals, places, row):
    index = lax.broadcasted_iota(jnp.int32, (8, LANES), 0)
    parts, tiles = [], []
    for half in range(2):
        table = jnp.zeros((8, LANES), jnp.float32)
        for tap in range(4):
            place = spread_row(places, 4 + tap, row)
            table = jnp.where(index + 8 * half == place, spread_row(reals, REAL_Z + tap, row), table)
        start = spread_row(places, 4, row)
        tiles.append(
            jnp.where(index + 8 * half >= start, spread_row(reals, REAL_TZ, row), spread_row(reals, REAL_TZ + 1, row))
        )
        parts.append(table)
    high, low = halves(jnp.concatenate(parts, axis=0))
    tile = jnp.concatenate(tiles, axis=0).astype(jnp.bfloat16)
    zero = jnp.zeros((16, LANES), jnp.bfloat16)
    highs, lows = [], []
    for t in range(TILES_Z):
        same = tile == jnp.bfloat16(t)
        highs.append(jnp.where(same, high, zero))
        lows.append(jnp.where(same, low, zero))
    return highs, lows


def along_xy(reals, places, row):
    table, tile = pattern_y(reals, places, row)
    tile = jnp.concatenate([tile, tile], axis=0).astype(jnp.bfloat16)
    zero = jnp.zeros((16, LANES), jnp.bfloat16)
    same = [tile == jnp.bfloat16(t) for t in range(TILES_Y)]
    highs, lows = [], []
    for pair in range(2):
        both = [table * spread_row(reals, REAL_X + 2 * pair + m, row) for m in range(2)]
        high, low = halves(jnp.concatenate(both, axis=0))
        highs += [jnp.where(mask, high, zero) for mask in same]
        lows += [jnp.where(mask, low, zero) for mask in same]
    return highs + lows


def triple(value):
    high, low = halves(value)
    return jnp.concatenate([high, low, high], axis=1)


def halves(value):
    high = value.astype(jnp.bfloat16)
    low = (value - high.astype(jnp.float32)).astype(jnp.bfloat16)
    return high, low


def lane_index(shape):
    return lax.broadcasted_iota(jnp.int32, shape, len(shape) - 1)


def restrict_x(load, window_in, window_out):
    first, count = window_in
    outs = []
    for m in range(window_out[0], window_out[0] + window_out[1]):
        total = None
        for k, weight in RESTRICT_TAPS:
            place = 2 * m + k - first
            if 0 <= place < count:
                term = load(place) if weight == 1.0 else weight * load(place)
                total = term if total is None else total + term
        outs.append(total)
    return outs


def restrict_y(source, window_in, window_out, rows_out):
    total = None
    for k, weight in RESTRICT_TAPS:
        start = 2 * window_out[0] + k - window_in[0] + PAD
        term = source[:, pl.ds(start, rows_out, stride=2), :]
        term = term if weight == 1.0 else weight * term
        total = term if total is None else total + term
    places = lax.broadcasted_iota(jnp.int32, total.shape, 1)
    return jnp.where(places < window_out[1], total, 0.0)


def deposit_kernel(
    charge_ref, frac_ref, cell_ref, depth_ref,
    raw_ref, part_ref, low_ref, high_ref, message_ref,
    reals, places, grid, coarse, half2, half3, half4, last,
    *, total_y, devices,
):
    fill_tables(reals, places, charge_ref[...], frac_ref, cell_ref, total_y)
    grid[...] = jnp.zeros_like(grid)
    half_rows = 4 * YP1

    def step(group, carry):
        sums = [[None] * TILES_Y for _ in range(GROUP + 3)]
        for p in range(GROUP):
            lefts, rights = [], []
            for chunk in range(CHUNKS):
                row = (group * GROUP + p) * CHUNKS + chunk
                lefts.append(jnp.concatenate(along_xy(reals, places, row), axis=0))
                highs, lows = along_z(reals, places, row)
                rights.append(jnp.concatenate(highs + lows, axis=0))
            left = jnp.concatenate(lefts, axis=1)
            right = jnp.concatenate(rights, axis=1)
            product = lax.dot_general(left, right, (((1,), (1,)), ((), ())), preferred_element_type=jnp.float32)
            for m in range(4):
                for t in range(TILES_Y):
                    at = ((m // 2) * TILES_Y + t) * 16 + (m % 2) * 8
                    layer = product[at : at + 8, :NZ] + product[at : at + 8, NZ:]
                    layer = layer + product[half_rows + at : half_rows + at + 8, :NZ]
                    old = sums[p + m][t]
                    sums[p + m][t] = layer if old is None else old + layer
        for i in range(GROUP + 3):
            at = group * GROUP + i
            grid[at] = grid[at] + jnp.concatenate(sums[i], axis=0)
        return carry

    lax.fori_loop(0, CX // GROUP, step, 0)
    flat = triple(grid[...].reshape(X1[1] * YP1, NZ))
    below = jnp.dot(flat, depth_ref[...], preferred_element_type=jnp.float32)
    raw_ref[...] = below[:, :LANES].reshape(X1[1], YP1, LANES)
    coarse[...] = below[:, LANES:].reshape(X1[1], YP1, LANES)

    def padded(half, outs, rows):
        half[...] = jnp.zeros_like(half)
        for i, value in enumerate(outs):
            half[i, PAD : PAD + rows, :] = value

    padded(half2, restrict_x(lambda i: coarse[i], X1, X2), YP1)
    level2 = restrict_y(half2, Y1, Y2, YP2)
    padded(half3, restrict_x(lambda i: level2[i], X2, X3), YP2)
    level3 = restrict_y(half3, Y2, Y3, YP3)
    padded(half4, restrict_x(lambda i: level3[i], X3, X4), YP3)
    last[...] = restrict_y(half4, Y3, Y4, YP4).reshape(X4[1] * YP4, LANES)

    lane2 = lane_index((YP2, LANES)) < Z2
    for i in range(X2[1]):
        other = level3[i] if i < X3[1] else jnp.zeros((YP2, LANES), jnp.float32)
        part_ref[i] = jnp.where(lane2, level2[i], other)
    for r in range(6):
        at = slice(r * Y1[1], (r + 1) * Y1[1])
        low_ref[at, :] = raw_ref[r, 0 : Y1[1], :]
        high_ref[at, :] = raw_ref[CX - 3 + r, 0 : Y1[1], :]
    base2 = CX // 2 - 4 - X2[0]
    base3 = CX // 4 - 5 - X3[0]
    for ref, at2, at3 in ((low_ref, 0, 0), (high_ref, base2, base3)):
        for r in range(4):
            first = part_ref[at2 + r, 0 : Y2[1], :]
            if r < 3:
                second = pltpu.roll(part_ref[at2 + 4 + r, 0 : YP2, :], Z2, 1)[: Y2[1]]
            else:
                second = jnp.zeros((Y2[1], LANES), jnp.float32)
            at = SLAB2 + r * Y2[1]
            ref[at : at + Y2[1], :] = jnp.where(lane_index((Y2[1], LANES)) < Z2, first, second)
        for r in range(2):
            total = jnp.zeros((YP3, LANES), jnp.float32)
            lanes3 = lane_index((YP3, LANES))
            for g in range(4):
                moved = part_ref[at3 + 2 * g + r, 0:YP3, :]
                moved = pltpu.roll(moved, (g * Z3 - LANE3) % LANES, 1)
                total = jnp.where((lanes3 >= g * Z3) & (lanes3 < (g + 1) * Z3), moved, total)
            at = SLAB3 + r * Y3[1]
            ref[at : at + Y3[1], :] = total[: Y3[1]]
        ref[SLAB3 + 2 * Y3[1] :, :] = jnp.zeros((SLAB - SLAB3 - 2 * Y3[1], LANES), jnp.float32)
    lanes = lane_index((8, LANES))
    message = jnp.zeros((8, LANES), jnp.float32)
    for b in range(Y4[1]):
        rows = last[pl.ds(b, 8, stride=YP4), :]
        moved = pltpu.roll(rows, (b * Z4 - LANE4) % LANES, 1)
        message = jnp.where((lanes >= b * Z4) & (lanes < (b + 1) * Z4), moved, message)
    tail = pltpu.roll(last[8 * YP4 : 9 * YP4, :], Y4[1] * Z4 - LANE4, 1)
    message = jnp.where(lanes >= Y4[1] * Z4, tail, message)
    for d in range(devices):
        message_ref[d] = message


def merge_pair(part_ref, below_ref, above_ref, pair, row0):
    lane2 = lane_index((Y2[1], LANES)) < Z2
    lanes3 = lane_index((Y3[1], LANES))
    inside3 = (lanes3 >= LANE3) & (lanes3 < LANE4)

    def add(x, value):
        if x < PAIR_X:
            rows = slice(row0, row0 + value.shape[0])
            pair[x, rows, :] = pair[x, rows, :] + value

    for r in range(X2[1]):
        pair[3 + r, row0 : row0 + YP2, :] = part_ref[r]
    for ref, at2, at3 in ((below_ref, 0, 0), (above_ref, CX // 2 + 3, CX // 4 + 3)):
        for r in range(4):
            both = ref[SLAB2 + r * Y2[1] : SLAB2 + (r + 1) * Y2[1], :]
            add(at2 + r, jnp.where(lane2, both, 0.0))
            if r < 3:
                add(at2 + 4 + r, jnp.where(lane2, pltpu.roll(both, Z2, 1), 0.0))
        for r in range(2):
            four = ref[SLAB3 + r * Y3[1] : SLAB3 + (r + 1) * Y3[1], :]
            for g in range(4):
                moved = pltpu.roll(four, (LANE3 - g * Z3) % LANES, 1)
                add(at3 + 2 * g + r, jnp.where(inside3, moved, 0.0))


def edges_kernel(raw_ref, part_ref, below_ref, above_ref, up_ref, down_ref, up2_ref, down2_ref, pair):
    for x in range(FINE_X):
        for ref, start in ((up_ref, CY - 3), (down_ref, 0)):
            value = None
            if 3 <= x < FINE_X - 3:
                value = raw_ref[x - 3, start : start + 6, :]
            for slab, at in ((below_ref, x), (above_ref, x - CX - 3)):
                if 0 <= at < 6:
                    extra = slab[at * Y1[1] + start : at * Y1[1] + start + 6, :]
                    value = extra if value is None else value + extra
            ref[6 * x : 6 * x + 6, :] = value
    pair[...] = jnp.zeros_like(pair)
    merge_pair(part_ref, below_ref, above_ref, pair, 0)
    low2 = lane_index((8, LANES)) < Z2
    lanes = lane_index((8, LANES))
    keep = lax.broadcasted_iota(jnp.int32, (8, LANES), 0) < 7
    zero = jnp.zeros((8, LANES), jnp.float32)
    for ref, far, at2, at3, at_far in (
        (up_ref, up2_ref, CY // 2 - 3, CY // 4 - 3, CY // 2 - 3),
        (down_ref, down2_ref, 0, 0, 0),
    ):
        if EDGE2 > 6 * FINE_X:
            ref[6 * FINE_X : EDGE2, :] = jnp.zeros((EDGE2 - 6 * FINE_X, LANES), jnp.float32)
        for r in range(PACK2):
            first = pair[r, at2 : at2 + 8, :]
            second = zero
            if r + PACK2 < PAIR_X:
                second = pltpu.roll(pair[r + PACK2, at2 : at2 + 8, :], Z2, 1)
            ref[EDGE2 + 8 * r : EDGE2 + 8 * r + 8, :] = jnp.where(keep, jnp.where(low2, first, second), 0.0)
        for r in range(PACK3):
            total, total_far = zero, zero
            for g in range(4):
                x = g * PACK3 + r
                if x >= SPAN3:
                    continue
                inside = (lanes >= g * Z3) & (lanes < (g + 1) * Z3)
                turn = (g * Z3 - LANE3) % LANES
                total = jnp.where(inside, pltpu.roll(pair[x, at3 : at3 + 8, :], turn, 1), total)
                total_far = jnp.where(inside, pltpu.roll(pair[x, at_far : at_far + 8, :], turn, 1), total_far)
            ref[EDGE3 + 8 * r : EDGE3 + 8 * r + 8, :] = total
            far[4 * r : 4 * r + 4, :] = total_far[0:4]
        if FAR > 4 * PACK3:
            far[4 * PACK3 :, :] = jnp.zeros((FAR - 4 * PACK3, LANES), jnp.float32)


def merge_fine(raw_ref, below_ref, above_ref, south_ref, north_ref, fine):
    fine[...] = jnp.zeros_like(fine)
    for x in range(FINE_X):
        if 3 <= x < FINE_X - 3:
            fine[x, 3 : 3 + YP1, :] = raw_ref[x - 3]
        for slab, at in ((below_ref, x), (above_ref, x - CX - 3)):
            if 0 <= at < 6:
                rows = slice(3, 3 + Y1[1])
                fine[x, rows, :] = fine[x, rows, :] + slab[at * Y1[1] : (at + 1) * Y1[1], :]
        fine[x, 0:6, :] = fine[x, 0:6, :] + south_ref[6 * x : 6 * x + 6, :]
        fine[x, CY + 3 : CY + 9, :] = fine[x, CY + 3 : CY + 9, :] + north_ref[6 * x : 6 * x + 6, :]


def merge_coarse(part_ref, below_ref, above_ref, south_ref, north_ref, south2_ref, north2_ref, pair):
    pair[...] = jnp.zeros_like(pair)
    merge_pair(part_ref, below_ref, above_ref, pair, 3)
    low2 = lane_index((8, LANES)) < Z2
    lanes = lane_index((8, LANES))
    inside = (lanes >= LANE3) & (lanes < LANE4)
    for ref, far, at2, at3, at_far in (
        (south_ref, south2_ref, 0, 0, 0),
        (north_ref, north2_ref, CY // 2 + 3, CY // 4 + 3, CY // 2 + 3),
    ):
        for r in range(PACK2):
            both = ref[EDGE2 + 8 * r : EDGE2 + 8 * r + 8, :]
            pair[r, at2 : at2 + 8, :] = pair[r, at2 : at2 + 8, :] + jnp.where(low2, both, 0.0)
            x = r + PACK2
            if x < PAIR_X:
                moved = jnp.where(low2, pltpu.roll(both, Z2, 1), 0.0)
                pair[x, at2 : at2 + 8, :] = pair[x, at2 : at2 + 8, :] + moved
        for r in range(PACK3):
            four = ref[EDGE3 + 8 * r : EDGE3 + 8 * r + 8, :]
            four_far = far[4 * r : 4 * r + 4, :]
            for g in range(4):
                x = g * PACK3 + r
                if x >= SPAN3:
                    continue
                turn = (LANE3 - g * Z3) % LANES
                moved = jnp.where(inside, pltpu.roll(four, turn, 1), 0.0)
                pair[x, at3 : at3 + 8, :] = pair[x, at3 : at3 + 8, :] + moved
                moved = jnp.where(inside[0:4], pltpu.roll(four_far, turn, 1), 0.0)
                pair[x, at_far : at_far + 4, :] = pair[x, at_far : at_far + 4, :] + moved


def stencil_rows(source, count, rows_out, table, target, planes):
    for i in range(count + 6):
        sums = [source[i, 3 : 3 + rows_out, :]]
        for b in range(1, 4):
            sums.append(source[i, 3 - b : 3 - b + rows_out, :] + source[i, 3 + b : 3 + b + rows_out, :])
        for a in range(4):
            value = table[4 * a : 4 * a + 1] * sums[0]
            for b in range(1, 4):
                value = value + table[4 * a + b : 4 * a + b + 1] * sums[b]
            planes[a, i] = value
    for i in range(count):
        value = planes[0, i + 3]
        for a in range(1, 4):
            value = value + (planes[a, i + 3 - a] + planes[a, i + 3 + a])
        target[i] = value


def prolong_x(load, window_in, window_out):
    outs = []
    first = window_in[0]
    for n in range(window_out[0], window_out[0] + window_out[1]):
        if n % 2 == 0:
            outs.append(load(n // 2 - first))
        else:
            m = (n - 1) // 2 - first
            outs.append(0.5625 * (load(m) + load(m + 1)) - 0.0625 * (load(m - 1) + load(m + 2)))
    return outs


def prolong_y(source, window_in, window_out, target):
    first, count = window_out
    even = first % 2
    evens = (count - even + 1) // 2
    start = (first + even) // 2 - window_in[0]
    target[:, pl.ds(even, evens, stride=2), :] = source[:, start : start + evens, :]
    odds = count - evens
    m = (first + 1 - even - 1) // 2 - window_in[0]

    def taken(shift):
        return source[:, m + shift : m + shift + odds, :]

    target[:, pl.ds(1 - even, odds, stride=2), :] = 0.5625 * (taken(0) + taken(1)) - 0.0625 * (taken(-1) + taken(2))


def rise(load, window_in, window_out, wide_in, wide_out, half, target):
    target[...] = jnp.zeros_like(target)
    for r, value in enumerate(prolong_x(load, window_in, window_out)):
        half[r] = value
    prolong_y(half, wide_in, wide_out, target)


def coarse_kernel(
    message_ref, gather_ref, basis_ref, spectrum_ref, window_ref, level3_ref, ninth, level4, half3, *, size_x, size_y
):
    devices = size_x * size_y
    width = CY // 8 * size_y * Z4
    blocks = width // LANES
    used = Y4[1] * Z4
    tails = lane_index((devices, LANES))
    gathered = jnp.zeros((devices, LANES), jnp.float32)
    for b in range(Y4[1]):
        rows = message_ref[pl.ds(b, devices, stride=8), :]
        moved = pltpu.roll(rows, (b * Z4 - used) % LANES, 1)
        gathered = jnp.where((tails >= b * Z4) & (tails < (b + 1) * Z4), moved, gathered)
    ninth[...] = gathered

    def assemble(load, rows):
        total = [jnp.zeros((rows, LANES), jnp.float32) for _ in range(blocks)]
        lanes = lane_index((rows, LANES))
        for j in range(size_y):
            position = (j * (CY // 8) + Y4[0]) * Z4 % width
            block, offset = (position // LANES, position % LANES)
            value = jnp.where(lanes < used, load(j), 0.0)
            if offset == 0:
                total[block] = total[block] + value
                continue
            value = pltpu.roll(value, offset, 1)
            following = (block + 1) % blocks
            total[block] = total[block] + jnp.where(lanes >= offset, value, 0.0)
            total[following] = total[following] + jnp.where(lanes < offset, value, 0.0)
        return jnp.concatenate(total, axis=1)

    strips = []
    for i in range(size_x):
        strips.append(assemble(lambda j: message_ref[(i * size_y + j) * 8 : (i * size_y + j + 1) * 8, :], 8))
    tail = assemble(lambda j: ninth[pl.ds(j, size_x, stride=size_y), :], size_x)
    if size_x % 8:
        tail = jnp.concatenate([tail, jnp.zeros((8 - size_x % 8, width), jnp.float32)], axis=0)
    strips.append(tail)
    strips = jnp.concatenate(strips, axis=0)
    exact = dict(precision=HIGHEST, preferred_element_type=jnp.float32)
    modes = jnp.dot(gather_ref[...], strips, **exact)
    modes = lax.dot_general(modes, basis_ref[...], (((1,), (1,)), ((), ())), **exact)
    modes = jnp.dot(modes * spectrum_ref[...], basis_ref[...], **exact)
    shift = (width - (lax.axis_index("gy") * (CY // 8) + Y4[0]) * Z4) % width
    modes = pltpu.roll(modes, shift, 1)[:, :LANES]
    own = jnp.dot(window_ref[lax.axis_index("gx")], modes, **exact)
    lanes = lane_index(own.shape)
    inside4 = (lanes >= LANE4) & (lanes < LANE4 + Z4)
    level4[...] = jnp.zeros_like(level4)
    for b in range(Y4[1]):
        moved = jnp.where(inside4, pltpu.roll(own, (LANE4 - b * Z4) % LANES, 1), 0.0)
        level4[pl.ds(b, X4[1], stride=YP4), :] = moved[: X4[1]]

    rise(lambda i: level4[i * YP4 : (i + 1) * YP4, :], X4, X3, Y4, Y3, half3, level3_ref)


def field_kernel(
    raw_ref, part_ref, below_ref, above_ref, south_ref, north_ref, south2_ref, north2_ref,
    coarse_ref, spectrum_ref, depth_ref, frac_ref, cell_ref,
    potential_ref, atom_ref,
    reals, places, fine, pair, planes, planes_pair, smooth, smooth_pair,
    level3, half2, level2, half1, level1, field, partial,
    *, total_y,
):
    fill_tables(reals, places, None, frac_ref, cell_ref, total_y)
    merge_fine(raw_ref, below_ref, above_ref, south_ref, north_ref, fine)
    merge_coarse(part_ref, below_ref, above_ref, south_ref, north_ref, south2_ref, north2_ref, pair)
    stencil_rows(pair, X2[1], YP2, spectrum_ref[1], smooth_pair, planes_pair)
    lanes3 = lane_index((YP3, LANES))
    inside3 = (lanes3 >= LANE3) & (lanes3 < LANE4)
    for r in range(X3[1]):
        level3[r] = coarse_ref[r] + jnp.where(inside3, smooth_pair[r, 0:YP3, :], 0.0)
    rise(lambda i: level3[i], X3, X2, Y3, Y2, half2, level2)
    inside2 = lane_index((YP2, LANES)) < Z2
    for r in range(X2[1]):
        level2[r] = level2[r] + jnp.where(inside2, smooth_pair[r], 0.0)
    rise(lambda i: level2[i], X2, X1, Y2, Y1, half1, level1)
    stencil_rows(fine, X1[1], YP1, spectrum_ref[0], smooth, planes)

    rows = X1[1] * YP1
    modes = jnp.concatenate([smooth[...].reshape(rows, LANES), level1[...].reshape(rows, LANES)], axis=1)
    total = jnp.dot(triple(modes), depth_ref[...], preferred_element_type=jnp.float32)
    field[...] = total.reshape(X1[1], YP1, NZ)
    potential_ref[...] = field[0:CX, 0:CY, :]

    def step(group, carry):
        for p in range(GROUP):
            plane = group * GROUP + p
            high, low = halves(jnp.concatenate([field[plane + m] for m in range(4)], axis=0))
            left = jnp.concatenate([high, high, low], axis=1)
            rights = []
            for chunk in range(CHUNKS):
                highs, lows = along_z(reals, places, plane * CHUNKS + chunk)
                rights.append(jnp.concatenate(highs + lows + highs, axis=0))
            product = jnp.dot(left, jnp.concatenate(rights, axis=1), preferred_element_type=jnp.float32)
            for chunk in range(CHUNKS):
                row = plane * CHUNKS + chunk
                lanes = slice(chunk * LANES, (chunk + 1) * LANES)
                weights = [spread_row(reals, REAL_X + m, row) for m in range(4)]
                table, tile = pattern_y(reals, places, row)
                value = None
                for t in range(TILES_Y):
                    layer = None
                    for m in range(4):
                        at = m * YP1 + 8 * t
                        term = product[at : at + 8, lanes] * weights[m]
                        layer = term if layer is None else layer + term
                    value = layer if value is None else jnp.where(tile == t, layer, value)
                partial[pl.ds(row * 8, 8), :] = value * table
        return carry

    lax.fori_loop(0, CX // GROUP, step, 0)
    for g in range(ROWS // 8):
        total = partial[pl.ds(g * 64, 8, stride=8), :]
        for r in range(1, 8):
            total = total + partial[pl.ds(g * 64 + r, 8, stride=8), :]
        atom_ref[g * 8 : g * 8 + 8, :] = total


VM = pl.BlockSpec(memory_space=pltpu.VMEM)


def f32(*shape):
    return jax.ShapeDtypeStruct(shape, jnp.float32)


def scratch(*shape):
    return pltpu.VMEM(shape, jnp.float32)


def shifted(value, axis, steps):
    count = lax.axis_size(axis)
    return lax.ppermute(value, axis, [(source, (source + steps) % count) for source in range(count)])


def integers(*shape):
    return pltpu.VMEM(shape, jnp.int32)


def call(kernel, name, outs, scratches, *operands):
    return pl.pallas_call(
        kernel,
        in_specs=[VM] * len(operands),
        out_specs=[VM] * len(outs),
        out_shape=outs,
        scratch_shapes=scratches,
        name=name,
    )(*operands)


def local(charges, fractions, cells):
    size_x = lax.axis_size("gx")
    size_y = lax.axis_size("gy")
    devices = size_x * size_y
    total_y = CY * size_y
    down_table, up_table = depth_tables()
    gather, basis, coarse_spectrum, window = (jnp.asarray(t) for t in coarse_tables(size_x, size_y))
    charge = charges.reshape(ROWS, LANES)
    frac = fractions.reshape(3, ROWS, LANES)
    cell = cells.reshape(2, ROWS, LANES).transpose(1, 0, 2).reshape(2 * ROWS, LANES)
    raw, part, low, high, message = call(
        functools.partial(deposit_kernel, total_y=total_y, devices=devices),
        "deposit",
        [
            f32(X1[1], YP1, LANES),
            f32(X2[1], YP2, LANES),
            f32(SLAB, LANES),
            f32(SLAB, LANES),
            f32(devices, 8, LANES),
        ],
        [
            scratch(REALS * ROWS, LANES),
            integers(PLACES * ROWS, LANES),
            scratch(X1[1], YP1, NZ),
            scratch(X1[1], YP1, LANES),
            scratch(X2[1], YP1 + 16, LANES),
            scratch(X3[1], YP2 + 24, LANES),
            scratch(X4[1], YP3 + 16, LANES),
            scratch(X4[1] * YP4, LANES),
        ],
        charge, frac, cell, down_table,
    )
    everyone = lax.all_to_all(message, ("gx", "gy"), 0, 0)
    below = shifted(high, "gx", 1)
    above = shifted(low, "gx", -1)
    up, down, up2, down2 = call(
        edges_kernel,
        "edges",
        [f32(EDGE, LANES), f32(EDGE, LANES), f32(FAR, LANES), f32(FAR, LANES)],
        [scratch(PAIR_X, YP2, LANES)],
        raw, part, below, above,
    )
    south = shifted(up, "gy", 1)
    north = shifted(down, "gy", -1)
    south2 = shifted(up2, "gy", 2)
    north2 = shifted(down2, "gy", -2)
    (coarse,) = call(
        functools.partial(coarse_kernel, size_x=size_x, size_y=size_y),
        "coarse",
        [f32(X3[1], YP3, LANES)],
        [scratch(devices, LANES), scratch(X4[1] * YP4, LANES), scratch(X3[1], YP4, LANES)],
        everyone.reshape(devices * 8, LANES), gather, basis, coarse_spectrum, window,
    )
    potential, atoms = call(
        functools.partial(field_kernel, total_y=total_y),
        "field",
        [f32(CX, CY, NZ), f32(ROWS, LANES)],
        [
            scratch(REALS * ROWS, LANES),
            integers(PLACES * ROWS, LANES),
            scratch(FINE_X, 32, LANES),
            scratch(PAIR_X, 24, LANES),
            scratch(4, FINE_X, YP1, LANES),
            scratch(4, PAIR_X, YP2, LANES),
            scratch(X1[1], YP1, LANES),
            scratch(X2[1], YP2, LANES),
            scratch(X3[1], YP3, LANES),
            scratch(X2[1], YP3, LANES),
            scratch(X2[1], YP2, LANES),
            scratch(X1[1], YP2, LANES),
            scratch(X1[1], YP1, LANES),
            scratch(X1[1], YP1, NZ),
            scratch(8 * ROWS, LANES),
        ],
        raw, part, below, above, south, north, south2, north2,
        coarse, jnp.asarray(spectra().astype(np.float32)), up_table, frac, cell,
    )
    return (potential, atoms.reshape(1, 1, ATOMS_DEV))


def solution(mesh):
    placed = (P("gx", "gy", None), P("gx", "gy", None, None), P("gx", "gy", None, None))
    return jax.shard_map(
        local,
        mesh=mesh,
        in_specs=placed,
        out_specs=(P("gx", "gy", None), P("gx", "gy", None)),
        check_vma=False,
    )
```

time: 65.9 us -> 40.1 us (0.61)
  Pallas kernels: 34.5 us -> 19.7 us
  waiting for transfers between devices: 11.3 us -> 0.02 us
  starting transfers between devices: 14.4 us -> 16.7 us
  local copies, waits for them, and re-layouts: 3.89 us -> 2.65 us
  other arithmetic: 0.66 us -> 0 us
    pallas_call x4, Pallas kernels: 34.5 us -> 19.7 us  [call(): pl.pallas_call(kernel, in_specs=[VM] * len(operands), out_specs=[VM] * le...]
    ppermute x6, waiting for transfers between devices: 11.3 us -> 0.02 us  [shifted(): lax.ppermute(value, axis, [(source, (source + steps) % count) for source...]
    all_to_all x1, starting transfers between devices: 3.1 us -> 5.42 us  [local(): everyone = lax.all_to_all(message, ('gx', 'gy'), 0, 0)]
    unnamed x19 -> x14, local copies, waits for them, and re-layouts: 3.89 us -> 2.65 us
    another operation x1 -> x0, other arithmetic: 0.66 us -> none  [local(): jnp.stack([lax.axis_index('gx'), lax.axis_index('gy')]).astype(jnp.int32)]
  transfers between devices with their start and end apart: 7 -> 7, of which waited for: 3 -> 0; matrix products, arithmetic and copies ran while one was open for 0% -> 0% of each run, Pallas kernels for 6% -> 13%
where the time goes in v2:
time: 40.1 us; the launch traced here: 39.8 us
  Pallas kernels  19.7 us (49%)
  starting transfers between devices  16.7 us (42%)
  local copies, waits for them, and re-layouts  2.65 us (7%)
  between operations  0.71 us (2%)
    pallas_call x4, Pallas kernels, call(): pl.pallas_call(kernel, in_specs=[VM] * len(operands), out_specs=[VM] * le...  19.7 us
    ppermute x6, starting transfers between devices, shifted(): lax.ppermute(value, axis, [(source, (source + steps) % count) for source...  11.3 us
    all_to_all x1, starting transfers between devices, local(): everyone = lax.all_to_all(message, ('gx', 'gy'), 0, 0)  5.42 us
    unnamed x14, local copies, waits for them, and re-layouts  2.65 us
  transfers between devices with their start and end apart: 7, of which 0 were waited for; matrix products, arithmetic and copies ran while one was open for 0% of the time, Pallas kernels for 13%

profile of v2, /device:TPU:0, one launch (start us, length us, event | category | flops | bytes accessed | tf_op | source)
XLA Modules:
  0.0 39.8 jit_solution(8134619263701179265)
XLA Ops:
  0.6 6.8 %deposit.1 = (f32[35,24,128]{2,1,0:T(8,128)}, f32[20,16,128]{2,1,0:T(8,128)}, f32[184,128]{1,0:T(8,128)}, f32[184,128]{1,0:T(8,128)}, f32[32,8,128]{2,1,0:T(8,128)}) custom-call(f32[128,128]{1,0:T(8,128)} %bitcast.14, f32[3,128,128]{2,1,0:T(8,128)} %bitcast.9, s32[256,128]{1,0:T(8,128)} %bitcast.11, bf16[384,256]{1,0:T(8,128)(2,1)} %constant.14.clone.depth_ref), custom_call_target="tpu_custom_call" | custom-call | tf_op jit(solution)/shard_map/deposit/pallas_call | solution.py:690
  7.4 3.0 %collective-permute-start = (f32[184,128]{1,0:T(8,128)}, f32[184,128]{1,0:T(8,128)S(1)}, u32[]{:S(2)}, u32[]{:S(2)}) collective-permute-start(f32[184,128]{1,0:T(8,128)} %get-tuple-element.15), channel_id=1, source_target_pairs={{0,8},{8,16},{16,24},{24,0},{1,9},{9,17},{17,25},{25,1},{2,10},{10... | collective-permute-start | bytes 282632 | tf_op jit(solution)/shard_map/ppermute | solution.py:682
  10.4 1.0 %collective-permute-start.1 = (f32[184,128]{1,0:T(8,128)}, f32[184,128]{1,0:T(8,128)S(1)}, u32[]{:S(2)}, u32[]{:S(2)}) collective-permute-start(f32[184,128]{1,0:T(8,128)} %get-tuple-element.16), channel_id=1, source_target_pairs={{0,24},{8,0},{16,8},{24,16},{1,25},{9,1},{17,9},{25,17},{2,26},{10... | collective-permute-start | bytes 282632 | tf_op jit(solution)/shard_map/ppermute | solution.py:682
  11.4 5.4 %all-to-all-start = ((f32[32,8,128]{2,1,0:T(8,128)}), f32[32,8,128]{2,1,0:T(8,128)S(1)}, u32[]{:S(2)}, u32[]{:S(2)}) async-start(f32[32,8,128]{2,1,0:T(8,128)} %get-tuple-element.21), calls=%async_computation | async-start | bytes 262144 | tf_op jit(solution)/shard_map/all_to_all | solution.py:732
  16.8 0.0 collective-permute-done.below_ref
  16.8 0.0 copy-start.1
  16.8 0.0 collective-permute-done.1.above_ref
  16.8 0.0 copy-start.2
  16.8 0.6 %copy-done.1 = f32[184,128]{1,0:T(8,128)} copy-done((f32[184,128]{1,0:T(8,128)}, f32[184,128]{1,0:T(8,128)S(1)}, u32[]{:S(2)}) %copy-start.1) | copy-done | bytes 94232
  17.4 0.0 copy-done.2
  17.5 2.1 %edges.1 = (f32[392,128]{1,0:T(8,128)}, f32[392,128]{1,0:T(8,128)}, f32[24,128]{1,0:T(8,128)}, f32[24,128]{1,0:T(8,128)}) custom-call(f32[35,24,128]{2,1,0:T(8,128)} %get-tuple-element.13.raw_ref, f32[20,16,128]{2,1,0:T(8,128)} %get-tuple-element.14.part_ref, f32[184,128]{1,0:T(8,128)} %copy-done.1, f32[184,128]{1,0:T(8,128)} %copy-done.2), custom_call_target="tpu_custom_call" | custom-call | tf_op jit(solution)/shard_map/edges/pallas_call | solution.py:690
  19.6 0.3 collective-permute-start.2
  19.9 3.3 %collective-permute-start.3 = (f32[392,128]{1,0:T(8,128)}, f32[392,128]{1,0:T(8,128)S(1)}, u32[]{:S(2)}, u32[]{:S(2)}) collective-permute-start(f32[392,128]{1,0:T(8,128)} %get-tuple-element.18), channel_id=1, source_target_pairs={{0,7},{1,0},{2,1},{3,2},{4,3},{5,4},{6,5},{7,6},{8,15},{9,8},{10,9... | collective-permute-start | bytes 602120 | tf_op jit(solution)/shard_map/ppermute | solution.py:682
  23.1 0.0 collective-permute-start.4
  23.1 3.8 %collective-permute-start.5 = (f32[24,128]{1,0:T(8,128)}, f32[24,128]{1,0:T(8,128)S(1)}, u32[]{:S(2)}, u32[]{:S(2)}) collective-permute-start(f32[24,128]{1,0:T(8,128)} %get-tuple-element.20), channel_id=1, source_target_pairs={{0,6},{1,7},{2,0},{3,1},{4,2},{5,3},{6,4},{7,5},{8,14},{9,15},{10,... | collective-permute-start | bytes 36872 | tf_op jit(solution)/shard_map/ppermute | solution.py:682
  27.0 0.0 all-to-all-done
  27.0 0.0 copy-start
  27.0 0.6 %copy-done = f32[32,8,128]{2,1,0:T(8,128)} copy-done((f32[32,8,128]{2,1,0:T(8,128)}, f32[32,8,128]{2,1,0:T(8,128)S(1)}, u32[]{:S(2)}) %copy-start) | copy-done | bytes 131096
  27.6 3.0 %coarse.1.coarse_ref = f32[13,16,128]{2,1,0:T(8,128)} custom-call(f32[256,128]{1,0:T(8,128)} %bitcast.13, f32[16,40]{1,0:T(8,128)} %constant.16.clone.gather_ref, f32[256,256]{1,0:T(8,128)} %constant.17.clone.basis_ref, f32[16,256]{1,0:T(8,128)} %constant.18.clone.spectrum_ref, f32[4,16,16]{2,1,0:T(8,128)} %constant.19.clone.window_ref), custom_call_target="tpu_custom_call" | custom-call | tf_op jit(solution)/shard_map/coarse/pallas_call | solution.py:690
  30.6 0.0 collective-permute-done.4.south2_ref
  30.6 0.0 copy-start.5
  30.6 0.0 collective-permute-done.5.north2_ref
  30.6 0.0 copy-start.6
  30.6 0.0 collective-permute-done.2.south_ref
  30.7 0.0 copy-start.3
  30.7 0.0 collective-permute-done.3.north_ref
  30.7 0.5 %copy-done.5 = f32[24,128]{1,0:T(8,128)} copy-done((f32[24,128]{1,0:T(8,128)}, f32[24,128]{1,0:T(8,128)S(1)}, u32[]{:S(2)}) %copy-start.5) | copy-done | bytes 12312
  31.2 0.0 copy-done.6
  31.2 0.1 copy-done.3
  31.3 0.0 copy-start.4
  31.3 0.7 %copy-done.4 = f32[392,128]{1,0:T(8,128)} copy-done((f32[392,128]{1,0:T(8,128)}, f32[392,128]{1,0:T(8,128)S(1)}, u32[]{:S(2)}) %copy-start.4) | copy-done | bytes 200728
  32.0 7.8 %field.1 = (f32[32,16,128]{2,1,0:T(8,128)}, f32[128,128]{1,0:T(8,128)}) custom-call(f32[35,24,128]{2,1,0:T(8,128)} %get-tuple-element.13.raw_ref, f32[20,16,128]{2,1,0:T(8,128)} %get-tuple-element.14.part_ref, f32[184,128]{1,0:T(8,128)} %copy-done.1, f32[184,128]{1,0:T(8,128)} %copy-done.2, f32[392,128]{1,0:T(8,128)} %copy-done.3, f32[392,128]{1,0:T(8,128)} %copy-done.4, ...), custom_call_target="tpu_custom_call" | custom-call | tf_op jit(solution)/shard_map/field/pallas_call | solution.py:690
Async XLA Ops:
  7.4 9.4 %collective-permute-start = (f32[184,128]{1,0:T(8,128)}, f32[184,128]{1,0:T(8,128)S(1)}, u32[]{:S(2)}, u32[]{:S(2)}) collective-permute-start(f32[184,128]{1,0:T(8,128)} %get-tuple-element.15), channel_id=1, source_target_pairs={{0,8},{8,16},{16,24},{24,0},{1,9},{9,17},{17,25},{25,1},{2,10},{10... | collective-permute-start | bytes 282632 | tf_op jit(solution)/shard_map/ppermute | solution.py:682
  10.4 6.4 %collective-permute-start.1 = (f32[184,128]{1,0:T(8,128)}, f32[184,128]{1,0:T(8,128)S(1)}, u32[]{:S(2)}, u32[]{:S(2)}) collective-permute-start(f32[184,128]{1,0:T(8,128)} %get-tuple-element.16), channel_id=1, source_target_pairs={{0,24},{8,0},{16,8},{24,16},{1,25},{9,1},{17,9},{25,17},{2,26},{10... | collective-permute-start | bytes 282632 | tf_op jit(solution)/shard_map/ppermute | solution.py:682
  11.4 15.6 %all-to-all-start = ((f32[32,8,128]{2,1,0:T(8,128)}), f32[32,8,128]{2,1,0:T(8,128)S(1)}, u32[]{:S(2)}, u32[]{:S(2)}) async-start(f32[32,8,128]{2,1,0:T(8,128)} %get-tuple-element.21), calls=%async_computation | async-start | bytes 262144 | tf_op jit(solution)/shard_map/all_to_all | solution.py:732
  16.8 0.6 %copy-start.1 = (f32[184,128]{1,0:T(8,128)}, f32[184,128]{1,0:T(8,128)S(1)}, u32[]{:S(2)}) copy-start(f32[184,128]{1,0:T(8,128)S(1)} %collective-permute-done.below_ref) | copy-start | bytes 282628
  16.8 0.7 %copy-start.2 = (f32[184,128]{1,0:T(8,128)}, f32[184,128]{1,0:T(8,128)S(1)}, u32[]{:S(2)}) copy-start(f32[184,128]{1,0:T(8,128)S(1)} %collective-permute-done.1.above_ref) | copy-start | bytes 282628
  19.6 11.0 %collective-permute-start.2 = (f32[392,128]{1,0:T(8,128)}, f32[392,128]{1,0:T(8,128)S(1)}, u32[]{:S(2)}, u32[]{:S(2)}) collective-permute-start(f32[392,128]{1,0:T(8,128)} %get-tuple-element.17), channel_id=1, source_target_pairs={{0,1},{1,2},{2,3},{3,4},{4,5},{5,6},{6,7},{7,0},{8,9},{9,10},{10,1... | collective-permute-start | bytes 602120 | tf_op jit(solution)/shard_map/ppermute | solution.py:682
  19.9 10.8 %collective-permute-start.3 = (f32[392,128]{1,0:T(8,128)}, f32[392,128]{1,0:T(8,128)S(1)}, u32[]{:S(2)}, u32[]{:S(2)}) collective-permute-start(f32[392,128]{1,0:T(8,128)} %get-tuple-element.18), channel_id=1, source_target_pairs={{0,7},{1,0},{2,1},{3,2},{4,3},{5,4},{6,5},{7,6},{8,15},{9,8},{10,9... | collective-permute-start | bytes 602120 | tf_op jit(solution)/shard_map/ppermute | solution.py:682
  23.1 7.5 %collective-permute-start.4 = (f32[24,128]{1,0:T(8,128)}, f32[24,128]{1,0:T(8,128)S(1)}, u32[]{:S(2)}, u32[]{:S(2)}) collective-permute-start(f32[24,128]{1,0:T(8,128)} %get-tuple-element.19), channel_id=1, source_target_pairs={{0,2},{1,3},{2,4},{3,5},{4,6},{5,7},{6,0},{7,1},{8,10},{9,11},{10,... | collective-permute-start | bytes 36872 | tf_op jit(solution)/shard_map/ppermute | solution.py:682
  23.1 7.5 %collective-permute-start.5 = (f32[24,128]{1,0:T(8,128)}, f32[24,128]{1,0:T(8,128)S(1)}, u32[]{:S(2)}, u32[]{:S(2)}) collective-permute-start(f32[24,128]{1,0:T(8,128)} %get-tuple-element.20), channel_id=1, source_target_pairs={{0,6},{1,7},{2,0},{3,1},{4,2},{5,3},{6,4},{7,5},{8,14},{9,15},{10,... | collective-permute-start | bytes 36872 | tf_op jit(solution)/shard_map/ppermute | solution.py:682
  27.0 0.6 %copy-start = (f32[32,8,128]{2,1,0:T(8,128)}, f32[32,8,128]{2,1,0:T(8,128)S(1)}, u32[]{:S(2)}) copy-start(f32[32,8,128]{2,1,0:T(8,128)S(1)} %all-to-all-done) | copy-start | bytes 393220
  30.6 0.6 %copy-start.5 = (f32[24,128]{1,0:T(8,128)}, f32[24,128]{1,0:T(8,128)S(1)}, u32[]{:S(2)}) copy-start(f32[24,128]{1,0:T(8,128)S(1)} %collective-permute-done.4.south2_ref) | copy-start | bytes 36868
  30.6 0.6 %copy-start.6 = (f32[24,128]{1,0:T(8,128)}, f32[24,128]{1,0:T(8,128)S(1)}, u32[]{:S(2)}) copy-start(f32[24,128]{1,0:T(8,128)S(1)} %collective-permute-done.5.north2_ref) | copy-start | bytes 36868
  30.7 0.7 %copy-start.3 = (f32[392,128]{1,0:T(8,128)}, f32[392,128]{1,0:T(8,128)S(1)}, u32[]{:S(2)}) copy-start(f32[392,128]{1,0:T(8,128)S(1)} %collective-permute-done.2.south_ref) | copy-start | bytes 602116
  31.3 0.7 %copy-start.4 = (f32[392,128]{1,0:T(8,128)}, f32[392,128]{1,0:T(8,128)S(1)}, u32[]{:S(2)}) copy-start(f32[392,128]{1,0:T(8,128)S(1)} %collective-permute-done.3.north_ref) | copy-start | bytes 602116

commit v3 on v2

--- a/solution.py
+++ b/solution.py
@@ -165,7 +165,7 @@
 
 
 ROWS = ATOMS_DEV // LANES
-GROUP = 4
+GROUP = 16
 TILES_Y = YP1 // 8
 TILES_Z = NZ // 16
 REAL_X, REAL_Y, REAL_Z, REAL_TY, REAL_TZ = 0, 4, 8, 12, 14
@@ -669,7 +669,12 @@
 VM = pl.BlockSpec(memory_space=pltpu.VMEM)
 
 
+RESIDENT = 2**19
+
+
 def f32(*shape):
+    if 4 * int(np.prod(shape)) <= RESIDENT:
+        return pltpu.VMEM(shape, jnp.float32)
     return jax.ShapeDtypeStruct(shape, jnp.float32)
 
 
@@ -695,6 +700,13 @@
         scratch_shapes=scratches,
         name=name,
     )(*operands)
+
+
+def resident(*values):
+    return [
+        pltpu.with_memory_space_constraint(value, pltpu.VMEM) if value.nbytes <= RESIDENT else value
+        for value in values
+    ]
 
 
 def local(charges, fractions, cells):
@@ -737,7 +749,7 @@
         "edges",
         [f32(EDGE, LANES), f32(EDGE, LANES), f32(FAR, LANES), f32(FAR, LANES)],
         [scratch(PAIR_X, YP2, LANES)],
-        raw, part, below, above,
+        *resident(raw, part, below, above),
     )
     south = shifted(up, "gy", 1)
     north = shifted(down, "gy", -1)
@@ -748,12 +760,12 @@
         "coarse",
         [f32(X3[1], YP3, LANES)],
         [scratch(devices, LANES), scratch(X4[1] * YP4, LANES), scratch(X3[1], YP4, LANES)],
-        everyone.reshape(devices * 8, LANES), gather, basis, coarse_spectrum, window,
+        *resident(everyone.reshape(devices * 8, LANES), gather, basis, coarse_spectrum, window),
     )
     potential, atoms = call(
         functools.partial(field_kernel, total_y=total_y),
         "field",
-        [f32(CX, CY, NZ), f32(ROWS, LANES)],
+        [jax.ShapeDtypeStruct((CX, CY, NZ), jnp.float32), jax.ShapeDtypeStruct((ROWS, LANES), jnp.float32)],
         [
             scratch(REALS * ROWS, LANES),
             integers(PLACES * ROWS, LANES),
@@ -771,8 +783,8 @@
             scratch(X1[1], YP1, NZ),
             scratch(8 * ROWS, LANES),
         ],
-        raw, part, below, above, south, north, south2, north2,
-        coarse, jnp.asarray(spectra().astype(np.float32)), up_table, frac, cell,
+        *resident(raw, part, below, above, south, north, south2, north2),
+        *resident(coarse, jnp.asarray(spectra().astype(np.float32)), up_table, frac, cell),
     )
     return (potential, atoms.reshape(1, 1, ATOMS_DEV))
 

time: 40.1 us -> 32.8 us (0.82)
  Pallas kernels: 19.7 us -> 12.7 us
  local copies, waits for them, and re-layouts: 2.65 us -> 0.05 us
  waiting for transfers between devices: 0.02 us -> 2.33 us
    pallas_call x4, Pallas kernels: 19.7 us -> 12.7 us  [call(): pl.pallas_call(kernel, in_specs=[VM] * len(operands), out_specs=[VM] * le...]
    unnamed x14 -> x16, local copies, waits for them, and re-layouts: 2.65 us -> 0.05 us
    ppermute x6, waiting for transfers between devices: 0.02 us -> 1.85 us  [shifted(): lax.ppermute(value, axis, [(source, (source + steps) % count) for source...]
    all_to_all x1, waiting for transfers between devices: 0.01 us -> 0.48 us  [local(): everyone = lax.all_to_all(message, ('gx', 'gy'), 0, 0)]
  transfers between devices with their start and end apart: 7 -> 7, of which waited for: 0 -> 2; matrix products, arithmetic and copies ran while one was open for 0% -> 0% of each run, Pallas kernels for 13% -> 5%
where the time goes in v3:
time: 32.8 us; the launch traced here: 32.6 us
  starting transfers between devices  16.8 us (51%)
  Pallas kernels  12.7 us (39%)
  waiting for transfers between devices  2.33 us (7%)
  between operations  0.78 us (2%)
    pallas_call x4, Pallas kernels, call(): pl.pallas_call(kernel, in_specs=[VM] * len(operands), out_specs=[VM] * le...  12.7 us
    ppermute x6, starting transfers between devices, shifted(): lax.ppermute(value, axis, [(source, (source + steps) % count) for source...  11.3 us
    all_to_all x1, starting transfers between devices, local(): everyone = lax.all_to_all(message, ('gx', 'gy'), 0, 0)  5.43 us
    ppermute x6, waiting for transfers between devices, shifted(): lax.ppermute(value, axis, [(source, (source + steps) % count) for source...  1.85 us
  transfers between devices with their start and end apart: 7, of which 2 were waited for; matrix products, arithmetic and copies ran while one was open for 0% of the time, Pallas kernels for 5%

profile of v3, /device:TPU:0, one launch (start us, length us, event | category | flops | bytes accessed | tf_op | source)
XLA Modules:
  0.0 32.6 jit_solution(2762165625191755390)
XLA Ops:
  0.6 5.7 %deposit.1 = (f32[35,24,128]{2,1,0:T(8,128)S(1)}, f32[20,16,128]{2,1,0:T(8,128)S(1)}, f32[184,128]{1,0:T(8,128)S(1)}, f32[184,128]{1,0:T(8,128)S(1)}, f32[32,8,128]{2,1,0:T(8,128)}) custom-call(f32[128,128]{1,0:T(8,128)} %bitcast.14, f32[3,128,128]{2,1,0:T(8,128)} %bitcast.9, s32[256,128]{1,0:T(8,128)} %bitcast.11, bf16[384,256]{1,0:T(8,128)(2,1)} %constant.14.clone.depth_ref), custom_call_target="tpu_custom_call" | custom-call | tf_op jit(solution)/shard_map/deposit/pallas_call | solution.py:695
  6.3 3.0 %collective-permute-start = (f32[184,128]{1,0:T(8,128)S(1)}, f32[184,128]{1,0:T(8,128)S(1)}, u32[]{:S(2)}, u32[]{:S(2)}) collective-permute-start(f32[184,128]{1,0:T(8,128)S(1)} %get-tuple-element.15), channel_id=1, source_target_pairs={{0,8},{8,16},{16,24},{24,0},{1,9},{9,17},{17,25},{25,1},{2,10},{10... | collective-permute-start | bytes 282632 | tf_op jit(solution)/shard_map/ppermute | solution.py:687
  9.2 1.0 %collective-permute-start.1 = (f32[184,128]{1,0:T(8,128)S(1)}, f32[184,128]{1,0:T(8,128)S(1)}, u32[]{:S(2)}, u32[]{:S(2)}) collective-permute-start(f32[184,128]{1,0:T(8,128)S(1)} %get-tuple-element.16), channel_id=1, source_target_pairs={{0,24},{8,0},{16,8},{24,16},{1,25},{9,1},{17,9},{25,17},{2,26},{10... | collective-permute-start | bytes 282632 | tf_op jit(solution)/shard_map/ppermute | solution.py:687
  10.2 5.4 %all-to-all-start = ((f32[32,8,128]{2,1,0:T(8,128)}), f32[32,8,128]{2,1,0:T(8,128)S(1)}, u32[]{:S(2)}, u32[]{:S(2)}) async-start(f32[32,8,128]{2,1,0:T(8,128)} %get-tuple-element.21), calls=%async_computation | async-start | bytes 262144 | tf_op jit(solution)/shard_map/all_to_all | solution.py:744
  15.6 0.0 collective-permute-done.below_ref
  15.7 0.0 collective-permute-done.1.above_ref
  15.7 0.0 copy-start.2
  15.7 0.0 copy-start.4
  15.7 0.0 copy-start.6
  15.7 0.3 edges.1
  16.0 0.0 copy-start.7
  16.0 0.3 collective-permute-start.2
  16.3 3.3 %collective-permute-start.3 = (f32[392,128]{1,0:T(8,128)S(1)}, f32[392,128]{1,0:T(8,128)S(1)}, u32[]{:S(2)}, u32[]{:S(2)}) collective-permute-start(f32[392,128]{1,0:T(8,128)S(1)} %get-tuple-element.18), channel_id=1, source_target_pairs={{0,7},{1,0},{2,1},{3,2},{4,3},{5,4},{6,5},{7,6},{8,15},{9,8},{10,9... | collective-permute-start | bytes 602120 | tf_op jit(solution)/shard_map/ppermute | solution.py:687
  19.6 0.0 collective-permute-start.4
  19.6 3.8 %collective-permute-start.5 = (f32[24,128]{1,0:T(8,128)S(1)}, f32[24,128]{1,0:T(8,128)S(1)}, u32[]{:S(2)}, u32[]{:S(2)}) collective-permute-start(f32[24,128]{1,0:T(8,128)S(1)} %get-tuple-element.20), channel_id=1, source_target_pairs={{0,6},{1,7},{2,0},{3,1},{4,2},{5,3},{6,4},{7,5},{8,14},{9,15},{10,... | collective-permute-start | bytes 36872 | tf_op jit(solution)/shard_map/ppermute | solution.py:687
  23.4 0.5 %all-to-all-done = f32[32,8,128]{2,1,0:T(8,128)S(1)} async-done(((f32[32,8,128]{2,1,0:T(8,128)}), f32[32,8,128]{2,1,0:T(8,128)S(1)}, u32[]{:S(2)}, u32[]{:S(2)}) %all-to-all-start) | async-done | bytes 131104 | tf_op jit(solution)/shard_map/all_to_all | solution.py:744
  23.9 0.0 copy-done.2
  23.9 0.0 copy-done.4
  23.9 0.0 copy-done.6
  23.9 0.0 copy-done.7
  23.9 0.0 copy-start
  23.9 0.0 copy-start.1
  23.9 0.0 copy-start.3
  23.9 0.0 copy-start.5
  24.0 1.3 %coarse.1.coarse_ref = f32[13,16,128]{2,1,0:T(8,128)S(1)} custom-call(f32[256,128]{1,0:T(8,128)S(1)} %bitcast.13, f32[16,40]{1,0:T(8,128)S(1)} %copy-done.7, f32[256,256]{1,0:T(8,128)S(1)} %copy-done.2, f32[16,256]{1,0:T(8,128)S(1)} %copy-done.6, f32[4,16,16]{2,1,0:T(8,128)S(1)} %copy-done.4), custom_call_target="tpu_custom_call" | custom-call | tf_op jit(solution)/shard_map/coarse/pallas_call | solution.py:695
  25.3 1.8 %collective-permute-done.4.south2_ref = f32[24,128]{1,0:T(8,128)S(1)} collective-permute-done((f32[24,128]{1,0:T(8,128)S(1)}, f32[24,128]{1,0:T(8,128)S(1)}, u32[]{:S(2)}, u32[]{:S(2)}) %collective-permute-start.4) | collective-permute-done | bytes 12320 | tf_op jit(solution)/shard_map/ppermute | solution.py:687
  27.1 0.0 collective-permute-done.5.north2_ref
  27.1 0.0 collective-permute-done.2.south_ref
  27.1 0.0 collective-permute-done.3.north_ref
  27.1 0.0 copy-done
  27.2 0.0 copy-done.1
  27.2 0.0 copy-done.3
  27.2 0.0 copy-done.5
  27.2 5.4 %field.1 = (f32[32,16,128]{2,1,0:T(8,128)}, f32[128,128]{1,0:T(8,128)}) custom-call(f32[35,24,128]{2,1,0:T(8,128)S(1)} %get-tuple-element.13.raw_ref, f32[20,16,128]{2,1,0:T(8,128)S(1)} %get-tuple-element.14.part_ref, f32[184,128]{1,0:T(8,128)S(1)} %collective-permute-done.below_ref, f32[184,128]{1,0:T(8,128)S(1)} %collective-permute-done.1.above_ref, ...), custom_call_target="tpu_custom_call" | custom-call | tf_op jit(solution)/shard_map/field/pallas_call | solution.py:695
Async XLA Ops:
  6.3 9.4 %collective-permute-start = (f32[184,128]{1,0:T(8,128)S(1)}, f32[184,128]{1,0:T(8,128)S(1)}, u32[]{:S(2)}, u32[]{:S(2)}) collective-permute-start(f32[184,128]{1,0:T(8,128)S(1)} %get-tuple-element.15), channel_id=1, source_target_pairs={{0,8},{8,16},{16,24},{24,0},{1,9},{9,17},{17,25},{25,1},{2,10},{10... | collective-permute-start | bytes 282632 | tf_op jit(solution)/shard_map/ppermute | solution.py:687
  9.2 6.4 %collective-permute-start.1 = (f32[184,128]{1,0:T(8,128)S(1)}, f32[184,128]{1,0:T(8,128)S(1)}, u32[]{:S(2)}, u32[]{:S(2)}) collective-permute-start(f32[184,128]{1,0:T(8,128)S(1)} %get-tuple-element.16), channel_id=1, source_target_pairs={{0,24},{8,0},{16,8},{24,16},{1,25},{9,1},{17,9},{25,17},{2,26},{10... | collective-permute-start | bytes 282632 | tf_op jit(solution)/shard_map/ppermute | solution.py:687
  10.2 13.7 %all-to-all-start = ((f32[32,8,128]{2,1,0:T(8,128)}), f32[32,8,128]{2,1,0:T(8,128)S(1)}, u32[]{:S(2)}, u32[]{:S(2)}) async-start(f32[32,8,128]{2,1,0:T(8,128)} %get-tuple-element.21), calls=%async_computation | async-start | bytes 262144 | tf_op jit(solution)/shard_map/all_to_all | solution.py:744
  15.7 8.2 %copy-start.2 = (f32[256,256]{1,0:T(8,128)S(1)}, f32[256,256]{1,0:T(8,128)}, u32[]{:S(2)}) copy-start(f32[256,256]{1,0:T(8,128)} %constant.17.clone.basis_ref) | copy-start | bytes 786436
  15.7 8.2 %copy-start.4 = (f32[4,16,16]{2,1,0:T(8,128)S(1)}, f32[4,16,16]{2,1,0:T(8,128)}, u32[]{:S(2)}) copy-start(f32[4,16,16]{2,1,0:T(8,128)} %constant.19.clone.window_ref) | copy-start | bytes 12292
  15.7 8.2 %copy-start.6 = (f32[16,256]{1,0:T(8,128)S(1)}, f32[16,256]{1,0:T(8,128)}, u32[]{:S(2)}) copy-start(f32[16,256]{1,0:T(8,128)} %constant.18.clone.spectrum_ref) | copy-start | bytes 49156
  16.0 7.9 %copy-start.7 = (f32[16,40]{1,0:T(8,128)S(1)}, f32[16,40]{1,0:T(8,128)}, u32[]{:S(2)}) copy-start(f32[16,40]{1,0:T(8,128)} %constant.16.clone.gather_ref) | copy-start | bytes 7684
  16.0 11.1 %collective-permute-start.2 = (f32[392,128]{1,0:T(8,128)S(1)}, f32[392,128]{1,0:T(8,128)S(1)}, u32[]{:S(2)}, u32[]{:S(2)}) collective-permute-start(f32[392,128]{1,0:T(8,128)S(1)} %get-tuple-element.17), channel_id=1, source_target_pairs={{0,1},{1,2},{2,3},{3,4},{4,5},{5,6},{6,7},{7,0},{8,9},{9,10},{10,1... | collective-permute-start | bytes 602120 | tf_op jit(solution)/shard_map/ppermute | solution.py:687
  16.3 10.8 %collective-permute-start.3 = (f32[392,128]{1,0:T(8,128)S(1)}, f32[392,128]{1,0:T(8,128)S(1)}, u32[]{:S(2)}, u32[]{:S(2)}) collective-permute-start(f32[392,128]{1,0:T(8,128)S(1)} %get-tuple-element.18), channel_id=1, source_target_pairs={{0,7},{1,0},{2,1},{3,2},{4,3},{5,4},{6,5},{7,6},{8,15},{9,8},{10,9... | collective-permute-start | bytes 602120 | tf_op jit(solution)/shard_map/ppermute | solution.py:687
  19.6 7.5 %collective-permute-start.4 = (f32[24,128]{1,0:T(8,128)S(1)}, f32[24,128]{1,0:T(8,128)S(1)}, u32[]{:S(2)}, u32[]{:S(2)}) collective-permute-start(f32[24,128]{1,0:T(8,128)S(1)} %get-tuple-element.19), channel_id=1, source_target_pairs={{0,2},{1,3},{2,4},{3,5},{4,6},{5,7},{6,0},{7,1},{8,10},{9,11},{10,... | collective-permute-start | bytes 36872 | tf_op jit(solution)/shard_map/ppermute | solution.py:687
  19.6 7.5 %collective-permute-start.5 = (f32[24,128]{1,0:T(8,128)S(1)}, f32[24,128]{1,0:T(8,128)S(1)}, u32[]{:S(2)}, u32[]{:S(2)}) collective-permute-start(f32[24,128]{1,0:T(8,128)S(1)} %get-tuple-element.20), channel_id=1, source_target_pairs={{0,6},{1,7},{2,0},{3,1},{4,2},{5,3},{6,4},{7,5},{8,14},{9,15},{10,... | collective-permute-start | bytes 36872 | tf_op jit(solution)/shard_map/ppermute | solution.py:687
  23.9 3.2 %copy-start = (f32[1,1,3,16384]{3,1,2,0:T(1,128)S(1)}, f32[1,1,3,16384]{3,1,2,0:T(1,128)}, u32[]{:S(2)}) copy-start(f32[1,1,3,16384]{3,1,2,0:T(1,128)} %param.11) | copy-start | bytes 589828
  23.9 3.2 %copy-start.1 = (s32[1,1,2,16384]{3,2,1,0:T(2,128)S(1)}, s32[1,1,2,16384]{3,2,1,0:T(2,128)}, u32[]{:S(2)}) copy-start(s32[1,1,2,16384]{3,2,1,0:T(2,128)} %param.12) | copy-start | bytes 393220
  23.9 3.2 %copy-start.3 = (bf16[768,128]{1,0:T(8,128)(2,1)S(1)}, bf16[768,128]{1,0:T(8,128)(2,1)}, u32[]{:S(2)}) copy-start(bf16[768,128]{1,0:T(8,128)(2,1)} %constant.15.clone.depth_ref) | copy-start | bytes 589828
  23.9 3.2 %copy-start.5 = (f32[2,16,128]{2,1,0:T(8,128)S(1)}, f32[2,16,128]{2,1,0:T(8,128)}, u32[]{:S(2)}) copy-start(f32[2,16,128]{2,1,0:T(8,128)} %constant.20.clone.spectrum_ref) | copy-start | bytes 49156

commit v4 on v3

--- a/solution.py
+++ b/solution.py
@@ -96,7 +96,7 @@
 
 def depth_tables():
     high, low = split_numpy(depth_matrix())
-    down = np.concatenate([high.T, high.T, low.T], axis=0)
+    down = np.concatenate([high.T, high.T, low.T, np.zeros_like(low.T)], axis=0)
     up = np.concatenate([high, high, low], axis=0)
     return jnp.asarray(down), jnp.asarray(up)
 
@@ -166,10 +166,14 @@
 
 ROWS = ATOMS_DEV // LANES
 GROUP = 16
+UNITS = 2
+SHARE = GROUP // UNITS
+GRID_X = X1[1] + X1[1] % 2
 TILES_Y = YP1 // 8
-TILES_Z = NZ // 16
+TILES_Z = NZ // 8
 REAL_X, REAL_Y, REAL_Z, REAL_TY, REAL_TZ = 0, 4, 8, 12, 14
 REALS, PLACES = 16, 8
+PARTS = 4
 
 
 def fill_tables(reals, places, charge, frac_ref, cell_ref, total_y):
@@ -187,9 +191,9 @@
     block_z = (cell_ref[pl.ds(1, ROWS, stride=2), :] - 1) & (NZ - 1)
     for tap in range(4):
         put(places, tap, (block_y + tap) & 7)
-        put(places, 4 + tap, (block_z + tap) & 15)
+        put(places, 4 + tap, (block_z + tap) & 7)
     tile_y = block_y >> 3
-    tile_z = block_z >> 4
+    tile_z = block_z >> 3
     put(reals, REAL_TY, tile_y.astype(jnp.float32))
     put(reals, REAL_TY + 1, (tile_y + 1).astype(jnp.float32))
     put(reals, REAL_TZ, tile_z.astype(jnp.float32))
@@ -213,22 +217,18 @@
 
 def along_z(reals, places, row):
     index = lax.broadcasted_iota(jnp.int32, (8, LANES), 0)
-    parts, tiles = [], []
-    for half in range(2):
-        table = jnp.zeros((8, LANES), jnp.float32)
-        for tap in range(4):
-            place = spread_row(places, 4 + tap, row)
-            table = jnp.where(index + 8 * half == place, spread_row(reals, REAL_Z + tap, row), table)
-        start = spread_row(places, 4, row)
-        tiles.append(
-            jnp.where(index + 8 * half >= start, spread_row(reals, REAL_TZ, row), spread_row(reals, REAL_TZ + 1, row))
-        )
-        parts.append(table)
-    high, low = halves(jnp.concatenate(parts, axis=0))
-    tile = jnp.concatenate(tiles, axis=0).astype(jnp.bfloat16)
+    table = jnp.zeros((8, LANES), jnp.float32)
+    for tap in range(4):
+        table = jnp.where(index == spread_row(places, 4 + tap, row), spread_row(reals, REAL_Z + tap, row), table)
+    start = spread_row(places, 4, row)
+    tile = jnp.where(index >= start, spread_row(reals, REAL_TZ, row), spread_row(reals, REAL_TZ + 1, row))
+    high = jnp.concatenate([table, table], axis=0).astype(jnp.bfloat16)
+    low = table - high.astype(jnp.float32)[0:8]
+    low = jnp.concatenate([low, low], axis=0).astype(jnp.bfloat16)
+    tile = jnp.concatenate([tile, tile - 1.0], axis=0).astype(jnp.bfloat16)
     zero = jnp.zeros((16, LANES), jnp.bfloat16)
     highs, lows = [], []
-    for t in range(TILES_Z):
+    for t in range(0, TILES_Z, 2):
         same = tile == jnp.bfloat16(t)
         highs.append(jnp.where(same, high, zero))
         lows.append(jnp.where(same, low, zero))
@@ -240,13 +240,15 @@
     tile = jnp.concatenate([tile, tile], axis=0).astype(jnp.bfloat16)
     zero = jnp.zeros((16, LANES), jnp.bfloat16)
     same = [tile == jnp.bfloat16(t) for t in range(TILES_Y)]
-    highs, lows = [], []
+    taps = []
     for pair in range(2):
-        both = [table * spread_row(reals, REAL_X + 2 * pair + m, row) for m in range(2)]
-        high, low = halves(jnp.concatenate(both, axis=0))
-        highs += [jnp.where(mask, high, zero) for mask in same]
-        lows += [jnp.where(mask, low, zero) for mask in same]
-    return highs + lows
+        both = jnp.concatenate([table * spread_row(reals, REAL_X + 2 * pair + m, row) for m in range(2)], axis=0)
+        high = both.astype(jnp.bfloat16).astype(jnp.float32)
+        low = both - high
+        for at in (slice(0, 8), slice(8, 16)):
+            value = jnp.concatenate([high[at], low[at]], axis=0).astype(jnp.bfloat16)
+            taps.append(jnp.concatenate([jnp.where(mask, value, zero) for mask in same], axis=0))
+    return taps
 
 
 def triple(value):
@@ -297,37 +299,68 @@
 ):
     fill_tables(reals, places, charge_ref[...], frac_ref, cell_ref, total_y)
     grid[...] = jnp.zeros_like(grid)
-    half_rows = 4 * YP1
-
-    def step(group, carry):
-        sums = [[None] * TILES_Y for _ in range(GROUP + 3)]
-        for p in range(GROUP):
-            lefts, rights = [], []
-            for chunk in range(CHUNKS):
-                row = (group * GROUP + p) * CHUNKS + chunk
-                lefts.append(jnp.concatenate(along_xy(reals, places, row), axis=0))
-                highs, lows = along_z(reals, places, row)
-                rights.append(jnp.concatenate(highs + lows, axis=0))
-            left = jnp.concatenate(lefts, axis=1)
-            right = jnp.concatenate(rights, axis=1)
-            product = lax.dot_general(left, right, (((1,), (1,)), ((), ())), preferred_element_type=jnp.float32)
-            for m in range(4):
-                for t in range(TILES_Y):
-                    at = ((m // 2) * TILES_Y + t) * 16 + (m % 2) * 8
-                    layer = product[at : at + 8, :NZ] + product[at : at + 8, NZ:]
-                    layer = layer + product[half_rows + at : half_rows + at + 8, :NZ]
-                    old = sums[p + m][t]
-                    sums[p + m][t] = layer if old is None else old + layer
+
+    def planes(group, *accs):
+        sums = [None] * (GROUP + 3)
+
+        def pop(unit, i):
+            value = pltpu.matmul_pop(accs[unit * (SHARE + 3) + i])
+            parts = []
+            for t in range(TILES_Y):
+                upper = value[16 * t : 16 * t + 8, :NZ] + value[16 * t : 16 * t + 8, NZ:]
+                parts.append(upper + value[16 * t + 8 : 16 * t + 16, :NZ])
+            layer = jnp.concatenate(parts, axis=0)
+            at = unit * SHARE + i
+            sums[at] = layer if sums[at] is None else sums[at] + layer
+
+        for q in range(SHARE):
+            for unit in range(UNITS):
+                taps, tables = [], []
+                for chunk in range(CHUNKS):
+                    row = (group * GROUP + unit * SHARE + q) * CHUNKS + chunk
+                    taps.append(along_xy(reals, places, row))
+                    highs, lows = along_z(reals, places, row)
+                    tables.append(jnp.concatenate(highs + lows, axis=0))
+                for half in range(CHUNKS // 2):
+                    both = (2 * half, 2 * half + 1)
+                    table = jnp.concatenate([tables[c] for c in both], axis=1)
+                    pltpu.matmul_push_rhs(table, half, unit, transpose=True)
+                    for m in range(4):
+                        left = jnp.concatenate([taps[c][m] for c in both], axis=1)
+                        target = accs[unit * (SHARE + 3) + q + m]
+                        pltpu.matmul_acc_lhs(target, left, half if m == 0 else None)
+                pop(unit, q)
+        for unit in range(UNITS):
+            for i in range(SHARE, SHARE + 3):
+                pop(unit, i)
         for i in range(GROUP + 3):
             at = group * GROUP + i
-            grid[at] = grid[at] + jnp.concatenate(sums[i], axis=0)
+            grid[at] = grid[at] + sums[i]
+
+    def step(group, carry):
+        shape = (2 * YP1, 2 * NZ)
+        units = [unit for unit in range(UNITS) for _ in range(SHARE + 3)]
+        pl.run_scoped(functools.partial(planes, group), *(pltpu.ACC(mxu_id=u)(shape, jnp.float32) for u in units))
         return carry
 
     lax.fori_loop(0, CX // GROUP, step, 0)
-    flat = triple(grid[...].reshape(X1[1] * YP1, NZ))
-    below = jnp.dot(flat, depth_ref[...], preferred_element_type=jnp.float32)
-    raw_ref[...] = below[:, :LANES].reshape(X1[1], YP1, LANES)
-    coarse[...] = below[:, LANES:].reshape(X1[1], YP1, LANES)
+
+    def transform(*accs):
+        span = GRID_X // UNITS
+        for unit, acc in enumerate(accs):
+            rows = grid[unit * span : (unit + 1) * span].reshape(span * YP1, NZ)
+            left = jnp.concatenate(halves(rows), axis=1)
+            for part in range(2):
+                pltpu.matmul_push_rhs(depth_ref[part * 2 * NZ : (part + 1) * 2 * NZ, :], part, unit)
+                pltpu.matmul_acc_lhs(acc, left, part)
+        for unit, acc in enumerate(accs):
+            value = pltpu.matmul_pop(acc).reshape(span, YP1, 2 * LANES)
+            count = min(span, X1[1] - unit * span)
+            raw_ref[unit * span : unit * span + count] = value[:count, :, :LANES]
+            coarse[unit * span : unit * span + count] = value[:count, :, LANES:]
+
+    shape = (GRID_X // UNITS * YP1, 2 * LANES)
+    pl.run_scoped(transform, *(pltpu.ACC(mxu_id=unit)(shape, jnp.float32) for unit in range(UNITS)))
 
     def padded(half, outs, rows):
         half[...] = jnp.zeros_like(half)
@@ -603,15 +636,41 @@
     rise(lambda i: level4[i * YP4 : (i + 1) * YP4, :], X4, X3, Y4, Y3, half3, level3_ref)
 
 
+def part_copies(pairs, sems, part):
+    copies = []
+    for i, (source, target) in enumerate(pairs):
+        rows = source.shape[0] // PARTS
+        at = pl.ds(pl.multiple_of(part * rows, 8), rows)
+        copies.append(pltpu.make_async_copy(source.at[at], target.at[at], sems.at[i, part]))
+    return copies
+
+
+def atoms_kernel(frac_ref, cell_ref, token_ref, real_ref, place_ref, reals, places, sems, *, total_y):
+    fill_tables(reals, places, None, frac_ref, cell_ref, total_y)
+    pairs = ((reals, real_ref), (places, place_ref))
+    for part in range(PARTS):
+        for copy in part_copies(pairs, sems, part):
+            copy.start()
+    for part in range(PARTS):
+        for copy in part_copies(pairs, sems, part):
+            copy.wait()
+
+
 def field_kernel(
     raw_ref, part_ref, below_ref, above_ref, south_ref, north_ref, south2_ref, north2_ref,
-    coarse_ref, spectrum_ref, depth_ref, frac_ref, cell_ref,
+    coarse_ref, spectrum_ref, depth_ref, real_ref, place_ref,
     potential_ref, atom_ref,
-    reals, places, fine, pair, planes, planes_pair, smooth, smooth_pair,
+    reals, places, sems, fine, pair, planes, planes_pair, smooth, smooth_pair,
     level3, half2, level2, half1, level1, field, partial,
-    *, total_y,
 ):
-    fill_tables(reals, places, None, frac_ref, cell_ref, total_y)
+    pairs = ((real_ref, reals), (place_ref, places))
+
+    def fetch(part, carry):
+        for copy in part_copies(pairs, sems, part):
+            copy.start()
+        return carry
+
+    lax.fori_loop(0, PARTS, fetch, 0)
     merge_fine(raw_ref, below_ref, above_ref, south_ref, north_ref, fine)
     merge_coarse(part_ref, below_ref, above_ref, south_ref, north_ref, south2_ref, north2_ref, pair)
     stencil_rows(pair, X2[1], YP2, spectrum_ref[1], smooth_pair, planes_pair)
@@ -631,6 +690,9 @@
     total = jnp.dot(triple(modes), depth_ref[...], preferred_element_type=jnp.float32)
     field[...] = total.reshape(X1[1], YP1, NZ)
     potential_ref[...] = field[0:CX, 0:CY, :]
+    for part in range(PARTS):
+        for copy in part_copies(pairs, sems, part):
+            copy.wait()
 
     def step(group, carry):
         for p in range(GROUP):
@@ -667,6 +729,7 @@
 
 
 VM = pl.BlockSpec(memory_space=pltpu.VMEM)
+HB = pl.BlockSpec(memory_space=pl.ANY)
 
 
 RESIDENT = 2**19
@@ -691,15 +754,15 @@
     return pltpu.VMEM(shape, jnp.int32)
 
 
-def call(kernel, name, outs, scratches, *operands):
+def call(kernel, name, outs, scratches, *operands, far_in=(), far_out=()):
     return pl.pallas_call(
         kernel,
-        in_specs=[VM] * len(operands),
-        out_specs=[VM] * len(outs),
-        out_shape=outs,
+        in_specs=[VM] * len(operands) + [HB] * len(far_in),
+        out_specs=[VM] * len(outs) + [HB] * len(far_out),
+        out_shape=[*outs, *far_out],
         scratch_shapes=scratches,
         name=name,
-    )(*operands)
+    )(*operands, *far_in)
 
 
 def resident(*values):
@@ -732,7 +795,7 @@
         [
             scratch(REALS * ROWS, LANES),
             integers(PLACES * ROWS, LANES),
-            scratch(X1[1], YP1, NZ),
+            scratch(GRID_X, YP1, NZ),
             scratch(X1[1], YP1, LANES),
             scratch(X2[1], YP1 + 16, LANES),
             scratch(X3[1], YP2 + 24, LANES),
@@ -762,13 +825,24 @@
         [scratch(devices, LANES), scratch(X4[1] * YP4, LANES), scratch(X3[1], YP4, LANES)],
         *resident(everyone.reshape(devices * 8, LANES), gather, basis, coarse_spectrum, window),
     )
+    sems = pltpu.SemaphoreType.DMA((2, PARTS))
+    tables = call(
+        functools.partial(atoms_kernel, total_y=total_y),
+        "atoms",
+        [],
+        [scratch(REALS * ROWS, LANES), integers(PLACES * ROWS, LANES), sems],
+        *resident(frac, cell),
+        far_in=[up2],
+        far_out=[pltpu.HBM((REALS * ROWS, LANES), jnp.float32), pltpu.HBM((PLACES * ROWS, LANES), jnp.int32)],
+    )
     potential, atoms = call(
-        functools.partial(field_kernel, total_y=total_y),
+        field_kernel,
         "field",
         [jax.ShapeDtypeStruct((CX, CY, NZ), jnp.float32), jax.ShapeDtypeStruct((ROWS, LANES), jnp.float32)],
         [
             scratch(REALS * ROWS, LANES),
             integers(PLACES * ROWS, LANES),
+            sems,
             scratch(FINE_X, 32, LANES),
             scratch(PAIR_X, 24, LANES),
             scratch(4, FINE_X, YP1, LANES),
@@ -784,7 +858,8 @@
             scratch(8 * ROWS, LANES),
         ],
         *resident(raw, part, below, above, south, north, south2, north2),
-        *resident(coarse, jnp.asarray(spectra().astype(np.float32)), up_table, frac, cell),
+        *resident(coarse, jnp.asarray(spectra().astype(np.float32)), up_table),
+        far_in=tables,
     )
     return (potential, atoms.reshape(1, 1, ATOMS_DEV))
 

time: 32.8 us -> 32.8 us (level)
  starting transfers between devices: 16.8 us -> 15 us
  Pallas kernels: 12.7 us -> 14 us
  waiting for transfers between devices: 2.33 us -> 2.83 us
    ppermute x6, starting transfers between devices: 11.3 us -> 9.54 us  [shifted(): lax.ppermute(value, axis, [(source, (source + steps) % count) for source...]
    pallas_call x4 -> x5, Pallas kernels: 12.7 us -> 14 us  [call(): pl.pallas_call(kernel, in_specs=[VM] * len(operands) + [HB] * len(far_in)...]
    all_to_all x1, waiting for transfers between devices: 0.48 us -> 0.83 us  [local(): everyone = lax.all_to_all(message, ('gx', 'gy'), 0, 0)]
  transfers between devices with their start and end apart: 7 -> 7, of which waited for: 2 -> 3; matrix products, arithmetic and copies ran while one was open for 0% -> 0% of each run, Pallas kernels for 5% -> 9%
where the time goes in v4:
time: 32.8 us; the launch traced here: 32.6 us
  starting transfers between devices  15 us (46%)
  Pallas kernels  14 us (43%)
  waiting for transfers between devices  2.83 us (9%)
  between operations  0.76 us (2%)
    pallas_call x5, Pallas kernels, call(): pl.pallas_call(kernel, in_specs=[VM] * len(operands) + [HB] * len(far_in)...  14 us
    ppermute x6, starting transfers between devices, shifted(): lax.ppermute(value, axis, [(source, (source + steps) % count) for source...  9.54 us
    all_to_all x1, starting transfers between devices, local(): everyone = lax.all_to_all(message, ('gx', 'gy'), 0, 0)  5.43 us
    ppermute x6, waiting for transfers between devices, shifted(): lax.ppermute(value, axis, [(source, (source + steps) % count) for source...  2 us
    all_to_all x1, waiting for transfers between devices, local(): everyone = lax.all_to_all(message, ('gx', 'gy'), 0, 0)  0.83 us
  transfers between devices with their start and end apart: 7, of which 3 were waited for; matrix products, arithmetic and copies ran while one was open for 0% of the time, Pallas kernels for 9%

profile of v4, /device:TPU:0, one launch (start us, length us, event | category | flops | bytes accessed | tf_op | source)
XLA Modules:
  0.0 32.6 jit_solution(9854530308218686222)
XLA Ops:
  0.6 5.7 %deposit.1 = (f32[35,24,128]{2,1,0:T(8,128)S(1)}, f32[20,16,128]{2,1,0:T(8,128)S(1)}, f32[184,128]{1,0:T(8,128)S(1)}, f32[184,128]{1,0:T(8,128)S(1)}, f32[32,8,128]{2,1,0:T(8,128)}) custom-call(f32[128,128]{1,0:T(8,128)} %bitcast.14, f32[3,128,128]{2,1,0:T(8,128)} %bitcast.9, s32[256,128]{1,0:T(8,128)} %bitcast.12, bf16[512,256]{1,0:T(8,128)(2,1)} %constant.14.clone.depth_ref), custom_call_target="tpu_custom_call" | custom-call | tf_op jit(solution)/shard_map/deposit/pallas_call | solution.py:758
  6.3 3.0 %collective-permute-start = (f32[184,128]{1,0:T(8,128)S(1)}, f32[184,128]{1,0:T(8,128)S(1)}, u32[]{:S(2)}, u32[]{:S(2)}) collective-permute-start(f32[184,128]{1,0:T(8,128)S(1)} %get-tuple-element.17), channel_id=1, source_target_pairs={{0,8},{8,16},{16,24},{24,0},{1,9},{9,17},{17,25},{25,1},{2,10},{10... | collective-permute-start | bytes 282632 | tf_op jit(solution)/shard_map/ppermute | solution.py:750
  9.3 1.0 %collective-permute-start.1 = (f32[184,128]{1,0:T(8,128)S(1)}, f32[184,128]{1,0:T(8,128)S(1)}, u32[]{:S(2)}, u32[]{:S(2)}) collective-permute-start(f32[184,128]{1,0:T(8,128)S(1)} %get-tuple-element.18), channel_id=1, source_target_pairs={{0,24},{8,0},{16,8},{24,16},{1,25},{9,1},{17,9},{25,17},{2,26},{10... | collective-permute-start | bytes 282632 | tf_op jit(solution)/shard_map/ppermute | solution.py:750
  10.2 5.4 %all-to-all-start = ((f32[32,8,128]{2,1,0:T(8,128)}), f32[32,8,128]{2,1,0:T(8,128)S(1)}, u32[]{:S(2)}, u32[]{:S(2)}) async-start(f32[32,8,128]{2,1,0:T(8,128)} %get-tuple-element.23), calls=%async_computation | async-start | bytes 262144 | tf_op jit(solution)/shard_map/all_to_all | solution.py:807
  15.6 0.0 collective-permute-done.below_ref
  15.6 0.0 collective-permute-done.1.above_ref
  15.7 0.0 copy-start
  15.7 0.0 copy-start.1
  15.7 0.3 edges.1
  16.0 0.0 copy-start.7
  16.0 0.0 copy-start.2
  16.0 0.3 collective-permute-start.2
  16.3 3.3 %collective-permute-start.3 = (f32[392,128]{1,0:T(8,128)S(1)}, f32[392,128]{1,0:T(8,128)S(1)}, u32[]{:S(2)}, u32[]{:S(2)}) collective-permute-start(f32[392,128]{1,0:T(8,128)S(1)} %get-tuple-element.20), channel_id=1, source_target_pairs={{0,7},{1,0},{2,1},{3,2},{4,3},{5,4},{6,5},{7,6},{8,15},{9,8},{10,9... | collective-permute-start | bytes 602120 | tf_op jit(solution)/shard_map/ppermute | solution.py:750
  19.6 1.8 %collective-permute-start.5 = (f32[24,128]{1,0:T(8,128)S(1)}, f32[24,128]{1,0:T(8,128)S(1)}, u32[]{:S(2)}, u32[]{:S(2)}) collective-permute-start(f32[24,128]{1,0:T(8,128)S(1)} %get-tuple-element.22), channel_id=1, source_target_pairs={{0,6},{1,7},{2,0},{3,1},{4,2},{5,3},{6,4},{7,5},{8,14},{9,15},{10,... | collective-permute-start | bytes 36872 | tf_op jit(solution)/shard_map/ppermute | solution.py:750
  21.4 0.0 copy-start.4
  21.4 0.0 copy-start.6
  21.4 0.0 copy-start.8
  21.4 0.2 collective-permute-start.4
  21.6 0.0 copy-done.7
  21.6 0.0 copy-done
  21.6 0.0 copy-done.1
  21.6 1.4 %atoms.1 = (f32[2048,128]{1,0:T(8,128)}, s32[1024,128]{1,0:T(8,128)}) custom-call(f32[3,128,128]{2,1,0:T(8,128)S(1)} %bitcast.10, s32[256,128]{1,0:T(8,128)S(1)} %bitcast.13, f32[24,128]{1,0:T(8,128)} %copy-done.7), custom_call_target="tpu_custom_call" | custom-call | tf_op jit(solution)/shard_map/atoms/pallas_call | solution.py:758
  23.1 0.8 %all-to-all-done = f32[32,8,128]{2,1,0:T(8,128)S(1)} async-done(((f32[32,8,128]{2,1,0:T(8,128)}), f32[32,8,128]{2,1,0:T(8,128)S(1)}, u32[]{:S(2)}, u32[]{:S(2)}) %all-to-all-start) | async-done | bytes 131104 | tf_op jit(solution)/shard_map/all_to_all | solution.py:807
  23.9 0.0 copy-done.2
  23.9 0.0 copy-done.4
  23.9 0.0 copy-done.6
  23.9 0.0 copy-done.8
  23.9 0.0 copy-start.3
  23.9 0.0 copy-start.5
  23.9 1.3 %coarse.1.coarse_ref = f32[13,16,128]{2,1,0:T(8,128)S(1)} custom-call(f32[256,128]{1,0:T(8,128)S(1)} %bitcast.11, f32[16,40]{1,0:T(8,128)S(1)} %copy-done.8, f32[256,256]{1,0:T(8,128)S(1)} %copy-done.2, f32[16,256]{1,0:T(8,128)S(1)} %copy-done.6, f32[4,16,16]{2,1,0:T(8,128)S(1)} %copy-done.4), custom_call_target="tpu_custom_call" | custom-call | tf_op jit(solution)/shard_map/coarse/pallas_call | solution.py:758
  25.3 0.8 %collective-permute-done.5.north2_ref = f32[24,128]{1,0:T(8,128)S(1)} collective-permute-done((f32[24,128]{1,0:T(8,128)S(1)}, f32[24,128]{1,0:T(8,128)S(1)}, u32[]{:S(2)}, u32[]{:S(2)}) %collective-permute-start.5) | collective-permute-done | bytes 12320 | tf_op jit(solution)/shard_map/ppermute | solution.py:750
  26.1 1.2 %collective-permute-done.4.south2_ref = f32[24,128]{1,0:T(8,128)S(1)} collective-permute-done((f32[24,128]{1,0:T(8,128)S(1)}, f32[24,128]{1,0:T(8,128)S(1)}, u32[]{:S(2)}, u32[]{:S(2)}) %collective-permute-start.4) | collective-permute-done | bytes 12320 | tf_op jit(solution)/shard_map/ppermute | solution.py:750
  27.3 0.0 collective-permute-done.2.south_ref
  27.3 0.0 collective-permute-done.3.north_ref
  27.3 0.0 copy-done.3
  27.3 0.0 copy-done.5
  27.3 5.3 %field.1 = (f32[32,16,128]{2,1,0:T(8,128)}, f32[128,128]{1,0:T(8,128)}) custom-call(f32[35,24,128]{2,1,0:T(8,128)S(1)} %get-tuple-element.15.raw_ref, f32[20,16,128]{2,1,0:T(8,128)S(1)} %get-tuple-element.16.part_ref, f32[184,128]{1,0:T(8,128)S(1)} %collective-permute-done.below_ref, f32[184,128]{1,0:T(8,128)S(1)} %collective-permute-done.1.above_ref, ...), custom_call_target="tpu_custom_call" | custom-call | tf_op jit(solution)/shard_map/field/pallas_call | solution.py:758
Async XLA Ops:
  6.3 9.4 %collective-permute-start = (f32[184,128]{1,0:T(8,128)S(1)}, f32[184,128]{1,0:T(8,128)S(1)}, u32[]{:S(2)}, u32[]{:S(2)}) collective-permute-start(f32[184,128]{1,0:T(8,128)S(1)} %get-tuple-element.17), channel_id=1, source_target_pairs={{0,8},{8,16},{16,24},{24,0},{1,9},{9,17},{17,25},{25,1},{2,10},{10... | collective-permute-start | bytes 282632 | tf_op jit(solution)/shard_map/ppermute | solution.py:750
  9.3 6.4 %collective-permute-start.1 = (f32[184,128]{1,0:T(8,128)S(1)}, f32[184,128]{1,0:T(8,128)S(1)}, u32[]{:S(2)}, u32[]{:S(2)}) collective-permute-start(f32[184,128]{1,0:T(8,128)S(1)} %get-tuple-element.18), channel_id=1, source_target_pairs={{0,24},{8,0},{16,8},{24,16},{1,25},{9,1},{17,9},{25,17},{2,26},{10... | collective-permute-start | bytes 282632 | tf_op jit(solution)/shard_map/ppermute | solution.py:750
  10.2 13.7 %all-to-all-start = ((f32[32,8,128]{2,1,0:T(8,128)}), f32[32,8,128]{2,1,0:T(8,128)S(1)}, u32[]{:S(2)}, u32[]{:S(2)}) async-start(f32[32,8,128]{2,1,0:T(8,128)} %get-tuple-element.23), calls=%async_computation | async-start | bytes 262144 | tf_op jit(solution)/shard_map/all_to_all | solution.py:807
  15.7 6.0 %copy-start = (f32[1,1,3,16384]{3,1,2,0:T(1,128)S(1)}, f32[1,1,3,16384]{3,1,2,0:T(1,128)}, u32[]{:S(2)}) copy-start(f32[1,1,3,16384]{3,1,2,0:T(1,128)} %param.11) | copy-start | bytes 589828
  15.7 6.0 %copy-start.1 = (s32[1,1,2,16384]{3,2,1,0:T(2,128)S(1)}, s32[1,1,2,16384]{3,2,1,0:T(2,128)}, u32[]{:S(2)}) copy-start(s32[1,1,2,16384]{3,2,1,0:T(2,128)} %param.12) | copy-start | bytes 393220
  16.0 5.7 %copy-start.7 = (f32[24,128]{1,0:T(8,128)}, f32[24,128]{1,0:T(8,128)S(1)}, u32[]{:S(2)}) copy-start(f32[24,128]{1,0:T(8,128)S(1)} %get-tuple-element.21.token_ref) | copy-start | bytes 36868
  16.0 7.9 %copy-start.2 = (f32[256,256]{1,0:T(8,128)S(1)}, f32[256,256]{1,0:T(8,128)}, u32[]{:S(2)}) copy-start(f32[256,256]{1,0:T(8,128)} %constant.17.clone.basis_ref) | copy-start | bytes 786436
  16.0 11.3 %collective-permute-start.2 = (f32[392,128]{1,0:T(8,128)S(1)}, f32[392,128]{1,0:T(8,128)S(1)}, u32[]{:S(2)}, u32[]{:S(2)}) collective-permute-start(f32[392,128]{1,0:T(8,128)S(1)} %get-tuple-element.19), channel_id=1, source_target_pairs={{0,1},{1,2},{2,3},{3,4},{4,5},{5,6},{6,7},{7,0},{8,9},{9,10},{10,1... | collective-permute-start | bytes 602120 | tf_op jit(solution)/shard_map/ppermute | solution.py:750
  16.3 11.0 %collective-permute-start.3 = (f32[392,128]{1,0:T(8,128)S(1)}, f32[392,128]{1,0:T(8,128)S(1)}, u32[]{:S(2)}, u32[]{:S(2)}) collective-permute-start(f32[392,128]{1,0:T(8,128)S(1)} %get-tuple-element.20), channel_id=1, source_target_pairs={{0,7},{1,0},{2,1},{3,2},{4,3},{5,4},{6,5},{7,6},{8,15},{9,8},{10,9... | collective-permute-start | bytes 602120 | tf_op jit(solution)/shard_map/ppermute | solution.py:750
  19.6 6.5 %collective-permute-start.5 = (f32[24,128]{1,0:T(8,128)S(1)}, f32[24,128]{1,0:T(8,128)S(1)}, u32[]{:S(2)}, u32[]{:S(2)}) collective-permute-start(f32[24,128]{1,0:T(8,128)S(1)} %get-tuple-element.22), channel_id=1, source_target_pairs={{0,6},{1,7},{2,0},{3,1},{4,2},{5,3},{6,4},{7,5},{8,14},{9,15},{10,... | collective-permute-start | bytes 36872 | tf_op jit(solution)/shard_map/ppermute | solution.py:750
  21.4 2.5 %copy-start.4 = (f32[4,16,16]{2,1,0:T(8,128)S(1)}, f32[4,16,16]{2,1,0:T(8,128)}, u32[]{:S(2)}) copy-start(f32[4,16,16]{2,1,0:T(8,128)} %constant.19.clone.window_ref) | copy-start | bytes 12292
  21.4 2.5 %copy-start.6 = (f32[16,256]{1,0:T(8,128)S(1)}, f32[16,256]{1,0:T(8,128)}, u32[]{:S(2)}) copy-start(f32[16,256]{1,0:T(8,128)} %constant.18.clone.spectrum_ref) | copy-start | bytes 49156
  21.4 2.5 %copy-start.8 = (f32[16,40]{1,0:T(8,128)S(1)}, f32[16,40]{1,0:T(8,128)}, u32[]{:S(2)}) copy-start(f32[16,40]{1,0:T(8,128)} %constant.16.clone.gather_ref) | copy-start | bytes 7684
  21.4 5.8 %collective-permute-start.4 = (f32[24,128]{1,0:T(8,128)S(1)}, f32[24,128]{1,0:T(8,128)S(1)}, u32[]{:S(2)}, u32[]{:S(2)}) collective-permute-start(f32[24,128]{1,0:T(8,128)S(1)} %get-tuple-element.21.token_ref), channel_id=1, source_target_pairs={{0,2},{1,3},{2,4},{3,5},{4,6},{5,7},{6,0},{7,1},{8,10},{9,11},{10,... | collective-permute-start | bytes 36872 | tf_op jit(solution)/shard_map/ppermute | solution.py:750
  23.9 3.4 %copy-start.3 = (bf16[768,128]{1,0:T(8,128)(2,1)S(1)}, bf16[768,128]{1,0:T(8,128)(2,1)}, u32[]{:S(2)}) copy-start(bf16[768,128]{1,0:T(8,128)(2,1)} %constant.15.clone.depth_ref) | copy-start | bytes 589828
  23.9 3.4 %copy-start.5 = (f32[2,16,128]{2,1,0:T(8,128)S(1)}, f32[2,16,128]{2,1,0:T(8,128)}, u32[]{:S(2)}) copy-start(f32[2,16,128]{2,1,0:T(8,128)} %constant.20.clone.spectrum_ref) | copy-start | bytes 49156

commit v5 on v4

--- a/solution.py
+++ b/solution.py
@@ -97,7 +97,7 @@
 def depth_tables():
     high, low = split_numpy(depth_matrix())
     down = np.concatenate([high.T, high.T, low.T, np.zeros_like(low.T)], axis=0)
-    up = np.concatenate([high, high, low], axis=0)
+    up = np.concatenate([high, low], axis=1)
     return jnp.asarray(down), jnp.asarray(up)
 
 
@@ -249,11 +249,6 @@
             value = jnp.concatenate([high[at], low[at]], axis=0).astype(jnp.bfloat16)
             taps.append(jnp.concatenate([jnp.where(mask, value, zero) for mask in same], axis=0))
     return taps
-
-
-def triple(value):
-    high, low = halves(value)
-    return jnp.concatenate([high, low, high], axis=1)
 
 
 def halves(value):
@@ -685,39 +680,73 @@
     rise(lambda i: level2[i], X2, X1, Y2, Y1, half1, level1)
     stencil_rows(fine, X1[1], YP1, spectrum_ref[0], smooth, planes)
 
-    rows = X1[1] * YP1
-    modes = jnp.concatenate([smooth[...].reshape(rows, LANES), level1[...].reshape(rows, LANES)], axis=1)
-    total = jnp.dot(triple(modes), depth_ref[...], preferred_element_type=jnp.float32)
-    field[...] = total.reshape(X1[1], YP1, NZ)
+
+    def transform(*accs):
+        span = GRID_X // UNITS
+        for unit, acc in enumerate(accs):
+            at = slice(unit * span, (unit + 1) * span)
+            parts = [value[at].reshape(span * YP1, LANES) for value in (smooth, level1)]
+            high, low = halves(jnp.concatenate(parts, axis=1))
+            pltpu.matmul_push_rhs(depth_ref[...], 0, unit)
+            pltpu.matmul_acc_lhs(acc, high, 0)
+            pltpu.matmul_acc_lhs(acc, low, None)
+        for unit, acc in enumerate(accs):
+            value = pltpu.matmul_pop(acc)
+            field[unit * span : (unit + 1) * span] = (value[:, :NZ] + value[:, NZ:]).reshape(span, YP1, NZ)
+
+    shape = (GRID_X // UNITS * YP1, 2 * NZ)
+    pl.run_scoped(transform, *(pltpu.ACC(mxu_id=unit)(shape, jnp.float32) for unit in range(UNITS)))
     potential_ref[...] = field[0:CX, 0:CY, :]
     for part in range(PARTS):
         for copy in part_copies(pairs, sems, part):
             copy.wait()
 
-    def step(group, carry):
+    half = CHUNKS // UNITS
+    rows = 4 * YP1
+
+    def sample(plane, unit, acc):
+        product = pltpu.matmul_pop(acc)
+        for c in range(half):
+            row = plane * CHUNKS + unit * half + c
+            lanes = slice(c * LANES, (c + 1) * LANES)
+            weights = [spread_row(reals, REAL_X + m, row) for m in range(4)]
+            table, tile = pattern_y(reals, places, row)
+            value = None
+            for t in range(TILES_Y):
+                layer = None
+                for m in range(4):
+                    at = m * YP1 + 8 * t
+                    term = product[at : at + 8, lanes] * weights[m]
+                    layer = term if layer is None else layer + term
+                value = layer if value is None else jnp.where(tile == t, layer, value)
+            partial[pl.ds(row * 8, 8), :] = value * table
+
+    def planes_of(group, *accs):
+        depth = len(accs) // UNITS
         for p in range(GROUP):
             plane = group * GROUP + p
             high, low = halves(jnp.concatenate([field[plane + m] for m in range(4)], axis=0))
-            left = jnp.concatenate([high, high, low], axis=1)
-            rights = []
-            for chunk in range(CHUNKS):
-                highs, lows = along_z(reals, places, plane * CHUNKS + chunk)
-                rights.append(jnp.concatenate(highs + lows + highs, axis=0))
-            product = jnp.dot(left, jnp.concatenate(rights, axis=1), preferred_element_type=jnp.float32)
-            for chunk in range(CHUNKS):
-                row = plane * CHUNKS + chunk
-                lanes = slice(chunk * LANES, (chunk + 1) * LANES)
-                weights = [spread_row(reals, REAL_X + m, row) for m in range(4)]
-                table, tile = pattern_y(reals, places, row)
-                value = None
-                for t in range(TILES_Y):
-                    layer = None
-                    for m in range(4):
-                        at = m * YP1 + 8 * t
-                        term = product[at : at + 8, lanes] * weights[m]
-                        layer = term if layer is None else layer + term
-                    value = layer if value is None else jnp.where(tile == t, layer, value)
-                partial[pl.ds(row * 8, 8), :] = value * table
+            first = jnp.concatenate([high, high], axis=1)
+            second = jnp.concatenate([low, jnp.zeros_like(low)], axis=1)
+            for unit in range(UNITS):
+                tables = []
+                for c in range(half):
+                    highs, lows = along_z(reals, places, plane * CHUNKS + unit * half + c)
+                    tables.append(jnp.concatenate(highs + lows, axis=0))
+                acc = accs[unit * depth + p % depth]
+                pltpu.matmul_push_rhs(jnp.concatenate(tables, axis=1), p % 2, unit)
+                pltpu.matmul_acc_lhs(acc, first, p % 2)
+                pltpu.matmul_acc_lhs(acc, second, None)
+            if p > 0:
+                for unit in range(UNITS):
+                    sample(plane - 1, unit, accs[unit * depth + (p - 1) % depth])
+        for unit in range(UNITS):
+            sample(group * GROUP + GROUP - 1, unit, accs[unit * depth + (GROUP - 1) % depth])
+
+    def step(group, carry):
+        units = [unit for unit in range(UNITS) for _ in range(4)]
+        accs = (pltpu.ACC(mxu_id=u)((rows, half * LANES), jnp.float32) for u in units)
+        pl.run_scoped(functools.partial(planes_of, group), *accs)
         return carry
 
     lax.fori_loop(0, CX // GROUP, step, 0)
@@ -847,14 +876,14 @@
             scratch(PAIR_X, 24, LANES),
             scratch(4, FINE_X, YP1, LANES),
             scratch(4, PAIR_X, YP2, LANES),
-            scratch(X1[1], YP1, LANES),
+            scratch(GRID_X, YP1, LANES),
             scratch(X2[1], YP2, LANES),
             scratch(X3[1], YP3, LANES),
             scratch(X2[1], YP3, LANES),
             scratch(X2[1], YP2, LANES),
-            scratch(X1[1], YP2, LANES),
-            scratch(X1[1], YP1, LANES),
-            scratch(X1[1], YP1, NZ),
+            scratch(GRID_X, YP2, LANES),
+            scratch(GRID_X, YP1, LANES),
+            scratch(GRID_X, YP1, NZ),
             scratch(8 * ROWS, LANES),
         ],
         *resident(raw, part, below, above, south, north, south2, north2),

time: 32.8 us -> 32.2 us (0.982)
  Pallas kernels: 14 us -> 13.4 us
    pallas_call x5, Pallas kernels: 14 us -> 13.4 us  [call(): pl.pallas_call(kernel, in_specs=[VM] * len(operands) + [HB] * len(far_in)...]
where the time goes in v5:
time: 32.2 us; the launch traced here: 32 us
  starting transfers between devices  15 us (47%)
  Pallas kernels  13.4 us (42%)
  waiting for transfers between devices  2.83 us (9%)
  between operations  0.76 us (2%)
    pallas_call x5, Pallas kernels, call(): pl.pallas_call(kernel, in_specs=[VM] * len(operands) + [HB] * len(far_in)...  13.4 us
    ppermute x6, starting transfers between devices, shifted(): lax.ppermute(value, axis, [(source, (source + steps) % count) for source...  9.54 us
    all_to_all x1, starting transfers between devices, local(): everyone = lax.all_to_all(message, ('gx', 'gy'), 0, 0)  5.43 us
    ppermute x6, waiting for transfers between devices, shifted(): lax.ppermute(value, axis, [(source, (source + steps) % count) for source...  2 us
    all_to_all x1, waiting for transfers between devices, local(): everyone = lax.all_to_all(message, ('gx', 'gy'), 0, 0)  0.83 us
  transfers between devices with their start and end apart: 7, of which 3 were waited for; matrix products, arithmetic and copies ran while one was open for 0% of the time, Pallas kernels for 9%

profile of v5, /device:TPU:0, one launch (start us, length us, event | category | flops | bytes accessed | tf_op | source)
XLA Modules:
  0.0 32.0 jit_solution(14308703451812409449)
XLA Ops:
  0.6 5.7 %deposit.1 = (f32[35,24,128]{2,1,0:T(8,128)S(1)}, f32[20,16,128]{2,1,0:T(8,128)S(1)}, f32[184,128]{1,0:T(8,128)S(1)}, f32[184,128]{1,0:T(8,128)S(1)}, f32[32,8,128]{2,1,0:T(8,128)}) custom-call(f32[128,128]{1,0:T(8,128)} %bitcast.14, f32[3,128,128]{2,1,0:T(8,128)} %bitcast.9, s32[256,128]{1,0:T(8,128)} %bitcast.12, bf16[512,256]{1,0:T(8,128)(2,1)} %constant.14.clone.depth_ref), custom_call_target="tpu_custom_call" | custom-call | tf_op jit(solution)/shard_map/deposit/pallas_call | solution.py:787
  6.3 3.0 %collective-permute-start = (f32[184,128]{1,0:T(8,128)S(1)}, f32[184,128]{1,0:T(8,128)S(1)}, u32[]{:S(2)}, u32[]{:S(2)}) collective-permute-start(f32[184,128]{1,0:T(8,128)S(1)} %get-tuple-element.17), channel_id=1, source_target_pairs={{0,8},{8,16},{16,24},{24,0},{1,9},{9,17},{17,25},{25,1},{2,10},{10... | collective-permute-start | bytes 282632 | tf_op jit(solution)/shard_map/ppermute | solution.py:779
  9.3 1.0 %collective-permute-start.1 = (f32[184,128]{1,0:T(8,128)S(1)}, f32[184,128]{1,0:T(8,128)S(1)}, u32[]{:S(2)}, u32[]{:S(2)}) collective-permute-start(f32[184,128]{1,0:T(8,128)S(1)} %get-tuple-element.18), channel_id=1, source_target_pairs={{0,24},{8,0},{16,8},{24,16},{1,25},{9,1},{17,9},{25,17},{2,26},{10... | collective-permute-start | bytes 282632 | tf_op jit(solution)/shard_map/ppermute | solution.py:779
  10.2 5.4 %all-to-all-start = ((f32[32,8,128]{2,1,0:T(8,128)}), f32[32,8,128]{2,1,0:T(8,128)S(1)}, u32[]{:S(2)}, u32[]{:S(2)}) async-start(f32[32,8,128]{2,1,0:T(8,128)} %get-tuple-element.23), calls=%async_computation | async-start | bytes 262144 | tf_op jit(solution)/shard_map/all_to_all | solution.py:836
  15.6 0.0 collective-permute-done.below_ref
  15.6 0.0 collective-permute-done.1.above_ref
  15.7 0.0 copy-start
  15.7 0.0 copy-start.1
  15.7 0.3 edges.1
  16.0 0.0 copy-start.7
  16.0 0.0 copy-start.2
  16.0 0.3 collective-permute-start.2
  16.3 3.3 %collective-permute-start.3 = (f32[392,128]{1,0:T(8,128)S(1)}, f32[392,128]{1,0:T(8,128)S(1)}, u32[]{:S(2)}, u32[]{:S(2)}) collective-permute-start(f32[392,128]{1,0:T(8,128)S(1)} %get-tuple-element.20), channel_id=1, source_target_pairs={{0,7},{1,0},{2,1},{3,2},{4,3},{5,4},{6,5},{7,6},{8,15},{9,8},{10,9... | collective-permute-start | bytes 602120 | tf_op jit(solution)/shard_map/ppermute | solution.py:779
  19.6 1.8 %collective-permute-start.5 = (f32[24,128]{1,0:T(8,128)S(1)}, f32[24,128]{1,0:T(8,128)S(1)}, u32[]{:S(2)}, u32[]{:S(2)}) collective-permute-start(f32[24,128]{1,0:T(8,128)S(1)} %get-tuple-element.22), channel_id=1, source_target_pairs={{0,6},{1,7},{2,0},{3,1},{4,2},{5,3},{6,4},{7,5},{8,14},{9,15},{10,... | collective-permute-start | bytes 36872 | tf_op jit(solution)/shard_map/ppermute | solution.py:779
  21.4 0.0 copy-start.4
  21.4 0.0 copy-start.6
  21.4 0.0 copy-start.8
  21.4 0.2 collective-permute-start.4
  21.6 0.0 copy-done.7
  21.6 0.0 copy-done
  21.6 0.0 copy-done.1
  21.6 1.4 %atoms.1 = (f32[2048,128]{1,0:T(8,128)}, s32[1024,128]{1,0:T(8,128)}) custom-call(f32[3,128,128]{2,1,0:T(8,128)S(1)} %bitcast.10, s32[256,128]{1,0:T(8,128)S(1)} %bitcast.13, f32[24,128]{1,0:T(8,128)} %copy-done.7), custom_call_target="tpu_custom_call" | custom-call | tf_op jit(solution)/shard_map/atoms/pallas_call | solution.py:787
  23.1 0.8 %all-to-all-done = f32[32,8,128]{2,1,0:T(8,128)S(1)} async-done(((f32[32,8,128]{2,1,0:T(8,128)}), f32[32,8,128]{2,1,0:T(8,128)S(1)}, u32[]{:S(2)}, u32[]{:S(2)}) %all-to-all-start) | async-done | bytes 131104 | tf_op jit(solution)/shard_map/all_to_all | solution.py:836
  23.9 0.0 copy-done.2
  23.9 0.0 copy-done.4
  23.9 0.0 copy-done.6
  23.9 0.0 copy-done.8
  23.9 0.0 copy-start.3
  23.9 0.0 copy-start.5
  23.9 1.3 %coarse.1.coarse_ref = f32[13,16,128]{2,1,0:T(8,128)S(1)} custom-call(f32[256,128]{1,0:T(8,128)S(1)} %bitcast.11, f32[16,40]{1,0:T(8,128)S(1)} %copy-done.8, f32[256,256]{1,0:T(8,128)S(1)} %copy-done.2, f32[16,256]{1,0:T(8,128)S(1)} %copy-done.6, f32[4,16,16]{2,1,0:T(8,128)S(1)} %copy-done.4), custom_call_target="tpu_custom_call" | custom-call | tf_op jit(solution)/shard_map/coarse/pallas_call | solution.py:787
  25.3 0.8 %collective-permute-done.5.north2_ref = f32[24,128]{1,0:T(8,128)S(1)} collective-permute-done((f32[24,128]{1,0:T(8,128)S(1)}, f32[24,128]{1,0:T(8,128)S(1)}, u32[]{:S(2)}, u32[]{:S(2)}) %collective-permute-start.5) | collective-permute-done | bytes 12320 | tf_op jit(solution)/shard_map/ppermute | solution.py:779
  26.1 1.2 %collective-permute-done.4.south2_ref = f32[24,128]{1,0:T(8,128)S(1)} collective-permute-done((f32[24,128]{1,0:T(8,128)S(1)}, f32[24,128]{1,0:T(8,128)S(1)}, u32[]{:S(2)}, u32[]{:S(2)}) %collective-permute-start.4) | collective-permute-done | bytes 12320 | tf_op jit(solution)/shard_map/ppermute | solution.py:779
  27.3 0.0 collective-permute-done.2.south_ref
  27.3 0.0 collective-permute-done.3.north_ref
  27.3 0.0 copy-done.3
  27.3 0.0 copy-done.5
  27.3 4.7 %field.1 = (f32[32,16,128]{2,1,0:T(8,128)}, f32[128,128]{1,0:T(8,128)}) custom-call(f32[35,24,128]{2,1,0:T(8,128)S(1)} %get-tuple-element.15.raw_ref, f32[20,16,128]{2,1,0:T(8,128)S(1)} %get-tuple-element.16.part_ref, f32[184,128]{1,0:T(8,128)S(1)} %collective-permute-done.below_ref, f32[184,128]{1,0:T(8,128)S(1)} %collective-permute-done.1.above_ref, ...), custom_call_target="tpu_custom_call" | custom-call | tf_op jit(solution)/shard_map/field/pallas_call | solution.py:787
Async XLA Ops:
  6.3 9.4 %collective-permute-start = (f32[184,128]{1,0:T(8,128)S(1)}, f32[184,128]{1,0:T(8,128)S(1)}, u32[]{:S(2)}, u32[]{:S(2)}) collective-permute-start(f32[184,128]{1,0:T(8,128)S(1)} %get-tuple-element.17), channel_id=1, source_target_pairs={{0,8},{8,16},{16,24},{24,0},{1,9},{9,17},{17,25},{25,1},{2,10},{10... | collective-permute-start | bytes 282632 | tf_op jit(solution)/shard_map/ppermute | solution.py:779
  9.3 6.4 %collective-permute-start.1 = (f32[184,128]{1,0:T(8,128)S(1)}, f32[184,128]{1,0:T(8,128)S(1)}, u32[]{:S(2)}, u32[]{:S(2)}) collective-permute-start(f32[184,128]{1,0:T(8,128)S(1)} %get-tuple-element.18), channel_id=1, source_target_pairs={{0,24},{8,0},{16,8},{24,16},{1,25},{9,1},{17,9},{25,17},{2,26},{10... | collective-permute-start | bytes 282632 | tf_op jit(solution)/shard_map/ppermute | solution.py:779
  10.2 13.7 %all-to-all-start = ((f32[32,8,128]{2,1,0:T(8,128)}), f32[32,8,128]{2,1,0:T(8,128)S(1)}, u32[]{:S(2)}, u32[]{:S(2)}) async-start(f32[32,8,128]{2,1,0:T(8,128)} %get-tuple-element.23), calls=%async_computation | async-start | bytes 262144 | tf_op jit(solution)/shard_map/all_to_all | solution.py:836
  15.7 6.0 %copy-start = (f32[1,1,3,16384]{3,1,2,0:T(1,128)S(1)}, f32[1,1,3,16384]{3,1,2,0:T(1,128)}, u32[]{:S(2)}) copy-start(f32[1,1,3,16384]{3,1,2,0:T(1,128)} %param.11) | copy-start | bytes 589828
  15.7 6.0 %copy-start.1 = (s32[1,1,2,16384]{3,2,1,0:T(2,128)S(1)}, s32[1,1,2,16384]{3,2,1,0:T(2,128)}, u32[]{:S(2)}) copy-start(s32[1,1,2,16384]{3,2,1,0:T(2,128)} %param.12) | copy-start | bytes 393220
  16.0 5.7 %copy-start.7 = (f32[24,128]{1,0:T(8,128)}, f32[24,128]{1,0:T(8,128)S(1)}, u32[]{:S(2)}) copy-start(f32[24,128]{1,0:T(8,128)S(1)} %get-tuple-element.21.token_ref) | copy-start | bytes 36868
  16.0 7.9 %copy-start.2 = (f32[256,256]{1,0:T(8,128)S(1)}, f32[256,256]{1,0:T(8,128)}, u32[]{:S(2)}) copy-start(f32[256,256]{1,0:T(8,128)} %constant.17.clone.basis_ref) | copy-start | bytes 786436
  16.0 11.3 %collective-permute-start.2 = (f32[392,128]{1,0:T(8,128)S(1)}, f32[392,128]{1,0:T(8,128)S(1)}, u32[]{:S(2)}, u32[]{:S(2)}) collective-permute-start(f32[392,128]{1,0:T(8,128)S(1)} %get-tuple-element.19), channel_id=1, source_target_pairs={{0,1},{1,2},{2,3},{3,4},{4,5},{5,6},{6,7},{7,0},{8,9},{9,10},{10,1... | collective-permute-start | bytes 602120 | tf_op jit(solution)/shard_map/ppermute | solution.py:779
  16.3 11.0 %collective-permute-start.3 = (f32[392,128]{1,0:T(8,128)S(1)}, f32[392,128]{1,0:T(8,128)S(1)}, u32[]{:S(2)}, u32[]{:S(2)}) collective-permute-start(f32[392,128]{1,0:T(8,128)S(1)} %get-tuple-element.20), channel_id=1, source_target_pairs={{0,7},{1,0},{2,1},{3,2},{4,3},{5,4},{6,5},{7,6},{8,15},{9,8},{10,9... | collective-permute-start | bytes 602120 | tf_op jit(solution)/shard_map/ppermute | solution.py:779
  19.6 6.5 %collective-permute-start.5 = (f32[24,128]{1,0:T(8,128)S(1)}, f32[24,128]{1,0:T(8,128)S(1)}, u32[]{:S(2)}, u32[]{:S(2)}) collective-permute-start(f32[24,128]{1,0:T(8,128)S(1)} %get-tuple-element.22), channel_id=1, source_target_pairs={{0,6},{1,7},{2,0},{3,1},{4,2},{5,3},{6,4},{7,5},{8,14},{9,15},{10,... | collective-permute-start | bytes 36872 | tf_op jit(solution)/shard_map/ppermute | solution.py:779
  21.4 2.5 %copy-start.4 = (f32[4,16,16]{2,1,0:T(8,128)S(1)}, f32[4,16,16]{2,1,0:T(8,128)}, u32[]{:S(2)}) copy-start(f32[4,16,16]{2,1,0:T(8,128)} %constant.19.clone.window_ref) | copy-start | bytes 12292
  21.4 2.5 %copy-start.6 = (f32[16,256]{1,0:T(8,128)S(1)}, f32[16,256]{1,0:T(8,128)}, u32[]{:S(2)}) copy-start(f32[16,256]{1,0:T(8,128)} %constant.18.clone.spectrum_ref) | copy-start | bytes 49156
  21.4 2.5 %copy-start.8 = (f32[16,40]{1,0:T(8,128)S(1)}, f32[16,40]{1,0:T(8,128)}, u32[]{:S(2)}) copy-start(f32[16,40]{1,0:T(8,128)} %constant.16.clone.gather_ref) | copy-start | bytes 7684
  21.4 5.8 %collective-permute-start.4 = (f32[24,128]{1,0:T(8,128)S(1)}, f32[24,128]{1,0:T(8,128)S(1)}, u32[]{:S(2)}, u32[]{:S(2)}) collective-permute-start(f32[24,128]{1,0:T(8,128)S(1)} %get-tuple-element.21.token_ref), channel_id=1, source_target_pairs={{0,2},{1,3},{2,4},{3,5},{4,6},{5,7},{6,0},{7,1},{8,10},{9,11},{10,... | collective-permute-start | bytes 36872 | tf_op jit(solution)/shard_map/ppermute | solution.py:779
  23.9 3.4 %copy-start.3 = (bf16[256,256]{1,0:T(8,128)(2,1)S(1)}, bf16[256,256]{1,0:T(8,128)(2,1)}, u32[]{:S(2)}) copy-start(bf16[256,256]{1,0:T(8,128)(2,1)} %constant.15.clone.depth_ref) | copy-start | bytes 393220
  23.9 3.4 %copy-start.5 = (f32[2,16,128]{2,1,0:T(8,128)S(1)}, f32[2,16,128]{2,1,0:T(8,128)}, u32[]{:S(2)}) copy-start(f32[2,16,128]{2,1,0:T(8,128)} %constant.20.clone.spectrum_ref) | copy-start | bytes 49156

commit v6 on v5

--- a/solution.py
+++ b/solution.py
@@ -289,9 +289,11 @@
 def deposit_kernel(
     charge_ref, frac_ref, cell_ref, depth_ref,
     raw_ref, part_ref, low_ref, high_ref, message_ref,
-    reals, places, grid, coarse, half2, half3, half4, last,
+    table, table_sem, reals, places, grid, coarse, half2, half3, half4, last,
     *, total_y, devices,
 ):
+    fetch = pltpu.make_async_copy(depth_ref, table, table_sem)
+    fetch.start()
     fill_tables(reals, places, charge_ref[...], frac_ref, cell_ref, total_y)
     grid[...] = jnp.zeros_like(grid)
 
@@ -339,6 +341,7 @@
         return carry
 
     lax.fori_loop(0, CX // GROUP, step, 0)
+    fetch.wait()
 
     def transform(*accs):
         span = GRID_X // UNITS
@@ -346,7 +349,7 @@
             rows = grid[unit * span : (unit + 1) * span].reshape(span * YP1, NZ)
             left = jnp.concatenate(halves(rows), axis=1)
             for part in range(2):
-                pltpu.matmul_push_rhs(depth_ref[part * 2 * NZ : (part + 1) * 2 * NZ, :], part, unit)
+                pltpu.matmul_push_rhs(table[part * 2 * NZ : (part + 1) * 2 * NZ, :], part, unit)
                 pltpu.matmul_acc_lhs(acc, left, part)
         for unit, acc in enumerate(accs):
             value = pltpu.matmul_pop(acc).reshape(span, YP1, 2 * LANES)
@@ -822,6 +825,8 @@
             f32(devices, 8, LANES),
         ],
         [
+            pltpu.VMEM(down_table.shape, down_table.dtype),
+            pltpu.SemaphoreType.DMA(()),
             scratch(REALS * ROWS, LANES),
             integers(PLACES * ROWS, LANES),
             scratch(GRID_X, YP1, NZ),
@@ -831,7 +836,8 @@
             scratch(X4[1], YP3 + 16, LANES),
             scratch(X4[1] * YP4, LANES),
         ],
-        charge, frac, cell, down_table,
+        charge, frac, cell,
+        far_in=[down_table],
     )
     everyone = lax.all_to_all(message, ("gx", "gy"), 0, 0)
     below = shifted(high, "gx", 1)

time: 32.2 us -> 32.2 us (level)
  no operation moved by 1% of the time
where the time goes in v6:
time: 32.2 us; the launch traced here: 32 us
  starting transfers between devices  15 us (47%)
  Pallas kernels  13.3 us (41%)
  waiting for transfers between devices  2.83 us (9%)
  between operations  0.76 us (2%)
    pallas_call x5, Pallas kernels, call(): pl.pallas_call(kernel, in_specs=[VM] * len(operands) + [HB] * len(far_in)...  13.3 us
    ppermute x6, starting transfers between devices, shifted(): lax.ppermute(value, axis, [(source, (source + steps) % count) for source...  9.67 us
    all_to_all x1, starting transfers between devices, local(): everyone = lax.all_to_all(message, ('gx', 'gy'), 0, 0)  5.36 us
    ppermute x6, waiting for transfers between devices, shifted(): lax.ppermute(value, axis, [(source, (source + steps) % count) for source...  2 us
    all_to_all x1, waiting for transfers between devices, local(): everyone = lax.all_to_all(message, ('gx', 'gy'), 0, 0)  0.83 us
  transfers between devices with their start and end apart: 7, of which 3 were waited for; matrix products, arithmetic and copies ran while one was open for 0% of the time, Pallas kernels for 9%

profile of v6, /device:TPU:0, one launch (start us, length us, event | category | flops | bytes accessed | tf_op | source)
XLA Modules:
  0.0 32.0 jit_solution(17598863155543829934)
XLA Ops:
  0.6 5.6 %deposit.1 = (f32[35,24,128]{2,1,0:T(8,128)S(1)}, f32[20,16,128]{2,1,0:T(8,128)S(1)}, f32[184,128]{1,0:T(8,128)S(1)}, f32[184,128]{1,0:T(8,128)S(1)}, f32[32,8,128]{2,1,0:T(8,128)}) custom-call(f32[128,128]{1,0:T(8,128)} %bitcast.14, f32[3,128,128]{2,1,0:T(8,128)} %bitcast.9, s32[256,128]{1,0:T(8,128)} %bitcast.12, bf16[512,256]{1,0:T(8,128)(2,1)} %constant.14.clone.depth_ref), custom_call_target="tpu_custom_call" | custom-call | tf_op jit(solution)/shard_map/deposit/pallas_call | solution.py:790
  6.2 3.0 %collective-permute-start = (f32[184,128]{1,0:T(8,128)S(1)}, f32[184,128]{1,0:T(8,128)S(1)}, u32[]{:S(2)}, u32[]{:S(2)}) collective-permute-start(f32[184,128]{1,0:T(8,128)S(1)} %get-tuple-element.17), channel_id=1, source_target_pairs={{0,8},{8,16},{16,24},{24,0},{1,9},{9,17},{17,25},{25,1},{2,10},{10... | collective-permute-start | bytes 282632 | tf_op jit(solution)/shard_map/ppermute | solution.py:782
  9.2 1.0 %collective-permute-start.1 = (f32[184,128]{1,0:T(8,128)S(1)}, f32[184,128]{1,0:T(8,128)S(1)}, u32[]{:S(2)}, u32[]{:S(2)}) collective-permute-start(f32[184,128]{1,0:T(8,128)S(1)} %get-tuple-element.18), channel_id=1, source_target_pairs={{0,24},{8,0},{16,8},{24,16},{1,25},{9,1},{17,9},{25,17},{2,26},{10... | collective-permute-start | bytes 282632 | tf_op jit(solution)/shard_map/ppermute | solution.py:782
  10.2 5.4 %all-to-all-start = ((f32[32,8,128]{2,1,0:T(8,128)}), f32[32,8,128]{2,1,0:T(8,128)S(1)}, u32[]{:S(2)}, u32[]{:S(2)}) async-start(f32[32,8,128]{2,1,0:T(8,128)} %get-tuple-element.23), calls=%async_computation | async-start | bytes 262144 | tf_op jit(solution)/shard_map/all_to_all | solution.py:842
  15.6 0.0 collective-permute-done.below_ref
  15.6 0.0 collective-permute-done.1.above_ref
  15.6 0.0 copy-start
  15.6 0.0 copy-start.1
  15.7 0.3 edges.1
  15.9 0.0 copy-start.7
  15.9 0.0 copy-start.2
  16.0 0.3 collective-permute-start.2
  16.3 3.3 %collective-permute-start.3 = (f32[392,128]{1,0:T(8,128)S(1)}, f32[392,128]{1,0:T(8,128)S(1)}, u32[]{:S(2)}, u32[]{:S(2)}) collective-permute-start(f32[392,128]{1,0:T(8,128)S(1)} %get-tuple-element.20), channel_id=1, source_target_pairs={{0,7},{1,0},{2,1},{3,2},{4,3},{5,4},{6,5},{7,6},{8,15},{9,8},{10,9... | collective-permute-start | bytes 602120 | tf_op jit(solution)/shard_map/ppermute | solution.py:782
  19.6 1.8 %collective-permute-start.5 = (f32[24,128]{1,0:T(8,128)S(1)}, f32[24,128]{1,0:T(8,128)S(1)}, u32[]{:S(2)}, u32[]{:S(2)}) collective-permute-start(f32[24,128]{1,0:T(8,128)S(1)} %get-tuple-element.22), channel_id=1, source_target_pairs={{0,6},{1,7},{2,0},{3,1},{4,2},{5,3},{6,4},{7,5},{8,14},{9,15},{10,... | collective-permute-start | bytes 36872 | tf_op jit(solution)/shard_map/ppermute | solution.py:782
  21.4 0.0 copy-start.4
  21.4 0.0 copy-start.6
  21.4 0.0 copy-start.8
  21.4 0.2 collective-permute-start.4
  21.6 0.0 copy-done.7
  21.6 0.0 copy-done
  21.6 0.0 copy-done.1
  21.6 1.4 %atoms.1 = (f32[2048,128]{1,0:T(8,128)}, s32[1024,128]{1,0:T(8,128)}) custom-call(f32[3,128,128]{2,1,0:T(8,128)S(1)} %bitcast.10, s32[256,128]{1,0:T(8,128)S(1)} %bitcast.13, f32[24,128]{1,0:T(8,128)} %copy-done.7), custom_call_target="tpu_custom_call" | custom-call | tf_op jit(solution)/shard_map/atoms/pallas_call | solution.py:790
  23.0 0.8 %all-to-all-done = f32[32,8,128]{2,1,0:T(8,128)S(1)} async-done(((f32[32,8,128]{2,1,0:T(8,128)}), f32[32,8,128]{2,1,0:T(8,128)S(1)}, u32[]{:S(2)}, u32[]{:S(2)}) %all-to-all-start) | async-done | bytes 131104 | tf_op jit(solution)/shard_map/all_to_all | solution.py:842
  23.9 0.0 copy-done.2
  23.9 0.0 copy-done.4
  23.9 0.0 copy-done.6
  23.9 0.0 copy-done.8
  23.9 0.0 copy-start.3
  23.9 0.0 copy-start.5
  23.9 1.3 %coarse.1.coarse_ref = f32[13,16,128]{2,1,0:T(8,128)S(1)} custom-call(f32[256,128]{1,0:T(8,128)S(1)} %bitcast.11, f32[16,40]{1,0:T(8,128)S(1)} %copy-done.8, f32[256,256]{1,0:T(8,128)S(1)} %copy-done.2, f32[16,256]{1,0:T(8,128)S(1)} %copy-done.6, f32[4,16,16]{2,1,0:T(8,128)S(1)} %copy-done.4), custom_call_target="tpu_custom_call" | custom-call | tf_op jit(solution)/shard_map/coarse/pallas_call | solution.py:790
  25.2 0.8 %collective-permute-done.5.north2_ref = f32[24,128]{1,0:T(8,128)S(1)} collective-permute-done((f32[24,128]{1,0:T(8,128)S(1)}, f32[24,128]{1,0:T(8,128)S(1)}, u32[]{:S(2)}, u32[]{:S(2)}) %collective-permute-start.5) | collective-permute-done | bytes 12320 | tf_op jit(solution)/shard_map/ppermute | solution.py:782
  26.1 1.2 %collective-permute-done.4.south2_ref = f32[24,128]{1,0:T(8,128)S(1)} collective-permute-done((f32[24,128]{1,0:T(8,128)S(1)}, f32[24,128]{1,0:T(8,128)S(1)}, u32[]{:S(2)}, u32[]{:S(2)}) %collective-permute-start.4) | collective-permute-done | bytes 12320 | tf_op jit(solution)/shard_map/ppermute | solution.py:782
  27.2 0.0 collective-permute-done.2.south_ref
  27.2 0.0 collective-permute-done.3.north_ref
  27.2 0.0 copy-done.3
  27.2 0.0 copy-done.5
  27.3 4.7 %field.1 = (f32[32,16,128]{2,1,0:T(8,128)}, f32[128,128]{1,0:T(8,128)}) custom-call(f32[35,24,128]{2,1,0:T(8,128)S(1)} %get-tuple-element.15.raw_ref, f32[20,16,128]{2,1,0:T(8,128)S(1)} %get-tuple-element.16.part_ref, f32[184,128]{1,0:T(8,128)S(1)} %collective-permute-done.below_ref, f32[184,128]{1,0:T(8,128)S(1)} %collective-permute-done.1.above_ref, ...), custom_call_target="tpu_custom_call" | custom-call | tf_op jit(solution)/shard_map/field/pallas_call | solution.py:790
Async XLA Ops:
  6.2 9.4 %collective-permute-start = (f32[184,128]{1,0:T(8,128)S(1)}, f32[184,128]{1,0:T(8,128)S(1)}, u32[]{:S(2)}, u32[]{:S(2)}) collective-permute-start(f32[184,128]{1,0:T(8,128)S(1)} %get-tuple-element.17), channel_id=1, source_target_pairs={{0,8},{8,16},{16,24},{24,0},{1,9},{9,17},{17,25},{25,1},{2,10},{10... | collective-permute-start | bytes 282632 | tf_op jit(solution)/shard_map/ppermute | solution.py:782
  9.2 6.4 %collective-permute-start.1 = (f32[184,128]{1,0:T(8,128)S(1)}, f32[184,128]{1,0:T(8,128)S(1)}, u32[]{:S(2)}, u32[]{:S(2)}) collective-permute-start(f32[184,128]{1,0:T(8,128)S(1)} %get-tuple-element.18), channel_id=1, source_target_pairs={{0,24},{8,0},{16,8},{24,16},{1,25},{9,1},{17,9},{25,17},{2,26},{10... | collective-permute-start | bytes 282632 | tf_op jit(solution)/shard_map/ppermute | solution.py:782
  10.2 13.6 %all-to-all-start = ((f32[32,8,128]{2,1,0:T(8,128)}), f32[32,8,128]{2,1,0:T(8,128)S(1)}, u32[]{:S(2)}, u32[]{:S(2)}) async-start(f32[32,8,128]{2,1,0:T(8,128)} %get-tuple-element.23), calls=%async_computation | async-start | bytes 262144 | tf_op jit(solution)/shard_map/all_to_all | solution.py:842
  15.6 6.0 %copy-start = (f32[1,1,3,16384]{3,1,2,0:T(1,128)S(1)}, f32[1,1,3,16384]{3,1,2,0:T(1,128)}, u32[]{:S(2)}) copy-start(f32[1,1,3,16384]{3,1,2,0:T(1,128)} %param.11) | copy-start | bytes 589828
  15.6 6.0 %copy-start.1 = (s32[1,1,2,16384]{3,2,1,0:T(2,128)S(1)}, s32[1,1,2,16384]{3,2,1,0:T(2,128)}, u32[]{:S(2)}) copy-start(s32[1,1,2,16384]{3,2,1,0:T(2,128)} %param.12) | copy-start | bytes 393220
  15.9 5.7 %copy-start.7 = (f32[24,128]{1,0:T(8,128)}, f32[24,128]{1,0:T(8,128)S(1)}, u32[]{:S(2)}) copy-start(f32[24,128]{1,0:T(8,128)S(1)} %get-tuple-element.21.token_ref) | copy-start | bytes 36868
  15.9 7.9 %copy-start.2 = (f32[256,256]{1,0:T(8,128)S(1)}, f32[256,256]{1,0:T(8,128)}, u32[]{:S(2)}) copy-start(f32[256,256]{1,0:T(8,128)} %constant.17.clone.basis_ref) | copy-start | bytes 786436
  16.0 11.3 %collective-permute-start.2 = (f32[392,128]{1,0:T(8,128)S(1)}, f32[392,128]{1,0:T(8,128)S(1)}, u32[]{:S(2)}, u32[]{:S(2)}) collective-permute-start(f32[392,128]{1,0:T(8,128)S(1)} %get-tuple-element.19), channel_id=1, source_target_pairs={{0,1},{1,2},{2,3},{3,4},{4,5},{5,6},{6,7},{7,0},{8,9},{9,10},{10,1... | collective-permute-start | bytes 602120 | tf_op jit(solution)/shard_map/ppermute | solution.py:782
  16.3 11.0 %collective-permute-start.3 = (f32[392,128]{1,0:T(8,128)S(1)}, f32[392,128]{1,0:T(8,128)S(1)}, u32[]{:S(2)}, u32[]{:S(2)}) collective-permute-start(f32[392,128]{1,0:T(8,128)S(1)} %get-tuple-element.20), channel_id=1, source_target_pairs={{0,7},{1,0},{2,1},{3,2},{4,3},{5,4},{6,5},{7,6},{8,15},{9,8},{10,9... | collective-permute-start | bytes 602120 | tf_op jit(solution)/shard_map/ppermute | solution.py:782
  19.6 6.5 %collective-permute-start.5 = (f32[24,128]{1,0:T(8,128)S(1)}, f32[24,128]{1,0:T(8,128)S(1)}, u32[]{:S(2)}, u32[]{:S(2)}) collective-permute-start(f32[24,128]{1,0:T(8,128)S(1)} %get-tuple-element.22), channel_id=1, source_target_pairs={{0,6},{1,7},{2,0},{3,1},{4,2},{5,3},{6,4},{7,5},{8,14},{9,15},{10,... | collective-permute-start | bytes 36872 | tf_op jit(solution)/shard_map/ppermute | solution.py:782
  21.4 2.5 %copy-start.4 = (f32[4,16,16]{2,1,0:T(8,128)S(1)}, f32[4,16,16]{2,1,0:T(8,128)}, u32[]{:S(2)}) copy-start(f32[4,16,16]{2,1,0:T(8,128)} %constant.19.clone.window_ref) | copy-start | bytes 12292
  21.4 2.5 %copy-start.6 = (f32[16,256]{1,0:T(8,128)S(1)}, f32[16,256]{1,0:T(8,128)}, u32[]{:S(2)}) copy-start(f32[16,256]{1,0:T(8,128)} %constant.18.clone.spectrum_ref) | copy-start | bytes 49156
  21.4 2.5 %copy-start.8 = (f32[16,40]{1,0:T(8,128)S(1)}, f32[16,40]{1,0:T(8,128)}, u32[]{:S(2)}) copy-start(f32[16,40]{1,0:T(8,128)} %constant.16.clone.gather_ref) | copy-start | bytes 7684
  21.4 5.8 %collective-permute-start.4 = (f32[24,128]{1,0:T(8,128)S(1)}, f32[24,128]{1,0:T(8,128)S(1)}, u32[]{:S(2)}, u32[]{:S(2)}) collective-permute-start(f32[24,128]{1,0:T(8,128)S(1)} %get-tuple-element.21.token_ref), channel_id=1, source_target_pairs={{0,2},{1,3},{2,4},{3,5},{4,6},{5,7},{6,0},{7,1},{8,10},{9,11},{10,... | collective-permute-start | bytes 36872 | tf_op jit(solution)/shard_map/ppermute | solution.py:782
  23.9 3.4 %copy-start.3 = (bf16[256,256]{1,0:T(8,128)(2,1)S(1)}, bf16[256,256]{1,0:T(8,128)(2,1)}, u32[]{:S(2)}) copy-start(bf16[256,256]{1,0:T(8,128)(2,1)} %constant.15.clone.depth_ref) | copy-start | bytes 393220
  23.9 3.4 %copy-start.5 = (f32[2,16,128]{2,1,0:T(8,128)S(1)}, f32[2,16,128]{2,1,0:T(8,128)}, u32[]{:S(2)}) copy-start(f32[2,16,128]{2,1,0:T(8,128)} %constant.20.clone.spectrum_ref) | copy-start | bytes 49156
